TPU v7x, 128 devices: a whole 4x4x4 slice. The times are simulated.
128 devices in a mesh: px: 8 (over x, core), py: 16 (over z, y).
Axes of the slice: x: 4, y: 4, z: 4, core: 2. Of those that a mesh axis runs over, the one named last changes fastest.
Arguments:
- theta_field: float32 [32, 128, 2048], P(None, 'px', 'py'), may hold values from -6 to 6
- wind_u: float32 [32, 128, 2048], P(None, 'px', 'py'), may hold values from -6 to 6
- wind_v: float32 [32, 128, 2048], P(None, 'px', 'py'), may hold values from -6 to 6
- hyper_coef: float32 [32], replicated, may hold values from 0.002 to 0.02
- damp_coef: float32 [32], replicated, may hold values from 0.05 to 0.4
- obs_cells: int32 [128, 128, 128], P(('px', 'py')), may hold values from 0 to 1918, as said below
- obs_levels: int32 [128, 128, 128], P(('px', 'py')), may hold values from 0 to 30
- obs_bary: float32 [128, 128, 3, 128], P(('px', 'py')), may hold values from 0 to 1, as said below
- obs_vfrac: float32 [128, 128, 128], P(('px', 'py')), may hold values from 0 to 1
- obs_values: float32 [128, 128, 128], P(('px', 'py')), may hold values from -6 to 6
- obs_mask: int32 [128, 128, 128], P(('px', 'py')), may hold values from 0 to 1, as said below
Outputs:
- theta_next: float32 [32, 128, 2048], P(None, 'px', 'py')
- wind_u_next: float32 [32, 128, 2048], P(None, 'px', 'py')
- wind_v_next: float32 [32, 128, 2048], P(None, 'px', 'py')
- departures: float32 [128, 128, 128], P(('px', 'py'))
Inputs may be any that keep to these rules, and one draw needn't show every extreme that they name: obs_cells is r * 128 + c with r below 15 and c below 127. `obs_bary`: each row of three weights is positive and sums to one. `obs_mask`: in every draw some destination patch has all 128 slots used from every owner.
All inputs are finite; a program needn't handle non-finite values.
Results may differ from a plain program's by a relative error of at most 0.000084.
Values sent between devices are 32-bit elements; how exact they have to be, the bound alone decides.
No kernel may reach another device: no remote copies, remote signals or barrier semaphores. Data moves between devices by JAX's collectives and lax.ppermute only.
A program may use at most 64 MiB of HBM per device.

v0:
```python
import math

import jax
import jax.numpy as jnp
from jax import lax
from jax.sharding import PartitionSpec as P


def padded(cells, sides, width):
    for axis, dim in sides:
        count = lax.axis_size(axis)
        head = lax.slice_in_dim(cells, 0, width, axis=dim)
        tail = lax.slice_in_dim(cells, cells.shape[dim] - width, cells.shape[dim], axis=dim)
        cells = jnp.concatenate(
            [
                lax.ppermute(tail, axis, [(i, (i + 1) % count) for i in range(count)]),
                cells,
                lax.ppermute(head, axis, [((i + 1) % count, i) for i in range(count)]),
            ],
            axis=dim,
        )
    return cells


def inner_view(field, step_i, step_j):
    rows = field.shape[-2]
    cols = field.shape[-1]
    return field[..., 1 + step_i : rows - 1 + step_i, 1 + step_j : cols - 1 + step_j]


def laplace(field):
    total = inner_view(field, 1, 0) + inner_view(field, -1, 0)
    total = total + inner_view(field, 0, 1) + inner_view(field, 0, -1)
    total = total + inner_view(field, 1, -1) + inner_view(field, -1, 1)
    return total - 6.0 * inner_view(field, 0, 0)


def diff_x(field):
    return (inner_view(field, 1, 0) - inner_view(field, -1, 0)) * 0.5


def diff_y(field):
    return (inner_view(field, 0, 1) - inner_view(field, 0, -1)) * 0.5


def interpolate(theta_next, cells, levels, bary, vfrac):
    levs = theta_next.shape[0]
    cols = theta_next.shape[2]
    count = theta_next.shape[1] * cols
    per_cell = theta_next.reshape(levs, count).T
    table = jnp.concatenate(
        [per_cell, jnp.roll(per_cell, -cols, axis=0), jnp.roll(per_cell, -1, axis=0)], axis=1
    )
    shape = cells.shape
    total = cells.size
    block = math.gcd(total, 2048)
    flat_cells = cells.reshape(total // block, block)
    flat_levels = levels.reshape(total // block, block)
    flat_vfrac = vfrac.reshape(total // block, block)
    flat_bary = jnp.moveaxis(bary, -2, 0).reshape(3, total // block, block)
    flat_bary = jnp.moveaxis(flat_bary, 0, 1)
    cell_iota = jnp.arange(count, dtype=jnp.int32)
    level_iota = jnp.arange(levs, dtype=jnp.int32)

    def one_block(pieces):
        blk_cells, blk_levels, blk_vfrac, blk_bary = pieces
        onehot = (blk_cells[:, None] == cell_iota[None, :]).astype(jnp.float32)
        picked = jnp.dot(
            onehot, table, preferred_element_type=jnp.float32, precision=lax.Precision.HIGHEST
        )
        picked = picked.reshape(block, 3, levs)
        weights = (1.0 - blk_vfrac[:, None]) * (level_iota[None, :] == blk_levels[:, None]).astype(
            jnp.float32
        )
        weights = weights + blk_vfrac[:, None] * (
            level_iota[None, :] == blk_levels[:, None] + 1
        ).astype(jnp.float32)
        columns = jnp.sum(picked * weights[:, None, :], axis=2)
        return jnp.sum(columns * blk_bary.T, axis=1)

    model = lax.map(one_block, (flat_cells, flat_levels, flat_vfrac, flat_bary))
    return model.reshape(shape)


def on_device(
    theta_field,
    wind_u,
    wind_v,
    hyper_coef,
    damp_coef,
    obs_cells,
    obs_levels,
    obs_bary,
    obs_vfrac,
    obs_values,
    obs_mask,
):
    stacked = jnp.stack([wind_u, wind_v, theta_field])
    bordered = padded(stacked, (("px", 2), ("py", 3)), 1)
    first_lap = laplace(bordered)
    divergence = diff_x(bordered[0]) + diff_y(bordered[1])
    theta_dx = diff_x(bordered[2])
    theta_dy = diff_y(bordered[2])
    joined = jnp.concatenate([first_lap, divergence[None]], axis=0)
    second = padded(joined, (("px", 2), ("py", 3)), 1)
    second_lap = laplace(second[:3])
    grad_x = diff_x(second[3])
    grad_y = diff_y(second[3])
    coef = hyper_coef[:, None, None]
    damp = damp_coef[:, None, None]
    theta_next = theta_field - coef * second_lap[2] - 0.5 * (wind_u * theta_dx + wind_v * theta_dy)
    wind_u_next = wind_u - coef * second_lap[0] + damp * grad_x
    wind_v_next = wind_v - coef * second_lap[1] + damp * grad_y
    got_cells, got_levels, got_bary, got_vfrac = (
        lax.all_to_all(obs_cells, ("px", "py"), split_axis=1, concat_axis=0, tiled=True),
        lax.all_to_all(obs_levels, ("px", "py"), split_axis=1, concat_axis=0, tiled=True),
        lax.all_to_all(obs_bary, ("px", "py"), split_axis=1, concat_axis=0, tiled=True),
        lax.all_to_all(obs_vfrac, ("px", "py"), split_axis=1, concat_axis=0, tiled=True),
    )
    model_here = interpolate(theta_next, got_cells, got_levels, got_bary, got_vfrac)
    model = lax.all_to_all(model_here, ("px", "py"), split_axis=0, concat_axis=1, tiled=True)
    departures = obs_mask.astype(jnp.float32) * (obs_values - model)
    return (theta_next, wind_u_next, wind_v_next, departures)


def solution(mesh):
    in_specs = (
        P(None, "px", "py"),
        P(None, "px", "py"),
        P(None, "px", "py"),
        P(),
        P(),
        P(("px", "py"), None, None),
        P(("px", "py"), None, None),
        P(("px", "py"), None, None, None),
        P(("px", "py"), None, None),
        P(("px", "py"), None, None),
        P(("px", "py"), None, None),
    )
    out_specs = (
        P(None, "px", "py"),
        P(None, "px", "py"),
        P(None, "px", "py"),
        P(("px", "py"), None, None),
    )
    return jax.shard_map(
        on_device, mesh=mesh, in_specs=in_specs, out_specs=out_specs, check_vma=False
    )
```

profile of v0, /device:TPU:1, one launch (start us, length us, event | category | flops | bytes accessed | tf_op | source)
XLA Modules:
  0.0 247.1 jit_solution(17076121440556735948)
XLA Ops:
  0.6 2.0 pad_maximum_fusion.15
  2.7 2.0 copy.153
  4.7 1.4 collective-permute-start
  6.1 1.2 collective-permute-start.1
  7.3 3.3 %collective-permute-done = f32[3,32,1,128]{1,3,2,0:T(8,128)S(1)} collective-permute-done((f32[3,32,1,128]{1,3,2,0:T(8,128)S(1)}, f32[3,32,1,128]{1,3,2,0:T(8,128)S(1)}, u32[]{:S(2)}, u32[]{:S(2)}) %collective-permute-start) | collective-permute-done | bytes 49184 | tf_op jit(solution)/shard_map/ppermute | solution.py:18
  10.7 6.3 %collective-permute-start.2 = (f32[3,32,18,1]{1,3,2,0:T(1,128)S(1)}, f32[3,32,18,1]{1,3,2,0:T(1,128)S(1)}, u32[]{:S(2)}, u32[]{:S(2)}) collective-permute-start(f32[3,32,18,1]{1,3,2,0:T(1,128)S(1)} %get-tuple-element.183), channel_id=1, source_target_pairs={{1,0},{2,1},{3,2},{4,3},{5,4},{6,5},{7,6},{8,7},{9,8},{10,9},{11,1... | collective-permute-start | bytes 20744 | tf_op jit(solution)/shard_map/ppermute | solution.py:18
  17.0 1.0 collective-permute-done.2
  18.0 5.1 %collective-permute-done.3 = f32[3,32,18,1]{1,3,2,0:T(1,128)S(1)} collective-permute-done((f32[3,32,18,1]{1,3,2,0:T(1,128)S(1)}, f32[3,32,18,1]{1,3,2,0:T(1,128)S(1)}, u32[]{:S(2)}, u32[]{:S(2)}) %collective-permute-start.3) | collective-permute-done | bytes 6944 | tf_op jit(solution)/shard_map/ppermute | solution.py:16
  23.6 1.3 slice_bitcast_fusion.2
  25.2 1.8 maximum_maximum_fusion.1
  27.0 5.1 %fusion.10 = f32[3,32,16,128]{1,3,2,0:T(8,128)S(1)} fusion(f32[3,32,18,129]{1,3,2,0:T(8,128)S(1)} %get-tuple-element.181, f32[3,32,18,129]{1,3,2,0:T(8,128)S(1)} %get-tuple-element.180, f32[3,32,16,128]{1,3,2,0:T(8,128)} %copy-done, f32[3,32,1,128]{1,3,2,0:T(8,128)S(1)} %collective-permute-done.1, f32[3,32,1,128]{1,3,2,0:T(8,128)S(1)} %collective-permute-done), kind=kLoop, calls=%fused_computation.34 | loop fusion | flops 1769472 | bytes 4816896 | tf_op jit(solution)/shard_map/sub | solution.py:35
  33.0 5.5 %collective-permute-start.4 = (f32[4,32,1,128]{1,3,2,0:T(8,128)}, f32[4,32,1,128]{1,3,2,0:T(8,128)S(1)}, u32[]{:S(2)}, u32[]{:S(2)}) collective-permute-start(f32[4,32,1,128]{1,3,2,0:T(8,128)} %get-tuple-element.176), channel_id=1, source_target_pairs={{16,0},{32,16},{48,32},{64,48},{80,64},{96,80},{112,96},{0,112},{1... | collective-permute-start | bytes 196616 | tf_op jit(solution)/shard_map/ppermute | solution.py:18
  38.5 13.4 %all_to_all.51 = s32[1,128,128]{2,0,1:T(1,128)S(1)} all-to-all(s32[1,128,128]{2,0,1:T(1,128)S(1)} %bitcast.104), channel_id=1, replica_groups=mesh['px'=8,'py'=16] {'px','py'}, dimensions={1} | all-to-all | bytes 131072 | tf_op jit(solution)/shard_map/all_to_all | solution.py:115
  51.9 4.3 %all-to-all-start.1 = ((s32[1,128,128]{2,0,1:T(1,128)}), s32[1,128,128]{2,0,1:T(1,128)S(1)}, u32[]{:S(2)}, u32[]{:S(2)}) async-start(s32[1,128,128]{2,0,1:T(1,128)} %bitcast.105), calls=%async_computation.1 | async-start | bytes 131072 | tf_op jit(solution)/shard_map/all_to_all | solution.py:116
  56.2 1.0 pad_maximum_fusion.18
  57.8 5.6 %collective-permute-start.6 = (f32[4,32,18,1]{1,0,3,2:T(4,128)}, f32[4,32,18,1]{1,0,3,2:T(4,128)}, u32[]{:S(2)}, u32[]{:S(2)}) collective-permute-start(f32[4,32,18,1]{1,0,3,2:T(4,128)} %copy.158), channel_id=1, source_target_pairs={{1,0},{2,1},{3,2},{4,3},{5,4},{6,5},{7,6},{8,7},{9,8},{10,9},{11,1... | collective-permute-start | bytes 27656 | tf_op jit(solution)/shard_map/ppermute | solution.py:18
  64.0 1.9 all-to-all-done.1
  65.9 7.9 %all-to-all-start.2 = ((f32[1,128,128]{2,0,1:T(1,128)}), f32[1,128,128]{2,0,1:T(1,128)}, u32[]{:S(2)}, u32[]{:S(2)}) async-start(f32[1,128,128]{2,0,1:T(1,128)} %bitcast.106), calls=%async_computation.2 | async-start | bytes 131072 | tf_op jit(solution)/shard_map/all_to_all | solution.py:118
  73.8 2.3 copy.162
  76.0 2.3 copy.163
  78.3 2.3 copy.164
  80.6 1.8 copy.173
  82.9 1.4 reduce.9
  84.3 1.5 reshape.143
  87.2 10.2 %all-to-all-start.3 = ((f32[1,128,3,128]{3,2,0,1:T(4,128)}), f32[1,128,3,128]{3,2,0,1:T(4,128)}, u32[]{:S(2)}, u32[]{:S(2)}) async-start(f32[1,128,3,128]{3,2,0,1:T(4,128)} %copy.173), calls=%async_computation.3 | async-start | bytes 524288 | tf_op jit(solution)/shard_map/all_to_all | solution.py:117
  98.0 1.6 reduce.11
  101.8 4.4 %maximum_maximum_fusion = (f32[4,32,18,129]{1,3,2,0:T(8,128)S(1)}, f32[4,32,18,129]{1,3,2,0:T(8,128)S(1)}) fusion(f32[4,32,1,128]{1,3,2,0:T(8,128)S(1)} %collective-permute-done.4, f32[1,32,16,128]{1,3,2,0:T(8,128)} %copy-done.1, f32[3,32,16,128]{1,3,2,0:T(8,128)S(1)} %fusion.10, f32[4,32,1,128]{1,3,2,0:T(8,128)} %collective-permute-done.5, ...), kind=kLoop, calls=%fused_computation.19 | loop fusion | flops 2377728 | bytes 3575808 | tf_op jit(solution)/shard_map/concatenate | solution.py:14
  106.3 1.0 fusion.12
  107.3 3.3 %fusion.8 = f32[3,32,16,128]{1,3,2,0:T(8,128)S(1)} fusion(f32[4,32,18,129]{1,3,2,0:T(8,128)S(1)} %get-tuple-element.169, f32[4,32,18,129]{1,3,2,0:T(8,128)S(1)} %get-tuple-element.168, f32[4,32,1,128]{1,3,2,0:T(8,128)} %collective-permute-done.5, f32[1,32,16,128]{1,3,2,0:T(8,128)S(1)} %copy-done.2, f32[3,32,16,128]{1,3,2,0:T(8,128)S(1)} %fusion.10, ...), kind=kLoop, calls=%fused_computation.24 | loop fusion | flops 2162688 | bytes 5111808 | tf_op jit(solution)/shard_map/sub | solution.py:35
  110.6 1.2 fusion.14
  112.3 1.0 fusion.33
  113.3 2.5 copy.175
  115.8 1.0 copy.174
  116.8 108.5 %while.12 = (s32[]{:T(128)}, f32[8,2048]{1,0:T(8,128)}, s32[8,2048]{1,0:T(8,128)}, f32[2048,96]{1,0:T(8,128)}, s32[8,2048]{1,0:T(8,128)}, /*index=5*/f32[8,2048]...) while((s32[]{:T(128)}, f32[8,2048]{1,0:T(8,128)}, s32[8,2048]{1,0:T(8,128)}, ...), condition=%wide.region_3.4_spmd.clone.clone, body=%wide.region_0.3_spmd.clone.clone.sunk | while | flops 4836761600 | bytes 3154029 | solution.py:81
  116.8 0.9 constant_dynamic-slice_fusion.7
  118.6 10.0 %fusion.41 = f32[2048,96]{0,1:T(8,128)S(1)} fusion(f32[2048,96]{1,0:T(8,128)} %get-tuple-element.254, s32[2048]{0:T(1024)S(1)} %bitcast.103), kind=kOutput, calls=%fused_computation.3.clone.1 | convolution fusion | flops 4836032512 | bytes 1581056 | tf_op jit(solution)/shard_map/while/body/eval_jaxpr/dot_general | solution.py:68
  128.8 1.5 dynamic_update_slice.7
  130.4 0.9 constant_dynamic-slice_fusion.7
  132.2 10.0 %fusion.41 = f32[2048,96]{0,1:T(8,128)S(1)} fusion(f32[2048,96]{1,0:T(8,128)} %get-tuple-element.254, s32[2048]{0:T(1024)S(1)} %bitcast.103), kind=kOutput, calls=%fused_computation.3.clone.1 | convolution fusion | flops 4836032512 | bytes 1581056 | tf_op jit(solution)/shard_map/while/body/eval_jaxpr/dot_general | solution.py:68
  142.4 1.5 dynamic_update_slice.7
  143.9 0.9 constant_dynamic-slice_fusion.7
  145.7 10.0 %fusion.41 = f32[2048,96]{0,1:T(8,128)S(1)} fusion(f32[2048,96]{1,0:T(8,128)} %get-tuple-element.254, s32[2048]{0:T(1024)S(1)} %bitcast.103), kind=kOutput, calls=%fused_computation.3.clone.1 | convolution fusion | flops 4836032512 | bytes 1581056 | tf_op jit(solution)/shard_map/while/body/eval_jaxpr/dot_general | solution.py:68
  156.0 1.5 dynamic_update_slice.7
  157.5 0.9 constant_dynamic-slice_fusion.7
  159.3 10.0 %fusion.41 = f32[2048,96]{0,1:T(8,128)S(1)} fusion(f32[2048,96]{1,0:T(8,128)} %get-tuple-element.254, s32[2048]{0:T(1024)S(1)} %bitcast.103), kind=kOutput, calls=%fused_computation.3.clone.1 | convolution fusion | flops 4836032512 | bytes 1581056 | tf_op jit(solution)/shard_map/while/body/eval_jaxpr/dot_general | solution.py:68
  169.5 1.5 dynamic_update_slice.7
  171.0 0.9 constant_dynamic-slice_fusion.7
  172.9 10.0 %fusion.41 = f32[2048,96]{0,1:T(8,128)S(1)} fusion(f32[2048,96]{1,0:T(8,128)} %get-tuple-element.254, s32[2048]{0:T(1024)S(1)} %bitcast.103), kind=kOutput, calls=%fused_computation.3.clone.1 | convolution fusion | flops 4836032512 | bytes 1581056 | tf_op jit(solution)/shard_map/while/body/eval_jaxpr/dot_general | solution.py:68
  183.1 1.5 dynamic_update_slice.7
  184.6 0.9 constant_dynamic-slice_fusion.7
  186.4 10.0 %fusion.41 = f32[2048,96]{0,1:T(8,128)S(1)} fusion(f32[2048,96]{1,0:T(8,128)} %get-tuple-element.254, s32[2048]{0:T(1024)S(1)} %bitcast.103), kind=kOutput, calls=%fused_computation.3.clone.1 | convolution fusion | flops 4836032512 | bytes 1581056 | tf_op jit(solution)/shard_map/while/body/eval_jaxpr/dot_general | solution.py:68
  196.7 1.5 dynamic_update_slice.7
  198.2 0.9 constant_dynamic-slice_fusion.7
  200.0 10.0 %fusion.41 = f32[2048,96]{0,1:T(8,128)S(1)} fusion(f32[2048,96]{1,0:T(8,128)} %get-tuple-element.254, s32[2048]{0:T(1024)S(1)} %bitcast.103), kind=kOutput, calls=%fused_computation.3.clone.1 | convolution fusion | flops 4836032512 | bytes 1581056 | tf_op jit(solution)/shard_map/while/body/eval_jaxpr/dot_general | solution.py:68
  210.2 1.5 dynamic_update_slice.7
  211.7 0.9 constant_dynamic-slice_fusion.7
  213.5 10.0 %fusion.41 = f32[2048,96]{0,1:T(8,128)S(1)} fusion(f32[2048,96]{1,0:T(8,128)} %get-tuple-element.254, s32[2048]{0:T(1024)S(1)} %bitcast.103), kind=kOutput, calls=%fused_computation.3.clone.1 | convolution fusion | flops 4836032512 | bytes 1581056 | tf_op jit(solution)/shard_map/while/body/eval_jaxpr/dot_general | solution.py:68
  223.8 1.5 dynamic_update_slice.7
  225.3 1.6 reshape.148
  226.9 9.8 %all-to-all-start.4 = ((f32[128,1,128]{2,1,0:T(1,128)}), f32[128,1,128]{2,1,0:T(1,128)S(1)}, u32[]{:S(2)}, u32[]{:S(2)}) async-start(f32[128,1,128]{2,1,0:T(1,128)} %reshape.148), calls=%async_computation.4 | async-start | bytes 131072 | tf_op jit(solution)/shard_map/all_to_all | solution.py:121
  236.6 1.0 copy.177
  237.7 1.0 copy.178
  238.7 1.0 copy.179
  239.7 6.7 %all-to-all-done.4 = f32[128,1,128]{2,1,0:T(1,128)S(1)} async-done(((f32[128,1,128]{2,1,0:T(1,128)}), f32[128,1,128]{2,1,0:T(1,128)S(1)}, u32[]{:S(2)}, u32[]{:S(2)}) %all-to-all-start.4) | async-done | bytes 65568 | tf_op jit(solution)/shard_map/all_to_all | solution.py:121
  (113 shorter events, 17.7 us)
Async XLA Ops:
  4.7 20.5 %copy-start = (f32[3,32,16,128]{1,3,2,0:T(8,128)}, f32[3,32,16,128]{1,3,2,0:T(8,128)S(1)}, u32[]{:S(2)}) copy-start(f32[3,32,16,128]{1,3,2,0:T(8,128)S(1)} %copy.153) | copy-start | bytes 2359300
  4.7 6.0 %collective-permute-start = (f32[3,32,1,128]{1,3,2,0:T(8,128)S(1)}, f32[3,32,1,128]{1,3,2,0:T(8,128)S(1)}, u32[]{:S(2)}, u32[]{:S(2)}) collective-permute-start(f32[3,32,1,128]{1,3,2,0:T(8,128)S(1)} %get-tuple-element.185), channel_id=1, source_target_pairs={{16,0},{32,16},{48,32},{64,48},{80,64},{96,80},{112,96},{0,112},{1... | collective-permute-start | bytes 147464 | tf_op jit(solution)/shard_map/ppermute | solution.py:18
  6.1 4.5 %collective-permute-start.1 = (f32[3,32,1,128]{1,3,2,0:T(8,128)S(1)}, f32[3,32,1,128]{1,3,2,0:T(8,128)S(1)}, u32[]{:S(2)}, u32[]{:S(2)}) collective-permute-start(f32[3,32,1,128]{1,3,2,0:T(8,128)S(1)} %get-tuple-element.184), channel_id=1, source_target_pairs={{0,16},{16,32},{32,48},{48,64},{64,80},{80,96},{96,112},{112,0},{1... | collective-permute-start | bytes 147464 | tf_op jit(solution)/shard_map/ppermute | solution.py:16
  10.7 7.3 %collective-permute-start.2 = (f32[3,32,18,1]{1,3,2,0:T(1,128)S(1)}, f32[3,32,18,1]{1,3,2,0:T(1,128)S(1)}, u32[]{:S(2)}, u32[]{:S(2)}) collective-permute-start(f32[3,32,18,1]{1,3,2,0:T(1,128)S(1)} %get-tuple-element.183), channel_id=1, source_target_pairs={{1,0},{2,1},{3,2},{4,3},{5,4},{6,5},{7,6},{8,7},{9,8},{10,9},{11,1... | collective-permute-start | bytes 20744 | tf_op jit(solution)/shard_map/ppermute | solution.py:18
  17.0 6.0 %collective-permute-start.3 = (f32[3,32,18,1]{1,3,2,0:T(1,128)S(1)}, f32[3,32,18,1]{1,3,2,0:T(1,128)S(1)}, u32[]{:S(2)}, u32[]{:S(2)}) collective-permute-start(f32[3,32,18,1]{1,3,2,0:T(1,128)S(1)} %get-tuple-element.182), channel_id=1, source_target_pairs={{0,1},{1,2},{2,3},{3,4},{4,5},{5,6},{6,7},{7,8},{8,9},{9,10},{10,1... | collective-permute-start | bytes 20744 | tf_op jit(solution)/shard_map/ppermute | solution.py:16
  25.2 6.9 %copy-start.1 = (f32[1,32,16,128]{1,3,2,0:T(8,128)}, f32[1,32,16,128]{1,3,2,0:T(8,128)S(1)}, u32[]{:S(2)}) copy-start(f32[1,32,16,128]{1,3,2,0:T(8,128)S(1)} %fusion.32) | copy-start | bytes 786436
  32.1 6.3 %copy-start.7 = (s32[1,128,128]{2,1,0:T(8,128)S(1)}, s32[1,128,128]{2,1,0:T(8,128)}, u32[]{:S(2)}) copy-start(s32[1,128,128]{2,1,0:T(8,128)} %param.18) | copy-start | bytes 196612
  33.0 40.8 %copy-start.11 = (f32[32]{0:T(128)S(1)}, f32[32]{0:T(128)}, u32[]{:S(2)}) copy-start(f32[32]{0:T(128)} %param.17) | copy-start | bytes 388
  33.0 23.2 %collective-permute-start.4 = (f32[4,32,1,128]{1,3,2,0:T(8,128)}, f32[4,32,1,128]{1,3,2,0:T(8,128)S(1)}, u32[]{:S(2)}, u32[]{:S(2)}) collective-permute-start(f32[4,32,1,128]{1,3,2,0:T(8,128)} %get-tuple-element.176), channel_id=1, source_target_pairs={{16,0},{32,16},{48,32},{64,48},{80,64},{96,80},{112,96},{0,112},{1... | collective-permute-start | bytes 196616 | tf_op jit(solution)/shard_map/ppermute | solution.py:18
  38.5 17.7 %collective-permute-start.5 = (f32[4,32,1,128]{1,3,2,0:T(8,128)}, f32[4,32,1,128]{1,3,2,0:T(8,128)}, u32[]{:S(2)}, u32[]{:S(2)}) collective-permute-start(f32[4,32,1,128]{1,3,2,0:T(8,128)} %get-tuple-element.175), channel_id=1, source_target_pairs={{0,16},{16,32},{32,48},{48,64},{64,80},{80,96},{96,112},{112,0},{1... | collective-permute-start | bytes 196616 | tf_op jit(solution)/shard_map/ppermute | solution.py:16
  51.9 14.0 %all-to-all-start.1 = ((s32[1,128,128]{2,0,1:T(1,128)}), s32[1,128,128]{2,0,1:T(1,128)S(1)}, u32[]{:S(2)}, u32[]{:S(2)}) async-start(s32[1,128,128]{2,0,1:T(1,128)} %bitcast.105), calls=%async_computation.1 | async-start | bytes 131072 | tf_op jit(solution)/shard_map/all_to_all | solution.py:116
  57.8 42.4 %collective-permute-start.6 = (f32[4,32,18,1]{1,0,3,2:T(4,128)}, f32[4,32,18,1]{1,0,3,2:T(4,128)}, u32[]{:S(2)}, u32[]{:S(2)}) collective-permute-start(f32[4,32,18,1]{1,0,3,2:T(4,128)} %copy.158), channel_id=1, source_target_pairs={{1,0},{2,1},{3,2},{4,3},{5,4},{6,5},{7,6},{8,7},{9,8},{10,9},{11,1... | collective-permute-start | bytes 27656 | tf_op jit(solution)/shard_map/ppermute | solution.py:18
  64.0 37.0 %collective-permute-start.7 = (f32[4,32,18,1]{1,0,3,2:T(4,128)}, f32[4,32,18,1]{1,0,3,2:T(4,128)}, u32[]{:S(2)}, u32[]{:S(2)}) collective-permute-start(f32[4,32,18,1]{1,0,3,2:T(4,128)} %copy.160), channel_id=1, source_target_pairs={{0,1},{1,2},{2,3},{3,4},{4,5},{5,6},{6,7},{7,8},{8,9},{9,10},{10,1... | collective-permute-start | bytes 27656 | tf_op jit(solution)/shard_map/ppermute | solution.py:16
  65.9 21.4 %all-to-all-start.2 = ((f32[1,128,128]{2,0,1:T(1,128)}), f32[1,128,128]{2,0,1:T(1,128)}, u32[]{:S(2)}, u32[]{:S(2)}) async-start(f32[1,128,128]{2,0,1:T(1,128)} %bitcast.106), calls=%async_computation.2 | async-start | bytes 131072 | tf_op jit(solution)/shard_map/all_to_all | solution.py:118
  87.2 28.5 %all-to-all-start.3 = ((f32[1,128,3,128]{3,2,0,1:T(4,128)}), f32[1,128,3,128]{3,2,0,1:T(4,128)}, u32[]{:S(2)}, u32[]{:S(2)}) async-start(f32[1,128,3,128]{3,2,0,1:T(4,128)} %copy.173), calls=%async_computation.3 | async-start | bytes 524288 | tf_op jit(solution)/shard_map/all_to_all | solution.py:117
  101.8 4.4 %copy-start.2 = (f32[1,32,16,128]{1,3,2,0:T(8,128)S(1)}, f32[1,32,16,128]{1,3,2,0:T(8,128)}, u32[]{:S(2)}) copy-start(f32[1,32,16,128]{1,3,2,0:T(8,128)} %copy-done.1) | copy-start | bytes 786436
  107.3 3.3 %copy-start.3 = (f32[32,18,130]{0,2,1:T(8,128)S(1)}, f32[32,18,130]{0,2,1:T(8,128)}, u32[]{:S(2)}) copy-start(f32[32,18,130]{0,2,1:T(8,128)} %get-tuple-element.178) | copy-start | bytes 898564
  107.3 3.3 %copy-start.4 = (f32[32,16,128]{0,2,1:T(8,128)S(1)}, f32[32,16,128]{0,2,1:T(8,128)}, u32[]{:S(2)}) copy-start(f32[32,16,128]{0,2,1:T(8,128)} %copy.162) | copy-start | bytes 786436
  107.3 3.3 %copy-start.5 = (f32[32,16,128]{0,2,1:T(8,128)S(1)}, f32[32,16,128]{0,2,1:T(8,128)}, u32[]{:S(2)}) copy-start(f32[32,16,128]{0,2,1:T(8,128)} %copy.163) | copy-start | bytes 786436
  107.3 3.3 %copy-start.6 = (f32[32,16,128]{0,2,1:T(8,128)S(1)}, f32[32,16,128]{0,2,1:T(8,128)}, u32[]{:S(2)}) copy-start(f32[32,16,128]{0,2,1:T(8,128)} %copy.164) | copy-start | bytes 786436
  107.3 3.3 %copy-start.10 = (f32[32]{0:T(128)S(1)}, f32[32]{0:T(128)}, u32[]{:S(2)}) copy-start(f32[32]{0:T(128)} %param.16) | copy-start | bytes 388
  225.3 21.1 %copy-start.8 = (f32[1,128,128]{2,1,0:T(8,128)S(1)}, f32[1,128,128]{2,1,0:T(8,128)}, u32[]{:S(2)}) copy-start(f32[1,128,128]{2,1,0:T(8,128)} %param.22) | copy-start | bytes 196612
  225.3 21.1 %copy-start.9 = (s32[1,128,128]{2,1,0:T(8,128)S(1)}, s32[1,128,128]{2,1,0:T(8,128)}, u32[]{:S(2)}) copy-start(s32[1,128,128]{2,1,0:T(8,128)} %param.23) | copy-start | bytes 196612
  226.9 19.6 %all-to-all-start.4 = ((f32[128,1,128]{2,1,0:T(1,128)}), f32[128,1,128]{2,1,0:T(1,128)S(1)}, u32[]{:S(2)}, u32[]{:S(2)}) async-start(f32[128,1,128]{2,1,0:T(1,128)} %reshape.148), calls=%async_computation.4 | async-start | bytes 131072 | tf_op jit(solution)/shard_map/all_to_all | solution.py:121
where the time goes:
time: 249 us; the launch traced here: 247 us
  matrix products  80.3 us (32%)
  local copies, waits for them, and re-layouts  53.3 us (21%)
  starting transfers between devices  52.1 us (21%)
  other arithmetic  28.6 us (11%)
  waiting for transfers between devices  18 us (7%)
  blocking collectives  13.4 us (5%)
    dot_general x8, matrix products, one_block(): jnp.dot(onehot, table, preferred_element_type=jnp.float32, precision=lax....  80.3 us
    ppermute x4, starting transfers between devices, padded(): lax.ppermute(head, axis, [((i + 1) % count, i) for i in range(count)])  18.8 us
    unnamed x32, local copies, waits for them, and re-layouts  14.2 us
    dynamic_slice x24, local copies, waits for them, and re-layouts, interpolate(): model = lax.map(one_block, (flat_cells, flat_levels, flat_vfrac, flat_bary))  14.1 us
    all_to_all x1, blocking collectives, on_device(): lax.all_to_all(obs_cells, ('px', 'py'), split_axis=1, concat_axis=0, tile...  13.4 us
    dynamic_update_slice x8, local copies, waits for them, and re-layouts, interpolate(): model = lax.map(one_block, (flat_cells, flat_levels, flat_vfrac, flat_bary))  12 us
    all_to_all x1, starting transfers between devices, on_device(): lax.all_to_all(obs_bary, ('px', 'py'), split_axis=1, concat_axis=0, tiled...  10.2 us
    all_to_all x1, starting transfers between devices, on_device(): lax.all_to_all(model_here, ('px', 'py'), split_axis=0, concat_axis=1, til...  9.76 us
  transfers between devices with their start and end apart: 12, of which 5 were waited for; matrix products, arithmetic and copies ran while one was open for 15% of the time, Pallas kernels for 0%

commit v1 on v0

v1 whole, which is shorter than its diff:
```python
import functools

import jax
import jax.numpy as jnp
from jax import lax
from jax.experimental import pallas as pl
from jax.experimental.pallas import tpu as pltpu
from jax.sharding import PartitionSpec as P

LEV = 32
CX = 16
CY = 128
RING = 24
FIELDS = 3
SENT = 5
BOTH = ("px", "py")
F32 = jnp.float32
VMEM = pl.BlockSpec(memory_space=pltpu.VMEM)


def call(kernel, outs, scratch=(), flops=1000, moved=1000):
    return pl.pallas_call(
        kernel,
        out_shape=outs,
        scratch_shapes=scratch,
        compiler_params=pltpu.CompilerParams(vmem_limit_bytes=48 << 20),
        cost_estimate=pl.CostEstimate(flops=flops, bytes_accessed=moved, transcendentals=0),
    )


def pack_obs(cells, levels, bary, vfrac, out):
    rows = cells.shape[0]
    parts = (
        cells[...].astype(F32),
        levels[...].astype(F32),
        vfrac[...],
        bary[:, 0, :],
        bary[:, 1, :],
    )
    for k, part in enumerate(parts):
        out[pl.ds(k, rows, stride=SENT), :] = part


def pack_rows(u, v, t, low, high):
    for f, field in enumerate((u, v, t)):
        for i in range(2):
            at = (i * FIELDS + f) * LEV
            low[at : at + LEV, :] = field[pl.ds(i, LEV, stride=CX), :]
            high[at : at + LEV, :] = field[pl.ds(CX - 2 + i, LEV, stride=CX), :]


def pack_columns(u, v, t, above, below, ring, first, last):
    for f, field in enumerate((u, v, t)):
        for i in range(2):
            at = (i * FIELDS + f) * LEV
            ring[pl.ds(f * LEV * RING + CX + i, LEV, stride=RING), :] = below[at : at + LEV, :]
            ring[pl.ds(f * LEV * RING + RING - 2 + i, LEV, stride=RING), :] = above[at : at + LEV, :]
            ring[pl.ds(f * LEV * RING + CX + 2 + i, LEV, stride=RING), :] = jnp.zeros((LEV, CY), F32)
            ring[pl.ds(f * LEV * RING + CX + 4 + i, LEV, stride=RING), :] = jnp.zeros((LEV, CY), F32)
        for lev in range(LEV):
            ring[(f * LEV + lev) * RING : (f * LEV + lev) * RING + CX, :] = field[lev * CX : (lev + 1) * CX, :]
    for k in range(FIELDS * LEV * RING // 128):
        turned = ring[k * 128 : (k + 1) * 128, :].T
        first[2 * k : 2 * k + 2, :] = turned[0:2, :]
        last[2 * k : 2 * k + 2, :] = turned[CY - 2 :, :]


def step(ring, east, west, hyper, damp, u_out, v_out, t_out, table, side, turn):
    turn[...] = jnp.zeros_like(turn)
    for k in range(FIELDS * LEV * RING // 128):
        turn[0:2, :] = east[2 * k : 2 * k + 2, :]
        turn[CY - 2 :, :] = west[2 * k : 2 * k + 2, :]
        side[k * 128 : (k + 1) * 128, :] = turn[...].T
    lane = lax.broadcasted_iota(jnp.int32, (RING, CY), 1)

    def shifted(field, border, b):
        if b > 0:
            return pltpu.roll(jnp.where(lane < b, border, field), CY - b, 1)
        return pltpu.roll(jnp.where(lane >= CY + b, border, field), -b, 1)

    def rows(value, a):
        return pltpu.roll(value, (RING - a) % RING, 0)[:CX, :]

    def level(lev, carry):
        coef = hyper[lev]
        quarter = damp[lev] * 0.25
        views = []
        fourth = []
        for f in range(FIELDS):
            at = pl.multiple_of((f * LEV + lev) * RING, 8)
            c = ring[pl.ds(at, RING), :]
            h = side[pl.ds(at, RING), :]
            e1, e2, w1, w2 = (shifted(c, h, b) for b in (1, 2, -1, -2))
            r0 = (42.0 * c - 10.0 * (e1 + w1) + (e2 + w2))[:CX, :]
            up1 = 2.0 * (e1 + w2) - 10.0 * (c + w1)
            dn1 = 2.0 * (w1 + e2) - 10.0 * (c + e1)
            up2 = c + w2 + 2.0 * w1
            dn2 = c + e2 + 2.0 * e1
            fourth.append(r0 + rows(up1, 1) + rows(dn1, -1) + rows(up2, 2) + rows(dn2, -2))
            views.append((c, e1, w1, e2, w2))
        (u, ue, uw, _, _), (v, ve, vw, ve2, vw2), (t, te, tw, _, _) = views
        u0, v0, t0 = u[:CX, :], v[:CX, :], t[:CX, :]
        du, dv = ue - uw, ve - vw
        uxx = rows(u, 2) - 2.0 * u0 + rows(u, -2)
        vxy = rows(dv, 1) - rows(dv, -1)
        uxy = rows(du, 1) - rows(du, -1)
        vyy = ve2[:CX, :] - 2.0 * v0 + vw2[:CX, :]
        out_at = pl.multiple_of(lev * CX, 8)
        u_out[pl.ds(out_at, CX), :] = u0 - coef * fourth[0] + quarter * (uxx + vxy)
        v_out[pl.ds(out_at, CX), :] = v0 - coef * fourth[1] + quarter * (uxy + vyy)
        t_out[pl.ds(out_at, CX), :] = (
            t0
            - coef * fourth[2]
            - 0.25 * (u0 * (rows(t, 1) - rows(t, -1)) + v0 * (te - tw)[:CX, :])
        )
        return carry

    lax.fori_loop(0, LEV, level, 0)
    for r in range(CX):
        here = t_out[pl.ds(r, LEV, stride=CX), :]
        for s, part in enumerate((here, pltpu.roll(here, CY - 1, 1))):
            high = part.astype(jnp.bfloat16)
            low = (part - high.astype(F32)).astype(jnp.bfloat16)
            at = (s * CX + r) * LEV
            table[at : at + LEV, :CY] = high
            table[at : at + LEV, CY:] = low


def interpolate(table, obs, model, col, row, lev, fra, b0, b1):
    owners = model.shape[0]
    cell = obs[pl.ds(0, owners, stride=SENT), :].astype(jnp.int32)
    col[...] = cell & (CY - 1)
    row[...] = cell >> 7
    lev[...] = obs[pl.ds(1, owners, stride=SENT), :].astype(jnp.int32)
    fra[...] = obs[pl.ds(2, owners, stride=SENT), :]
    b0[...] = obs[pl.ds(3, owners, stride=SENT), :]
    b1[...] = obs[pl.ds(4, owners, stride=SENT), :]
    cell_iota = lax.broadcasted_iota(jnp.int32, (CY, 256), 0)
    lev_iota = lax.broadcasted_iota(jnp.int32, (LEV, 256), 0)

    def pair(p, carry):
        def two(ref):
            return jnp.concatenate([ref[pl.ds(2 * p, 1), :], ref[pl.ds(2 * p + 1, 1), :]], axis=1)

        c, r, l, a, w0, w1 = (two(ref) for ref in (col, row, lev, fra, b0, b1))
        w2 = 1.0 - w0 - w1
        hot = jnp.where(cell_iota == c, 1.0, 0.0).astype(jnp.bfloat16)
        hot = jnp.concatenate([hot, hot], axis=0)
        got = jnp.dot(table[...], hot, preferred_element_type=F32)
        total = jnp.zeros((LEV, 256), F32)
        for i in range(CX):
            here = jnp.where(r == i, w0, jnp.where(r == i - 1, w1, 0.0))
            total = total + here * got[i * LEV : (i + 1) * LEV, :]
            if i < CX - 1:
                beside = jnp.where(r == i, w2, 0.0)
                total = total + beside * got[(CX + i) * LEV : (CX + i + 1) * LEV, :]
        weight = jnp.where(lev_iota == l, 1.0 - a, jnp.where(lev_iota == l + 1, a, 0.0))
        out = jnp.sum(weight * total, axis=0, keepdims=True)
        model[pl.ds(2 * p, 1), :] = out[:, :128]
        model[pl.ds(2 * p + 1, 1), :] = out[:, 128:]
        return carry

    lax.fori_loop(0, owners // 2, pair, 0)


def neighbour(axis, move):
    count = lax.axis_size(axis)
    return [(i, (i + move) % count) for i in range(count)]


def on_device(theta, wind_u, wind_v, hyper, damp, cells, levels, bary, vfrac, values, mask):
    flat = LEV * CX
    fields = tuple(f.reshape(flat, CY) for f in (wind_u, wind_v, theta))
    owners, slots = cells.shape[1], cells.shape[2]
    shape = jax.ShapeDtypeStruct
    edge = shape((2 * FIELDS * LEV, CY), F32)
    low, high = call(pack_rows, (edge, edge))(*fields)
    sent = call(pack_obs, shape((owners * SENT, slots), F32))(
        cells[0], levels[0], bary[0], vfrac[0]
    )
    above = lax.ppermute(high, "px", neighbour("px", 1))
    below = lax.ppermute(low, "px", neighbour("px", -1))
    got = lax.all_to_all(sent, BOTH, split_axis=0, concat_axis=0, tiled=True)
    ring_rows = FIELDS * LEV * RING
    side = shape((ring_rows // 64, CY), F32)
    ring, first, last = call(pack_columns, (shape((ring_rows, CY), F32), side, side))(
        *fields, above, below
    )
    west = lax.ppermute(last, "py", neighbour("py", 1))
    east = lax.ppermute(first, "py", neighbour("py", -1))
    patch = shape((flat, CY), F32)
    smem = pl.BlockSpec(memory_space=pltpu.SMEM)
    u_next, v_next, t_next, table = pl.pallas_call(
        step,
        out_shape=(patch, patch, patch, shape((2 * flat, 2 * CY), jnp.bfloat16)),
        in_specs=[VMEM, VMEM, VMEM, smem, smem],
        scratch_shapes=[pltpu.VMEM((ring_rows, CY), F32), pltpu.VMEM((CY, CY), F32)],
        compiler_params=pltpu.CompilerParams(vmem_limit_bytes=48 << 20),
        cost_estimate=pl.CostEstimate(flops=4000000, bytes_accessed=4000000, transcendentals=0),
    )(ring, east, west, hyper, damp)
    ints = pltpu.VMEM((owners, slots), jnp.int32)
    floats = pltpu.VMEM((owners, slots), F32)
    model = call(
        interpolate,
        shape((owners, slots), F32),
        scratch=[ints, ints, ints, floats, floats, floats],
        flops=8000000000,
        moved=1000000,
    )(table, got)
    back = lax.all_to_all(model, BOTH, split_axis=0, concat_axis=0, tiled=True)
    departures = mask.astype(F32) * (values - back[None])
    whole = theta.shape
    return t_next.reshape(whole), u_next.reshape(whole), v_next.reshape(whole), departures


def solution(mesh):
    field = P(None, "px", "py")
    obs = P(BOTH, None, None)
    return jax.shard_map(
        on_device,
        mesh=mesh,
        in_specs=(field, field, field, P(), P(), obs, obs, P(BOTH, None, None, None), obs, obs, obs),
        out_specs=(field, field, field, obs),
        check_vma=False,
    )
```

time: 249 us -> 79.3 us (0.32)
  matrix products: 80.3 us -> 0 us
  local copies, waits for them, and re-layouts: 53.3 us -> 4.51 us
  starting transfers between devices: 52.1 us -> 18.6 us
  other arithmetic: 28.6 us -> 0.65 us
  Pallas kernels: 0 us -> 25.9 us
  waiting for transfers between devices: 18 us -> 12.8 us
    dot_general x8 -> x0, matrix products: 80.3 us -> none  [one_block(): jnp.dot(onehot, table, preferred_element_type=jnp.float32, precision=lax....]
    pallas_call x0 -> x5, Pallas kernels: none -> 25.9 us  [the longest x1 19.4 us: on_device(): call(interpolate, shape((owners, slots), F32), scratch=[ints, ints, ints,...]
    all_to_all x4 -> x1, starting transfers between devices: 32.1 us -> 11.5 us  [on_device(): got = lax.all_to_all(sent, BOTH, split_axis=0, concat_axis=0, tiled=True)]
    dynamic_slice x24 -> x0, local copies, waits for them, and re-layouts: 14.1 us -> none  [interpolate(): model = lax.map(one_block, (flat_cells, flat_levels, flat_vfrac, flat_bary))]
    ppermute x8 -> x4, starting transfers between devices: 20 us -> 7.1 us  [the longest x1 5.45 us: on_device(): east = lax.ppermute(first, 'py', neighbour('py', -1))]
    dynamic_update_slice x8 -> x0, local copies, waits for them, and re-layouts: 12 us -> none  [interpolate(): model = lax.map(one_block, (flat_cells, flat_levels, flat_vfrac, flat_bary))]
    unnamed x32 -> x21, local copies, waits for them, and re-layouts: 14.2 us -> 3.61 us
    concatenate x7 -> x0, other arithmetic: 9.62 us -> none  [the longest x5 7.8 us: padded(): jnp.concatenate([lax.ppermute(tail, axis, [(i, (i + 1) % count) for i in...]
  transfers between devices with their start and end apart: 12 -> 5, of which waited for: 5 -> 4; matrix products, arithmetic and copies ran while one was open for 15% -> 0% of each run, Pallas kernels for 0% -> 8%
where the time goes in v1:
time: 79.3 us; the launch traced here: 79 us
  Pallas kernels  25.9 us (33%)
  starting transfers between devices  18.6 us (23%)
  blocking collectives  15.8 us (20%)
  waiting for transfers between devices  12.8 us (16%)
  local copies, waits for them, and re-layouts  4.51 us (6%)
    pallas_call x1, Pallas kernels, on_device(): call(interpolate, shape((owners, slots), F32), scratch=[ints, ints, ints,...  19.4 us
    all_to_all x1, blocking collectives, on_device(): back = lax.all_to_all(model, BOTH, split_axis=0, concat_axis=0, tiled=True)  15.8 us
    all_to_all x1, starting transfers between devices, on_device(): got = lax.all_to_all(sent, BOTH, split_axis=0, concat_axis=0, tiled=True)  11.5 us
    pallas_call x1, Pallas kernels, on_device(): pl.pallas_call(step, out_shape=(patch, patch, patch, shape((2 * flat, 2 *...  5.88 us
    ppermute x1, starting transfers between devices, on_device(): east = lax.ppermute(first, 'py', neighbour('py', -1))  5.45 us
    ppermute x1, waiting for transfers between devices, on_device(): west = lax.ppermute(last, 'py', neighbour('py', 1))  5.04 us
    ppermute x1, waiting for transfers between devices, on_device(): above = lax.ppermute(high, 'px', neighbour('px', 1))  4.69 us
    unnamed x21, local copies, waits for them, and re-layouts  3.61 us
  transfers between devices with their start and end apart: 5, of which 4 were waited for; matrix products, arithmetic and copies ran while one was open for 0% of the time, Pallas kernels for 8%

profile of v1, /device:TPU:1, one launch (start us, length us, event | category | flops | bytes accessed | tf_op | source)
XLA Modules:
  0.0 79.0 jit_solution(2948302034963803647)
XLA Ops:
  0.6 1.1 %copy.20 = f32[1,128,3,128]{3,2,1,0:T(4,128)S(1)} copy(f32[1,128,3,128]{3,1,2,0:T(8,128)} %param.18) | data formatting | bytes 393216 | tf_op args[7]
  1.7 0.0 copy-start.3
  1.7 0.8 %copy-done.3 = s32[1,128,128]{2,1,0:T(8,128)S(1)} copy-done((s32[1,128,128]{2,1,0:T(8,128)S(1)}, s32[1,128,128]{2,1,0:T(8,128)}, u32[]{:S(2)}) %copy-start.3) | copy-done | bytes 65560
  2.5 0.0 copy-start.4
  2.5 0.8 %copy-done.4 = s32[1,128,128]{2,1,0:T(8,128)S(1)} copy-done((s32[1,128,128]{2,1,0:T(8,128)S(1)}, s32[1,128,128]{2,1,0:T(8,128)}, u32[]{:S(2)}) %copy-start.4) | copy-done | bytes 65560
  3.4 0.0 copy-start.5
  3.4 0.8 %copy-done.5 = f32[1,128,128]{2,1,0:T(8,128)S(1)} copy-done((f32[1,128,128]{2,1,0:T(8,128)S(1)}, f32[1,128,128]{2,1,0:T(8,128)}, u32[]{:S(2)}) %copy-start.5) | copy-done | bytes 65560
  4.2 0.0 copy-start
  4.2 0.0 copy-start.1
  4.2 0.0 copy-start.2
  4.2 0.1 shard_map.141
  4.3 0.9 %all_to_all.13 = f32[128,5,128]{2,1,0:T(8,128)} reshape(f32[640,128]{1,0:T(8,128)S(1)} %shard_map.141) | data formatting | bytes 655360 | tf_op jit(solution)/shard_map/all_to_all | solution.py:183
  5.2 0.0 copy-start.6
  5.2 0.0 copy-start.7
  5.2 11.5 %all-to-all-start = ((f32[128,5,128]{2,1,0:T(8,128)}), f32[128,5,128]{2,1,0:T(8,128)S(1)}, u32[]{:S(2)}, u32[]{:S(2)}) async-start(f32[128,5,128]{2,1,0:T(8,128)} %all_to_all.13), calls=%async_computation | async-start | bytes 1048576 | tf_op jit(solution)/shard_map/all_to_all | solution.py:183
  16.7 0.0 copy-done
  16.7 0.0 copy-done.1
  16.7 0.0 copy-done.2
  16.7 0.1 shard_map.138
  16.8 1.6 %collective-permute-start = (f32[192,128]{1,0:T(8,128)S(1)}, f32[192,128]{1,0:T(8,128)S(1)}, u32[]{:S(2)}, u32[]{:S(2)}) collective-permute-start(f32[192,128]{1,0:T(8,128)S(1)} %get-tuple-element.13), channel_id=1, source_target_pairs={{0,16},{16,32},{32,48},{48,64},{64,80},{80,96},{96,112},{112,0},{1... | collective-permute-start | bytes 294920 | tf_op jit(solution)/shard_map/ppermute | solution.py:181
  18.4 0.0 collective-permute-start.1
  18.4 4.7 %collective-permute-done.above = f32[192,128]{1,0:T(8,128)S(1)} collective-permute-done((f32[192,128]{1,0:T(8,128)S(1)}, f32[192,128]{1,0:T(8,128)S(1)}, u32[]{:S(2)}, u32[]{:S(2)}) %collective-permute-start) | collective-permute-done | bytes 98336 | tf_op jit(solution)/shard_map/ppermute | solution.py:181
  23.1 2.2 %collective-permute-done.1.below = f32[192,128]{1,0:T(8,128)S(1)} collective-permute-done((f32[192,128]{1,0:T(8,128)S(1)}, f32[192,128]{1,0:T(8,128)S(1)}, u32[]{:S(2)}, u32[]{:S(2)}) %collective-permute-start.1) | collective-permute-done | bytes 98336 | tf_op jit(solution)/shard_map/ppermute | solution.py:182
  25.3 0.4 shard_map.139
  25.7 5.5 %collective-permute-start.2 = (f32[36,128]{1,0:T(8,128)S(1)}, f32[36,128]{1,0:T(8,128)S(1)}, u32[]{:S(2)}, u32[]{:S(2)}) collective-permute-start(f32[36,128]{1,0:T(8,128)S(1)} %get-tuple-element.16), channel_id=1, source_target_pairs={{0,15},{1,0},{2,1},{3,2},{4,3},{5,4},{6,5},{7,6},{8,7},{9,8},{10,9... | collective-permute-start | bytes 55304 | tf_op jit(solution)/shard_map/ppermute | solution.py:190
  31.2 0.0 collective-permute-start.3
  31.2 0.9 %collective-permute-done.2.east = f32[36,128]{1,0:T(8,128)S(1)} collective-permute-done((f32[36,128]{1,0:T(8,128)S(1)}, f32[36,128]{1,0:T(8,128)S(1)}, u32[]{:S(2)}, u32[]{:S(2)}) %collective-permute-start.2) | collective-permute-done | bytes 18464 | tf_op jit(solution)/shard_map/ppermute | solution.py:190
  32.1 5.0 %collective-permute-done.3.west = f32[36,128]{1,0:T(8,128)S(1)} collective-permute-done((f32[36,128]{1,0:T(8,128)S(1)}, f32[36,128]{1,0:T(8,128)S(1)}, u32[]{:S(2)}, u32[]{:S(2)}) %collective-permute-start.3) | collective-permute-done | bytes 18464 | tf_op jit(solution)/shard_map/ppermute | solution.py:189
  37.1 0.0 copy-done.6
  37.1 0.0 copy-done.7
  37.1 5.9 %shard_map.140 = (f32[512,128]{1,0:T(8,128)}, f32[512,128]{1,0:T(8,128)}, f32[512,128]{1,0:T(8,128)}, bf16[1024,256]{1,0:T(8,128)(2,1)S(1)}) custom-call(f32[2304,128]{1,0:T(8,128)S(1)} %get-tuple-element.15.ring, f32[36,128]{1,0:T(8,128)S(1)} %collective-permute-done.2.east, f32[36,128]{1,0:T(8,128)S(1)} %collective-permute-done.3.west, f32[32]{0:T(128)S(1)} %copy-done.6, ...), custom_call_target="tpu_custom_call" | custom-call | flops 4000000 | bytes 4000000 | tf_op jit(solution)/shard_map/pallas_call | solution.py:193
  43.0 0.0 all-to-all-done
  43.1 0.0 copy-start.8
  43.1 0.0 copy-start.9
  43.1 19.4 %shard_map.142 = f32[128,128]{1,0:T(8,128)S(1)} custom-call(bf16[1024,256]{1,0:T(8,128)(2,1)S(1)} %get-tuple-element.21.table, f32[640,128]{1,0:T(8,128)S(1)} %all_to_all.15.obs), custom_call_target="tpu_custom_call" | custom-call | flops 8000000000 | bytes 1000000 | tf_op jit(solution)/shard_map/pallas_call | solution.py:203
  62.6 15.8 %all_to_all.20 = f32[128,1,128]{2,1,0:T(1,128)S(1)} all-to-all(f32[128,1,128]{2,1,0:T(1,128)S(1)} %bitcast.30), channel_id=1, replica_groups=mesh['px'=8,'py'=16] {'px','py'}, dimensions={0} | all-to-all | bytes 131072 | tf_op jit(solution)/shard_map/all_to_all | solution.py:210
  78.3 0.0 copy-done.8
  78.3 0.0 copy-done.9
  78.3 0.6 fusion
  (1 shorter events, 0.0 us)
Async XLA Ops:
  1.7 0.8 %copy-start.3 = (s32[1,128,128]{2,1,0:T(8,128)S(1)}, s32[1,128,128]{2,1,0:T(8,128)}, u32[]{:S(2)}) copy-start(s32[1,128,128]{2,1,0:T(8,128)} %param.16) | copy-start | bytes 196612
  2.5 0.8 %copy-start.4 = (s32[1,128,128]{2,1,0:T(8,128)S(1)}, s32[1,128,128]{2,1,0:T(8,128)}, u32[]{:S(2)}) copy-start(s32[1,128,128]{2,1,0:T(8,128)} %param.17) | copy-start | bytes 196612
  3.4 0.8 %copy-start.5 = (f32[1,128,128]{2,1,0:T(8,128)S(1)}, f32[1,128,128]{2,1,0:T(8,128)}, u32[]{:S(2)}) copy-start(f32[1,128,128]{2,1,0:T(8,128)} %param.19) | copy-start | bytes 196612
  4.2 12.5 %copy-start = (f32[32,16,128]{2,1,0:T(8,128)S(1)}, f32[32,16,128]{2,1,0:T(8,128)}, u32[]{:S(2)}) copy-start(f32[32,16,128]{2,1,0:T(8,128)} %param.12) | copy-start | bytes 786436
  4.2 12.5 %copy-start.1 = (f32[32,16,128]{2,1,0:T(8,128)S(1)}, f32[32,16,128]{2,1,0:T(8,128)}, u32[]{:S(2)}) copy-start(f32[32,16,128]{2,1,0:T(8,128)} %param.13) | copy-start | bytes 786436
  4.2 12.5 %copy-start.2 = (f32[32,16,128]{2,1,0:T(8,128)S(1)}, f32[32,16,128]{2,1,0:T(8,128)}, u32[]{:S(2)}) copy-start(f32[32,16,128]{2,1,0:T(8,128)} %param.11) | copy-start | bytes 786436
  5.2 32.0 %copy-start.6 = (f32[32]{0:T(128)S(1)}, f32[32]{0:T(128)}, u32[]{:S(2)}) copy-start(f32[32]{0:T(128)} %hyper.1) | copy-start | bytes 388
  5.2 32.0 %copy-start.7 = (f32[32]{0:T(128)S(1)}, f32[32]{0:T(128)}, u32[]{:S(2)}) copy-start(f32[32]{0:T(128)} %damp.1) | copy-start | bytes 388
  5.2 37.8 %all-to-all-start = ((f32[128,5,128]{2,1,0:T(8,128)}), f32[128,5,128]{2,1,0:T(8,128)S(1)}, u32[]{:S(2)}, u32[]{:S(2)}) async-start(f32[128,5,128]{2,1,0:T(8,128)} %all_to_all.13), calls=%async_computation | async-start | bytes 1048576 | tf_op jit(solution)/shard_map/all_to_all | solution.py:183
  16.8 6.3 %collective-permute-start = (f32[192,128]{1,0:T(8,128)S(1)}, f32[192,128]{1,0:T(8,128)S(1)}, u32[]{:S(2)}, u32[]{:S(2)}) collective-permute-start(f32[192,128]{1,0:T(8,128)S(1)} %get-tuple-element.13), channel_id=1, source_target_pairs={{0,16},{16,32},{32,48},{48,64},{64,80},{80,96},{96,112},{112,0},{1... | collective-permute-start | bytes 294920 | tf_op jit(solution)/shard_map/ppermute | solution.py:181
  18.4 6.9 %collective-permute-start.1 = (f32[192,128]{1,0:T(8,128)S(1)}, f32[192,128]{1,0:T(8,128)S(1)}, u32[]{:S(2)}, u32[]{:S(2)}) collective-permute-start(f32[192,128]{1,0:T(8,128)S(1)} %get-tuple-element.14), channel_id=1, source_target_pairs={{0,112},{16,0},{32,16},{48,32},{64,48},{80,64},{96,80},{112,96},{1... | collective-permute-start | bytes 294920 | tf_op jit(solution)/shard_map/ppermute | solution.py:182
  25.7 6.4 %collective-permute-start.2 = (f32[36,128]{1,0:T(8,128)S(1)}, f32[36,128]{1,0:T(8,128)S(1)}, u32[]{:S(2)}, u32[]{:S(2)}) collective-permute-start(f32[36,128]{1,0:T(8,128)S(1)} %get-tuple-element.16), channel_id=1, source_target_pairs={{0,15},{1,0},{2,1},{3,2},{4,3},{5,4},{6,5},{7,6},{8,7},{9,8},{10,9... | collective-permute-start | bytes 55304 | tf_op jit(solution)/shard_map/ppermute | solution.py:190
  31.2 6.0 %collective-permute-start.3 = (f32[36,128]{1,0:T(8,128)S(1)}, f32[36,128]{1,0:T(8,128)S(1)}, u32[]{:S(2)}, u32[]{:S(2)}) collective-permute-start(f32[36,128]{1,0:T(8,128)S(1)} %get-tuple-element.17), channel_id=1, source_target_pairs={{0,1},{1,2},{2,3},{3,4},{4,5},{5,6},{6,7},{7,8},{8,9},{9,10},{10,1... | collective-permute-start | bytes 55304 | tf_op jit(solution)/shard_map/ppermute | solution.py:189
  43.1 35.2 %copy-start.8 = (f32[1,128,128]{2,1,0:T(8,128)S(1)}, f32[1,128,128]{2,1,0:T(8,128)}, u32[]{:S(2)}) copy-start(f32[1,128,128]{2,1,0:T(8,128)} %param.20) | copy-start | bytes 196612
  43.1 35.2 %copy-start.9 = (s32[1,128,128]{2,1,0:T(8,128)S(1)}, s32[1,128,128]{2,1,0:T(8,128)}, u32[]{:S(2)}) copy-start(s32[1,128,128]{2,1,0:T(8,128)} %param.21) | copy-start | bytes 196612

commit v2 on v1

v2 whole, which is shorter than its diff:
```python
import jax
import jax.numpy as jnp
from jax import lax
from jax.experimental import pallas as pl
from jax.experimental.pallas import tpu as pltpu
from jax.sharding import PartitionSpec as P

LEV = 32
CX = 16
CY = 128
FLAT = LEV * CX
FIELDS = 3
OBS = 5
SENT = OBS + FIELDS
ROWS = (0, 1, CX - 2, CX - 1)
BLOCKS = FIELDS * FLAT // 128
EDGE = 2 * FIELDS * LEV
UNROLL = 16
BOTH = ("px", "py")
F32 = jnp.float32
BF16 = jnp.bfloat16
VMEM = pl.BlockSpec(memory_space=pltpu.VMEM)
SMEM = pl.BlockSpec(memory_space=pltpu.SMEM)
HBM = pl.BlockSpec(memory_space=pltpu.MemorySpace.HBM)
PARAMS = pltpu.CompilerParams(vmem_limit_bytes=48 << 20)


WHOLE = pltpu.CompilerParams(vmem_limit_bytes=60 << 20)


def cost(flops, moved):
    return pl.CostEstimate(flops=flops, bytes_accessed=moved, transcendentals=0)


def diagonal(move_x, move_y):
    count_x, count_y = lax.axis_size("px"), lax.axis_size("py")
    x = lax.rem(lax.axis_index("px") + count_x + move_x, count_x)
    return x * count_y + lax.rem(lax.axis_index("py") + count_y + move_y, count_y)


def messages_out(u, v, t, cells, levels, bary, vfrac, sent, fields, ints, floats, weights, packed, turn, sems):
    copies = [
        pltpu.make_async_copy(u, fields.at[0], sems.at[0]),
        pltpu.make_async_copy(v, fields.at[1], sems.at[1]),
        pltpu.make_async_copy(t, fields.at[2], sems.at[2]),
        pltpu.make_async_copy(cells, ints.at[0], sems.at[3]),
        pltpu.make_async_copy(levels, ints.at[1], sems.at[4]),
        pltpu.make_async_copy(vfrac, floats, sems.at[5]),
        pltpu.make_async_copy(bary.at[pl.ds(0, 2)], weights, sems.at[6]),
    ]
    for copy in copies:
        copy.start()
    packed[:, OBS:, :] = jnp.zeros((packed.shape[0], FIELDS, CY), F32)
    for copy in copies:
        copy.wait()
    packed[:, 0, :] = ints[0].astype(F32)
    packed[:, 1, :] = ints[1].astype(F32)
    packed[:, 2, :] = floats[...]
    packed[:, 3, :] = weights[0]
    packed[:, 4, :] = weights[1]
    half = lax.broadcasted_iota(jnp.int32, (1, CY), 1) < CY // 2
    for f in range(FIELDS):
        for i, r in enumerate(ROWS):
            turn[i * LEV : (i + 1) * LEV, :] = fields[f, pl.ds(r, LEV, stride=CX), :]
        turned = turn[...].T
        for move_y, c in ((-1, 0), (1, CY - 2)):
            one, two = turned[c : c + 1, :], turned[c + 1 : c + 2, :]
            row = OBS + f
            packed[diagonal(-1, move_y), row : row + 1, :] = jnp.where(
                half, one, pltpu.roll(two, CY // 2, 1)
            )
            packed[diagonal(1, move_y), row : row + 1, :] = jnp.where(
                half, pltpu.roll(one, CY // 2, 1), two
            )
    pltpu.sync_copy(packed, sent)


def edges_out(u, v, t, first, last, low, high):
    for f, field in enumerate((u, v, t)):
        for i in range(2):
            at = (i * FIELDS + f) * LEV
            low[at : at + LEV, :] = field[pl.ds(i, LEV, stride=CX), :]
            high[at : at + LEV, :] = field[pl.ds(CX - 2 + i, LEV, stride=CX), :]
        for k in range(FLAT // 128):
            turned = field[k * 128 : (k + 1) * 128, :].T
            at = 2 * (f * FLAT // 128 + k)
            first[at : at + 2, :] = turned[0:2, :]
            last[at : at + 2, :] = turned[CY - 2 :, :]


def shifted(lane, field, border, b):
    if b > 0:
        return pltpu.roll(jnp.where(lane < b, border, field), CY - b, 1)
    return pltpu.roll(jnp.where(lane >= CY + b, border, field), -b, 1)


def spread(turn, ahead, behind):
    turn[0:2, :] = ahead
    turn[CY - 2 :, :] = behind
    return turn[...].T


def inner(u, v, t, east, west, hyper, damp, u_out, v_out, t_out, pick, side, turn):
    turn[...] = jnp.zeros_like(turn)
    for k in range(BLOCKS):
        side[k * 128 : (k + 1) * 128, :] = spread(
            turn, east[2 * k : 2 * k + 2, :], west[2 * k : 2 * k + 2, :]
        )
    lane = lax.broadcasted_iota(jnp.int32, (CX, CY), 1)
    none = jnp.zeros((8, CY), F32)

    def rows(value, a):
        return pltpu.roll(jnp.concatenate([value, none], axis=0), -a % (CX + 8), 0)[:CX, :]

    def level(lev, carry):
        coef = hyper[lev]
        quarter = damp[lev] * 0.25
        at = pl.multiple_of(lev * CX, 8)
        views = []
        fourth = []
        for f, field in enumerate((u, v, t)):
            c = field[pl.ds(at, CX), :]
            h = side[pl.ds(f * FLAT + at, CX), :]
            e1, e2, w1, w2 = (shifted(lane, c, h, b) for b in (1, 2, -1, -2))
            total = 42.0 * c - 10.0 * (e1 + w1) + (e2 + w2)
            total = total + rows(2.0 * (e1 + w2) - 10.0 * (c + w1), 1)
            total = total + rows(2.0 * (w1 + e2) - 10.0 * (c + e1), -1)
            total = total + rows(c + w2 + 2.0 * w1, 2) + rows(c + e2 + 2.0 * e1, -2)
            fourth.append(total)
            views.append((c, e1, w1, e2, w2))
        (u0, ue, uw, _, _), (v0, ve, vw, ve2, vw2), (t0, te, tw, _, _) = views
        du, dv = ue - uw, ve - vw
        uxx = rows(u0, 2) - 2.0 * u0 + rows(u0, -2)
        vxy = rows(dv, 1) - rows(dv, -1)
        uxy = rows(du, 1) - rows(du, -1)
        vyy = ve2 - 2.0 * v0 + vw2
        u_out[pl.ds(at, CX), :] = u0 - coef * fourth[0] + quarter * (uxx + vxy)
        v_out[pl.ds(at, CX), :] = v0 - coef * fourth[1] + quarter * (uxy + vyy)
        drift = u0 * (rows(t0, 1) - rows(t0, -1)) + v0 * (te - tw)
        t_out[pl.ds(at, CX), :] = t0 - coef * fourth[2] - 0.25 * drift
        return carry

    lax.fori_loop(0, LEV, level, 0, unroll=4)
    k = lax.broadcasted_iota(jnp.int32, pick.shape, 0)
    n = lax.broadcasted_iota(jnp.int32, pick.shape, 1)
    want = ((n >> 5) & 3) * CY + (n & 31) * 4 + (n >> 7)
    pick[...] = jnp.where(k == want, 1.0, 0.0).astype(BF16)


def per_level(coef, quarter, hyper, damp):
    for lev in range(LEV):
        coef[lev : lev + 1, :] = jnp.full((1, CY), hyper[lev], F32)
        quarter[lev : lev + 1, :] = jnp.full((1, CY), damp[lev] * 0.25, F32)


def one(line, sign):
    c, e1, e2, w1, w2 = line
    if sign > 0:
        return 2.0 * (e1 + w2) - 10.0 * (c + w1)
    return 2.0 * (w1 + e2) - 10.0 * (c + e1)


def two(line, sign):
    c, e1, e2, w1, w2 = line
    return c + w2 + 2.0 * w1 if sign > 0 else c + e2 + 2.0 * e1


def add(out, r, value):
    out[pl.ds(r, LEV, stride=CX), :] += value


def add_rows(u_out, v_out, t_out, near, far, sign, k4, k2, wind):
    edge, following = (CX - 1, CX - 2) if sign > 0 else (0, 1)
    cross = [line[1] - line[3] for line in near]
    fourth = [one(near[f], sign) + two(far[f], sign) for f in range(FIELDS)]
    add(u_out, edge, k2 * (far[0][0] + sign * cross[1]) - k4 * fourth[0])
    add(u_out, following, k2 * near[0][0] - k4 * two(near[0], sign))
    add(v_out, edge, k2 * (sign * cross[0]) - k4 * fourth[1])
    add(v_out, following, -k4 * two(near[1], sign))
    add(t_out, edge, -k4 * fourth[2] - (0.25 * sign) * wind * near[2][0])
    add(t_out, following, -k4 * two(near[2], sign))


def finish(u, u_in, v_in, t_in, above, below, hyper, damp, pick, u_out, v_out, t_out, table, coef, quarter):
    per_level(coef, quarter, hyper, damp)
    u_out[...] = u_in[...]
    v_out[...] = v_in[...]
    t_out[...] = t_in[...]
    lane = lax.broadcasted_iota(jnp.int32, (LEV, CY), 1)
    none = jnp.zeros((LEV, CY), F32)

    def outside(rows, i):
        line = []
        for f in range(FIELDS):
            c = rows[(i * FIELDS + f) * LEV : (i * FIELDS + f + 1) * LEV, :]
            line.append((c,) + tuple(shifted(lane, c, none, b) for b in (1, 2, -1, -2)))
        return line

    for sign, rows, near, far in ((-1, above, 1, 0), (1, below, 0, 1)):
        wind = u[pl.ds(0 if sign < 0 else CX - 1, LEV, stride=CX), :]
        add_rows(
            u_out, v_out, t_out, outside(rows, near), outside(rows, far), sign, coef[...], quarter[...], wind
        )
    for rl in range(4):
        parts = [t_out[pl.ds(4 * rh + rl, LEV, stride=CX), :] for rh in range(4)]
        tops = [part.astype(BF16) for part in parts]
        rests = [(part - top.astype(F32)).astype(BF16) for part, top in zip(parts, tops)]
        both = jnp.concatenate(
            [jnp.concatenate(tops, axis=1), jnp.concatenate(rests, axis=1)], axis=0
        )
        put = jnp.dot(both, pick[...], preferred_element_type=F32)
        for half in range(2):
            lanes = slice(half * 128, half * 128 + 128)
            for cl in range(4):
                x = put[half * LEV : (half + 1) * LEV, cl * 128 : (cl + 1) * 128]
                table[(rl * 5 + cl) * LEV : (rl * 5 + cl + 1) * LEV, lanes] = x.astype(BF16)
                if cl == 0:
                    table[(rl * 5 + 4) * LEV : (rl * 5 + 5) * LEV, lanes] = pltpu.roll(
                        x, 127, 1
                    ).astype(BF16)
                if rl == 0:
                    table[(20 + cl) * LEV : (21 + cl) * LEV, lanes] = pltpu.roll(x, 96, 1).astype(BF16)


def corner_lines(obs, turn, f):
    turn[...] = jnp.zeros_like(turn)
    row = OBS + f
    half = lax.broadcasted_iota(jnp.int32, (1, CY), 1) < CY // 2
    for move_y, c in ((1, 0), (-1, CY - 2)):
        upper = obs[diagonal(-1, move_y), row : row + 1, :]
        lower = obs[diagonal(1, move_y), row : row + 1, :]
        turn[c : c + 1, :] = jnp.where(half, upper, pltpu.roll(lower, CY // 2, 1))
        turn[c + 1 : c + 2, :] = jnp.where(half, pltpu.roll(upper, CY // 2, 1), lower)
    spots = turn[...].T
    lane = lax.broadcasted_iota(jnp.int32, (LEV, CY), 1)
    none = jnp.zeros((LEV, CY), F32)
    lines = []
    for i in range(4):
        h = spots[i * LEV : (i + 1) * LEV, :]
        lines.append((none,) + tuple(shifted(lane, none, h, b) for b in (1, 2, -1, -2)))
    return lines


def corners(obs, u_in, v_in, t_in, hyper, damp, u_out, v_out, t_out, turn, coef, quarter):
    per_level(coef, quarter, hyper, damp)
    u_out[...] = u_in[...]
    v_out[...] = v_in[...]
    t_out[...] = t_in[...]
    lines = [corner_lines(obs, turn, f) for f in range(FIELDS)]
    none = jnp.zeros((LEV, CY), F32)
    for sign, near, far in ((-1, 1, 0), (1, 2, 3)):
        add_rows(
            u_out,
            v_out,
            t_out,
            [line[near] for line in lines],
            [line[far] for line in lines],
            sign,
            coef[...],
            quarter[...],
            none,
        )


def interpolate(start, obs, t, hyper, model, table, block, row, col, lev, turn, coef):
    table[...] = start[...]
    for k in range(LEV):
        coef[k : k + 1, :] = jnp.full((1, CY), hyper[k], F32)
    far_up, near_up, near_down, far_down = corner_lines(obs, turn, 2)
    terms = (
        one(near_up, -1) + two(far_up, -1),
        two(near_up, -1),
        two(near_down, 1),
        one(near_down, 1) + two(far_down, 1),
    )
    lane = lax.broadcasted_iota(jnp.int32, (LEV, CY), 1)
    for r, term in zip(ROWS, terms):
        value = t[pl.ds(r, LEV, stride=CX), :] - coef[...] * term
        for c in (0, 1, CY - 2, CY - 1):
            to = (r >> 2) * 32 + (c >> 2)
            moved = pltpu.roll(value, (to - c) % CY, 1)
            high = moved.astype(BF16).astype(F32)
            at = ((r & 3) * 5 + (c & 3)) * LEV
            for k, part in enumerate((high, moved - high)):
                old = table[at : at + LEV, k * CY : (k + 1) * CY].astype(F32)
                table[at : at + LEV, k * CY : (k + 1) * CY] = jnp.where(lane == to, part, old).astype(BF16)
    owners = model.shape[0]
    cell = obs[:, 0, :].astype(jnp.int32)
    c, r = cell & (CY - 1), cell >> 7
    block[...] = (r >> 2) * 32 + (c >> 2)
    row[...] = r & 3
    col[...] = c & 3
    lev[...] = obs[:, 1, :].astype(jnp.int32)
    wide = 256
    block_iota = lax.broadcasted_iota(jnp.int32, (128, wide), 0)
    lev_iota = lax.broadcasted_iota(jnp.int32, (LEV, wide), 0)

    def pair(p, carry):
        def two(ref):
            return jnp.concatenate([ref[pl.ds(2 * p, 1), :], ref[pl.ds(2 * p + 1, 1), :]], axis=1)

        def sent(k):
            return jnp.concatenate([obs[2 * p, k : k + 1, :], obs[2 * p + 1, k : k + 1, :]], axis=1)

        def bit(value, mask):
            return jnp.broadcast_to(value & mask, (LEV, wide)) != 0

        at, r, c, l = two(block), two(row), two(col), two(lev)
        a, w0, w1 = sent(2), sent(3), sent(4)
        w2 = 1.0 - w0 - w1
        hot = jnp.where(block_iota == at, 1.0, 0.0).astype(BF16)
        got = jnp.dot(
            table[...], jnp.concatenate([hot, hot], axis=0), preferred_element_type=F32
        )
        c1, c2, r1, r2 = bit(c, 1), bit(c, 2), bit(r, 1), bit(r, 2)
        here, beside = [], []
        for i in range(5):
            g = [got[(i * 5 + j) * LEV : (i * 5 + j + 1) * LEV, :] for j in range(5 if i < 4 else 4)]
            h1 = jnp.where(c2, g[3], g[1])
            here.append(jnp.where(c1, h1, jnp.where(c2, g[2], g[0])))
            if i < 4:
                beside.append(jnp.where(c1, jnp.where(c2, g[4], g[2]), h1))
        h0, h1, h2 = (jnp.where(r2, here[i + 2], here[i]) for i in range(3))
        t0, t1 = jnp.where(r1, h1, h0), jnp.where(r1, h2, h1)
        t2 = jnp.where(
            r1, jnp.where(r2, beside[3], beside[1]), jnp.where(r2, beside[2], beside[0])
        )
        weight = jnp.where(lev_iota == l, 1.0 - a, jnp.where(lev_iota == l + 1, a, 0.0))
        out = jnp.sum(weight * (w0 * t0 + w1 * t1 + w2 * t2), axis=0, keepdims=True)
        model[pl.ds(2 * p, 1), :] = out[:, :128]
        model[pl.ds(2 * p + 1, 1), :] = out[:, 128:]
        return carry

    lax.fori_loop(0, owners // 2, pair, 0, unroll=UNROLL)


def neighbour(axis, move):
    count = lax.axis_size(axis)
    return [(i, (i + move) % count) for i in range(count)]


def on_device(theta, wind_u, wind_v, hyper, damp, cells, levels, bary, vfrac, values, mask):
    u, v, t = (f.reshape(FLAT, CY) for f in (wind_u, wind_v, theta))
    owners, slots = cells.shape[1], cells.shape[2]
    shape = jax.ShapeDtypeStruct
    sent = pl.pallas_call(
        messages_out,
        out_shape=shape((owners, SENT, slots), F32),
        in_specs=[HBM] * 7,
        out_specs=HBM,
        scratch_shapes=[
            pltpu.VMEM((FIELDS, FLAT, CY), F32),
            pltpu.VMEM((2, owners, slots), jnp.int32),
            pltpu.VMEM((owners, slots), F32),
            pltpu.VMEM((2, owners, slots), F32),
            pltpu.VMEM((owners, SENT, slots), F32),
            pltpu.VMEM((CY, CY), F32),
            pltpu.SemaphoreType.DMA((7,)),
        ],
        compiler_params=WHOLE,
        cost_estimate=cost(100000, 3000000),
    )(u, v, t, cells[0], levels[0], jnp.swapaxes(bary[0], 0, 1), vfrac[0])
    got = lax.all_to_all(sent, BOTH, split_axis=0, concat_axis=0, tiled=True)
    columns = shape((2 * BLOCKS, CY), F32)
    edge = shape((EDGE, CY), F32)
    first, last, low, high = pl.pallas_call(
        edges_out,
        out_shape=(columns, columns, edge, edge),
        in_specs=[VMEM] * 3,
        compiler_params=PARAMS,
        cost_estimate=cost(100000, 1000000),
    )(u, v, t)
    west = lax.ppermute(last, "py", neighbour("py", 1))
    east = lax.ppermute(first, "py", neighbour("py", -1))
    above = lax.ppermute(high, "px", neighbour("px", 1))
    below = lax.ppermute(low, "px", neighbour("px", -1))
    patch = shape((FLAT, CY), F32)
    turn = pltpu.VMEM((CY, CY), F32)
    each = pltpu.VMEM((LEV, CY), F32)
    u_part, v_part, t_part, pick = pl.pallas_call(
        inner,
        out_shape=(patch, patch, patch, shape((4 * CY, 4 * CY), BF16)),
        in_specs=[VMEM] * 5 + [SMEM] * 2,
        scratch_shapes=[pltpu.VMEM((FIELDS * FLAT, CY), F32), turn],
        compiler_params=PARAMS,
        cost_estimate=cost(8000000, 3000000),
    )(u, v, t, east, west, hyper, damp)
    u_most, v_most, t_most, table = pl.pallas_call(
        finish,
        out_shape=(patch, patch, patch, shape((24 * LEV, 2 * CY), BF16)),
        in_specs=[VMEM] * 6 + [SMEM] * 2 + [VMEM],
        scratch_shapes=[each, each],
        compiler_params=PARAMS,
        cost_estimate=cost(4000000, 3000000),
    )(u, u_part, v_part, t_part, above, below, hyper, damp, pick)
    model = pl.pallas_call(
        interpolate,
        out_shape=shape((owners, slots), F32),
        in_specs=[VMEM] * 3 + [SMEM],
        scratch_shapes=[pltpu.VMEM((24 * LEV, 2 * CY), BF16)]
        + [pltpu.VMEM((owners, slots), jnp.int32)] * 4
        + [turn, each],
        compiler_params=PARAMS,
        cost_estimate=cost(6500000000, 1000000),
    )(table, got, t_most, hyper)
    u_next, v_next, t_next = pl.pallas_call(
        corners,
        out_shape=(patch, patch, patch),
        in_specs=[VMEM] * 4 + [SMEM] * 2,
        scratch_shapes=[turn, each, each],
        compiler_params=PARAMS,
        cost_estimate=cost(4000000, 3000000),
    )(got, u_most, v_most, t_most, hyper, damp)
    back = lax.all_to_all(model, BOTH, split_axis=0, concat_axis=0, tiled=True)
    departures = mask.astype(F32) * (values - back[None])
    whole = theta.shape
    return t_next.reshape(whole), u_next.reshape(whole), v_next.reshape(whole), departures


def solution(mesh):
    field = P(None, "px", "py")
    obs = P(BOTH, None, None)
    return jax.shard_map(
        on_device,
        mesh=mesh,
        in_specs=(field, field, field, P(), P(), obs, obs, P(BOTH, None, None, None), obs, obs, obs),
        out_specs=(field, field, field, obs),
        check_vma=False,
    )
```

time: 79.3 us -> 59.3 us (0.75)
  blocking collectives: 15.8 us -> 0 us
  Pallas kernels: 25.9 us -> 18.6 us
  starting transfers between devices: 18.6 us -> 24.9 us
  local copies, waits for them, and re-layouts: 4.51 us -> 0.04 us
  waiting for transfers between devices: 12.8 us -> 14.2 us
    all_to_all x1 -> x0, blocking collectives: 15.8 us -> none  [on_device(): back = lax.all_to_all(model, BOTH, split_axis=0, concat_axis=0, tiled=True)]
    all_to_all x0 -> x1, waiting for transfers between devices: none -> 7.98 us  [on_device(): back = lax.all_to_all(model, BOTH, split_axis=0, concat_axis=0, tiled=True)]
    pallas_call x5 -> x6, Pallas kernels: 25.9 us -> 18.6 us  [the longest x1 10.1 us: on_device(): pl.pallas_call(interpolate, out_shape=shape((owners, slots), F32), in_spe...]
    all_to_all x0 -> x1, starting transfers between devices: none -> 6.35 us  [on_device(): back = lax.all_to_all(model, BOTH, split_axis=0, concat_axis=0, tiled=True)]
    ppermute x1, waiting for transfers between devices: 4.69 us -> 0.01 us  [on_device(): above = lax.ppermute(high, 'px', neighbour('px', 1))]
    unnamed x21 -> x14, local copies, waits for them, and re-layouts: 3.61 us -> 0.04 us
    ppermute x1, waiting for transfers between devices: 2.2 us -> 0.01 us  [on_device(): below = lax.ppermute(low, 'px', neighbour('px', -1))]
    all_to_all x2 -> x0, local copies, waits for them, and re-layouts: 0.9 us -> none  [on_device(): got = lax.all_to_all(sent, BOTH, split_axis=0, concat_axis=0, tiled=True)]
  transfers between devices with their start and end apart: 5 -> 6, of which waited for: 4 -> 3; matrix products, arithmetic and copies ran while one was open for 0% -> 0% of each run, Pallas kernels for 8% -> 10%
where the time goes in v2:
time: 59.3 us; the launch traced here: 59.1 us
  starting transfers between devices  24.9 us (42%)
  Pallas kernels  18.6 us (31%)
  waiting for transfers between devices  14.2 us (24%)
  between operations  0.76 us (1%)
  other arithmetic  0.64 us (1%)
    all_to_all x1, starting transfers between devices, on_device(): got = lax.all_to_all(sent, BOTH, split_axis=0, concat_axis=0, tiled=True)  11.5 us
    pallas_call x1, Pallas kernels, on_device(): pl.pallas_call(interpolate, out_shape=shape((owners, slots), F32), in_spe...  10.1 us
    all_to_all x1, waiting for transfers between devices, on_device(): back = lax.all_to_all(model, BOTH, split_axis=0, concat_axis=0, tiled=True)  7.98 us
    all_to_all x1, starting transfers between devices, on_device(): back = lax.all_to_all(model, BOTH, split_axis=0, concat_axis=0, tiled=True)  6.35 us
    ppermute x1, starting transfers between devices, on_device(): east = lax.ppermute(first, 'py', neighbour('py', -1))  5.38 us
    ppermute x1, waiting for transfers between devices, on_device(): west = lax.ppermute(last, 'py', neighbour('py', 1))  5.36 us
    pallas_call x1, Pallas kernels, on_device(): pl.pallas_call(inner, out_shape=(patch, patch, patch, shape((4 * CY, 4 *...  2.79 us
    pallas_call x1, Pallas kernels, on_device(): pl.pallas_call(messages_out, out_shape=shape((owners, SENT, slots), F32),...  2.32 us
  transfers between devices with their start and end apart: 6, of which 3 were waited for; matrix products, arithmetic and copies ran while one was open for 0% of the time, Pallas kernels for 10%

profile of v2, /device:TPU:1, one launch (start us, length us, event | category | flops | bytes accessed | tf_op | source)
XLA Modules:
  0.0 59.1 jit_solution(132469301202094847)
XLA Ops:
  0.6 2.3 %shard_map.138 = f32[128,8,128]{2,1,0:T(8,128)} custom-call(f32[512,128]{1,0:T(8,128)} %bitcast.20, f32[512,128]{1,0:T(8,128)} %bitcast.24, f32[512,128]{1,0:T(8,128)} %bitcast.27, s32[128,128]{1,0:T(8,128)} %bitcast.32, s32[128,128]{1,0:T(8,128)} %bitcast.33, f32[3,128,128]{2,1,0:T(8,128)} %bitcast.31, f32[128,128]{1,0:T(8,128)} %bitcast.34), custom_call_target="tpu_custom_call" | custom-call | flops 100000 | bytes 3000000 | tf_op jit(solution)/shard_map/pallas_call | solution.py:346
  3.0 0.0 copy-start
  3.0 0.0 copy-start.1
  3.0 0.0 copy-start.2
  3.0 11.5 %all-to-all-start = ((f32[128,8,128]{2,1,0:T(8,128)}), f32[128,8,128]{2,1,0:T(8,128)S(1)}, u32[]{:S(2)}, u32[]{:S(2)}) async-start(f32[128,8,128]{2,1,0:T(8,128)} %shard_map.138), calls=%async_computation | async-start | bytes 1048576 | tf_op jit(solution)/shard_map/all_to_all | solution.py:363
  14.5 0.0 copy-done
  14.5 0.0 copy-done.1
  14.5 0.0 copy-done.2
  14.5 0.3 shard_map.139
  14.8 1.6 %collective-permute-start.2 = (f32[192,128]{1,0:T(8,128)S(1)}, f32[192,128]{1,0:T(8,128)S(1)}, u32[]{:S(2)}, u32[]{:S(2)}) collective-permute-start(f32[192,128]{1,0:T(8,128)S(1)} %get-tuple-element.24), channel_id=1, source_target_pairs={{0,16},{16,32},{32,48},{48,64},{64,80},{80,96},{96,112},{112,0},{1... | collective-permute-start | bytes 294920 | tf_op jit(solution)/shard_map/ppermute | solution.py:375
  16.4 0.0 collective-permute-start.3
  16.5 0.0 copy-start.3
  16.5 0.0 copy-start.4
  16.5 5.4 %collective-permute-start = (f32[24,128]{1,0:T(8,128)S(1)}, f32[24,128]{1,0:T(8,128)S(1)}, u32[]{:S(2)}, u32[]{:S(2)}) collective-permute-start(f32[24,128]{1,0:T(8,128)S(1)} %get-tuple-element.19), channel_id=1, source_target_pairs={{0,15},{1,0},{2,1},{3,2},{4,3},{5,4},{6,5},{7,6},{8,7},{9,8},{10,9... | collective-permute-start | bytes 36872 | tf_op jit(solution)/shard_map/ppermute | solution.py:374
  21.8 0.0 collective-permute-start.1
  21.8 0.8 %collective-permute-done.east = f32[24,128]{1,0:T(8,128)S(1)} collective-permute-done((f32[24,128]{1,0:T(8,128)S(1)}, f32[24,128]{1,0:T(8,128)S(1)}, u32[]{:S(2)}, u32[]{:S(2)}) %collective-permute-start) | collective-permute-done | bytes 12320 | tf_op jit(solution)/shard_map/ppermute | solution.py:374
  22.7 5.4 %collective-permute-done.1.west = f32[24,128]{1,0:T(8,128)S(1)} collective-permute-done((f32[24,128]{1,0:T(8,128)S(1)}, f32[24,128]{1,0:T(8,128)S(1)}, u32[]{:S(2)}, u32[]{:S(2)}) %collective-permute-start.1) | collective-permute-done | bytes 12320 | tf_op jit(solution)/shard_map/ppermute | solution.py:373
  28.0 0.0 copy-done.3
  28.0 0.0 copy-done.4
  28.0 2.8 %shard_map.140 = (f32[512,128]{1,0:T(8,128)S(1)}, f32[512,128]{1,0:T(8,128)S(1)}, f32[512,128]{1,0:T(8,128)S(1)}, bf16[512,512]{1,0:T(8,128)(2,1)S(1)}) custom-call(f32[512,128]{1,0:T(8,128)S(1)} %bitcast.22, f32[512,128]{1,0:T(8,128)S(1)} %bitcast.26, f32[512,128]{1,0:T(8,128)S(1)} %bitcast.29, f32[24,128]{1,0:T(8,128)S(1)} %collective-permute-done.east, ...), custom_call_target="tpu_custom_call" | custom-call | flops 8000000 | bytes 3000000 | tf_op jit(solution)/shard_map/pallas_call | solution.py:380
  30.8 0.0 collective-permute-done.2.above
  30.8 0.0 collective-permute-done.3.below
  30.9 1.3 %shard_map.141 = (f32[512,128]{1,0:T(8,128)S(1)}, f32[512,128]{1,0:T(8,128)S(1)}, f32[512,128]{1,0:T(8,128)S(1)}, bf16[768,256]{1,0:T(8,128)(2,1)S(1)}) custom-call(f32[512,128]{1,0:T(8,128)S(1)} %bitcast.23, f32[512,128]{1,0:T(8,128)S(1)} %get-tuple-element.21.u_in, f32[512,128]{1,0:T(8,128)S(1)} %get-tuple-element.22.v_in, ...), custom_call_target="tpu_custom_call" | custom-call | flops 4000000 | bytes 3000000 | tf_op jit(solution)/shard_map/pallas_call | solution.py:388
  32.1 0.0 all-to-all-done.obs
  32.1 10.1 %shard_map.143 = f32[128,128]{1,0:T(8,128)} custom-call(bf16[768,256]{1,0:T(8,128)(2,1)S(1)} %get-tuple-element.33.start, f32[128,8,128]{2,1,0:T(8,128)S(1)} %all-to-all-done.obs, f32[512,128]{1,0:T(8,128)S(1)} %get-tuple-element.29.t_in.t, f32[32]{0:T(128)S(1)} %copy-done.3), custom_call_target="tpu_custom_call" | custom-call | flops 6499999744 | bytes 1000000 | tf_op jit(solution)/shard_map/pallas_call | solution.py:396
  42.3 6.4 %all-to-all-start.1 = ((f32[128,1,128]{2,1,0:T(1,128)}), f32[128,1,128]{2,1,0:T(1,128)S(1)}, u32[]{:S(2)}, u32[]{:S(2)}) async-start(f32[128,1,128]{2,1,0:T(1,128)} %bitcast.12), calls=%async_computation.1 | async-start | bytes 131072 | tf_op jit(solution)/shard_map/all_to_all | solution.py:414
  48.6 0.0 copy-start.5
  48.7 0.0 copy-start.6
  48.7 1.8 %shard_map.142 = (f32[512,128]{1,0:T(8,128)}, f32[512,128]{1,0:T(8,128)}, f32[512,128]{1,0:T(8,128)}) custom-call(f32[128,8,128]{2,1,0:T(8,128)S(1)} %all-to-all-done.obs, f32[512,128]{1,0:T(8,128)S(1)} %get-tuple-element.27.u_in, f32[512,128]{1,0:T(8,128)S(1)} %get-tuple-element.28.v_in, f32[512,128]{1,0:T(8,128)S(1)} %get-tuple-element.29.t_in.t, ...), custom_call_target="tpu_custom_call" | custom-call | flops 4000000 | bytes 3000000 | tf_op jit(solution)/shard_map/pallas_call | solution.py:406
  50.5 8.0 %all-to-all-done.1 = f32[128,1,128]{2,1,0:T(1,128)S(1)} async-done(((f32[128,1,128]{2,1,0:T(1,128)}), f32[128,1,128]{2,1,0:T(1,128)S(1)}, u32[]{:S(2)}, u32[]{:S(2)}) %all-to-all-start.1) | async-done | bytes 65568 | tf_op jit(solution)/shard_map/all_to_all | solution.py:414
  58.5 0.0 copy-done.5
  58.5 0.0 copy-done.6
  58.5 0.6 %fusion = f32[1,128,128]{2,1,0:T(8,128)} fusion(f32[1,128,128]{2,1,0:T(8,128)S(1)} %copy-done.5, s32[1,128,128]{2,1,0:T(8,128)S(1)} %copy-done.6, f32[1,128,128]{2,1,0:T(8,128)S(1)} %bitcast.30), kind=kLoop, calls=%fused_computation.1 | loop fusion | flops 49152 | bytes 262144 | tf_op jit(solution)/shard_map/mul | solution.py:415
Async XLA Ops:
  3.0 11.5 %copy-start = (f32[32,16,128]{2,1,0:T(8,128)S(1)}, f32[32,16,128]{2,1,0:T(8,128)}, u32[]{:S(2)}) copy-start(f32[32,16,128]{2,1,0:T(8,128)} %param.12) | copy-start | bytes 786436
  3.0 11.5 %copy-start.1 = (f32[32,16,128]{2,1,0:T(8,128)S(1)}, f32[32,16,128]{2,1,0:T(8,128)}, u32[]{:S(2)}) copy-start(f32[32,16,128]{2,1,0:T(8,128)} %param.13) | copy-start | bytes 786436
  3.0 11.5 %copy-start.2 = (f32[32,16,128]{2,1,0:T(8,128)S(1)}, f32[32,16,128]{2,1,0:T(8,128)}, u32[]{:S(2)}) copy-start(f32[32,16,128]{2,1,0:T(8,128)} %param.11) | copy-start | bytes 786436
  3.0 29.1 %all-to-all-start = ((f32[128,8,128]{2,1,0:T(8,128)}), f32[128,8,128]{2,1,0:T(8,128)S(1)}, u32[]{:S(2)}, u32[]{:S(2)}) async-start(f32[128,8,128]{2,1,0:T(8,128)} %shard_map.138), calls=%async_computation | async-start | bytes 1048576 | tf_op jit(solution)/shard_map/all_to_all | solution.py:363
  14.8 16.0 %collective-permute-start.2 = (f32[192,128]{1,0:T(8,128)S(1)}, f32[192,128]{1,0:T(8,128)S(1)}, u32[]{:S(2)}, u32[]{:S(2)}) collective-permute-start(f32[192,128]{1,0:T(8,128)S(1)} %get-tuple-element.24), channel_id=1, source_target_pairs={{0,16},{16,32},{32,48},{48,64},{64,80},{80,96},{96,112},{112,0},{1... | collective-permute-start | bytes 294920 | tf_op jit(solution)/shard_map/ppermute | solution.py:375
  16.4 14.4 %collective-permute-start.3 = (f32[192,128]{1,0:T(8,128)S(1)}, f32[192,128]{1,0:T(8,128)S(1)}, u32[]{:S(2)}, u32[]{:S(2)}) collective-permute-start(f32[192,128]{1,0:T(8,128)S(1)} %get-tuple-element.25), channel_id=1, source_target_pairs={{0,112},{16,0},{32,16},{48,32},{64,48},{80,64},{96,80},{112,96},{1... | collective-permute-start | bytes 294920 | tf_op jit(solution)/shard_map/ppermute | solution.py:376
  16.5 11.6 %copy-start.3 = (f32[32]{0:T(128)S(1)}, f32[32]{0:T(128)}, u32[]{:S(2)}) copy-start(f32[32]{0:T(128)} %hyper.7) | copy-start | bytes 388
  16.5 11.6 %copy-start.4 = (f32[32]{0:T(128)S(1)}, f32[32]{0:T(128)}, u32[]{:S(2)}) copy-start(f32[32]{0:T(128)} %damp.5) | copy-start | bytes 388
  16.5 6.2 %collective-permute-start = (f32[24,128]{1,0:T(8,128)S(1)}, f32[24,128]{1,0:T(8,128)S(1)}, u32[]{:S(2)}, u32[]{:S(2)}) collective-permute-start(f32[24,128]{1,0:T(8,128)S(1)} %get-tuple-element.19), channel_id=1, source_target_pairs={{0,15},{1,0},{2,1},{3,2},{4,3},{5,4},{6,5},{7,6},{8,7},{9,8},{10,9... | collective-permute-start | bytes 36872 | tf_op jit(solution)/shard_map/ppermute | solution.py:374
  21.8 6.2 %collective-permute-start.1 = (f32[24,128]{1,0:T(8,128)S(1)}, f32[24,128]{1,0:T(8,128)S(1)}, u32[]{:S(2)}, u32[]{:S(2)}) collective-permute-start(f32[24,128]{1,0:T(8,128)S(1)} %get-tuple-element.20), channel_id=1, source_target_pairs={{0,1},{1,2},{2,3},{3,4},{4,5},{5,6},{6,7},{7,8},{8,9},{9,10},{10,1... | collective-permute-start | bytes 36872 | tf_op jit(solution)/shard_map/ppermute | solution.py:373
  42.3 16.2 %all-to-all-start.1 = ((f32[128,1,128]{2,1,0:T(1,128)}), f32[128,1,128]{2,1,0:T(1,128)S(1)}, u32[]{:S(2)}, u32[]{:S(2)}) async-start(f32[128,1,128]{2,1,0:T(1,128)} %bitcast.12), calls=%async_computation.1 | async-start | bytes 131072 | tf_op jit(solution)/shard_map/all_to_all | solution.py:414
  48.6 9.8 %copy-start.5 = (f32[1,128,128]{2,1,0:T(8,128)S(1)}, f32[1,128,128]{2,1,0:T(8,128)}, u32[]{:S(2)}) copy-start(f32[1,128,128]{2,1,0:T(8,128)} %param.20) | copy-start | bytes 196612
  48.7 9.8 %copy-start.6 = (s32[1,128,128]{2,1,0:T(8,128)S(1)}, s32[1,128,128]{2,1,0:T(8,128)}, u32[]{:S(2)}) copy-start(s32[1,128,128]{2,1,0:T(8,128)} %param.21) | copy-start | bytes 196612

commit v3 on v2

--- a/solution.py
+++ b/solution.py
@@ -75,17 +75,32 @@
     pltpu.sync_copy(packed, sent)
 
 
-def edges_out(u, v, t, first, last, low, high):
+def is_even(axis):
+    return lax.rem(lax.axis_index(axis), 2) == 0
+
+
+def edges_out(u, v, t, col_a, col_b, row_a, row_b):
+    even_x, even_y = is_even("px"), is_even("py")
     for f, field in enumerate((u, v, t)):
         for i in range(2):
             at = (i * FIELDS + f) * LEV
-            low[at : at + LEV, :] = field[pl.ds(i, LEV, stride=CX), :]
-            high[at : at + LEV, :] = field[pl.ds(CX - 2 + i, LEV, stride=CX), :]
+            low = field[pl.ds(i, LEV, stride=CX), :]
+            high = field[pl.ds(CX - 2 + i, LEV, stride=CX), :]
+            row_a[at : at + LEV, :] = jnp.where(even_x, high, low)
+            row_b[at : at + LEV, :] = jnp.where(even_x, low, high)
         for k in range(FLAT // 128):
             turned = field[k * 128 : (k + 1) * 128, :].T
+            first, last = turned[0:2, :], turned[CY - 2 :, :]
             at = 2 * (f * FLAT // 128 + k)
-            first[at : at + 2, :] = turned[0:2, :]
-            last[at : at + 2, :] = turned[CY - 2 :, :]
+            col_a[at : at + 2, :] = jnp.where(even_y, last, first)
+            col_b[at : at + 2, :] = jnp.where(even_y, first, last)
+
+
+def selector(pick):
+    k = lax.broadcasted_iota(jnp.int32, pick.shape, 0)
+    n = lax.broadcasted_iota(jnp.int32, pick.shape, 1)
+    want = ((n >> 5) & 3) * CY + (n & 31) * 4 + (n >> 7)
+    pick[...] = jnp.where(k == want, 1.0, 0.0).astype(BF16)
 
 
 def shifted(lane, field, border, b):
@@ -100,12 +115,49 @@
     return turn[...].T
 
 
-def inner(u, v, t, east, west, hyper, damp, u_out, v_out, t_out, pick, side, turn):
+def per_level(coef, quarter, hyper, damp):
+    for lev in range(LEV):
+        coef[lev : lev + 1, :] = jnp.full((1, CY), hyper[lev], F32)
+        quarter[lev : lev + 1, :] = jnp.full((1, CY), damp[lev] * 0.25, F32)
+
+
+def one(line, sign):
+    c, e1, e2, w1, w2 = line
+    if sign > 0:
+        return 2.0 * (e1 + w2) - 10.0 * (c + w1)
+    return 2.0 * (w1 + e2) - 10.0 * (c + e1)
+
+
+def two(line, sign):
+    c, e1, e2, w1, w2 = line
+    return c + w2 + 2.0 * w1 if sign > 0 else c + e2 + 2.0 * e1
+
+
+def add(out, r, value):
+    out[pl.ds(r, LEV, stride=CX), :] += value
+
+
+def add_rows(u_out, v_out, t_out, near, far, sign, k4, k2, wind):
+    edge, following = (CX - 1, CX - 2) if sign > 0 else (0, 1)
+    cross = [line[1] - line[3] for line in near]
+    fourth = [one(near[f], sign) + two(far[f], sign) for f in range(FIELDS)]
+    add(u_out, edge, k2 * (far[0][0] + sign * cross[1]) - k4 * fourth[0])
+    add(u_out, following, k2 * near[0][0] - k4 * two(near[0], sign))
+    add(v_out, edge, k2 * (sign * cross[0]) - k4 * fourth[1])
+    add(v_out, following, -k4 * two(near[1], sign))
+    add(t_out, edge, -k4 * fourth[2] - (0.25 * sign) * wind * near[2][0])
+    add(t_out, following, -k4 * two(near[2], sign))
+
+
+def step(u, v, t, col_a, col_b, row_a, row_b, hyper, damp, pick, u_out, v_out, t_out, table, side, turn, coef, quarter):
+    even_x, even_y = is_even("px"), is_even("py")
     turn[...] = jnp.zeros_like(turn)
     for k in range(BLOCKS):
+        a, b = col_a[2 * k : 2 * k + 2, :], col_b[2 * k : 2 * k + 2, :]
         side[k * 128 : (k + 1) * 128, :] = spread(
-            turn, east[2 * k : 2 * k + 2, :], west[2 * k : 2 * k + 2, :]
-        )
+            turn, jnp.where(even_y, a, b), jnp.where(even_y, b, a)
+        )
+    per_level(coef, quarter, hyper, damp)
     lane = lax.broadcasted_iota(jnp.int32, (CX, CY), 1)
     none = jnp.zeros((8, CY), F32)
 
@@ -141,65 +193,29 @@
         return carry
 
     lax.fori_loop(0, LEV, level, 0, unroll=4)
-    k = lax.broadcasted_iota(jnp.int32, pick.shape, 0)
-    n = lax.broadcasted_iota(jnp.int32, pick.shape, 1)
-    want = ((n >> 5) & 3) * CY + (n & 31) * 4 + (n >> 7)
-    pick[...] = jnp.where(k == want, 1.0, 0.0).astype(BF16)
-
-
-def per_level(coef, quarter, hyper, damp):
-    for lev in range(LEV):
-        coef[lev : lev + 1, :] = jnp.full((1, CY), hyper[lev], F32)
-        quarter[lev : lev + 1, :] = jnp.full((1, CY), damp[lev] * 0.25, F32)
-
-
-def one(line, sign):
-    c, e1, e2, w1, w2 = line
-    if sign > 0:
-        return 2.0 * (e1 + w2) - 10.0 * (c + w1)
-    return 2.0 * (w1 + e2) - 10.0 * (c + e1)
-
-
-def two(line, sign):
-    c, e1, e2, w1, w2 = line
-    return c + w2 + 2.0 * w1 if sign > 0 else c + e2 + 2.0 * e1
-
-
-def add(out, r, value):
-    out[pl.ds(r, LEV, stride=CX), :] += value
-
-
-def add_rows(u_out, v_out, t_out, near, far, sign, k4, k2, wind):
-    edge, following = (CX - 1, CX - 2) if sign > 0 else (0, 1)
-    cross = [line[1] - line[3] for line in near]
-    fourth = [one(near[f], sign) + two(far[f], sign) for f in range(FIELDS)]
-    add(u_out, edge, k2 * (far[0][0] + sign * cross[1]) - k4 * fourth[0])
-    add(u_out, following, k2 * near[0][0] - k4 * two(near[0], sign))
-    add(v_out, edge, k2 * (sign * cross[0]) - k4 * fourth[1])
-    add(v_out, following, -k4 * two(near[1], sign))
-    add(t_out, edge, -k4 * fourth[2] - (0.25 * sign) * wind * near[2][0])
-    add(t_out, following, -k4 * two(near[2], sign))
-
-
-def finish(u, u_in, v_in, t_in, above, below, hyper, damp, pick, u_out, v_out, t_out, table, coef, quarter):
-    per_level(coef, quarter, hyper, damp)
-    u_out[...] = u_in[...]
-    v_out[...] = v_in[...]
-    t_out[...] = t_in[...]
     lane = lax.broadcasted_iota(jnp.int32, (LEV, CY), 1)
     none = jnp.zeros((LEV, CY), F32)
 
-    def outside(rows, i):
+    def outside(this, other, keep, i):
         line = []
         for f in range(FIELDS):
-            c = rows[(i * FIELDS + f) * LEV : (i * FIELDS + f + 1) * LEV, :]
+            at = (i * FIELDS + f) * LEV
+            c = jnp.where(keep, this[at : at + LEV, :], other[at : at + LEV, :])
             line.append((c,) + tuple(shifted(lane, c, none, b) for b in (1, 2, -1, -2)))
         return line
 
-    for sign, rows, near, far in ((-1, above, 1, 0), (1, below, 0, 1)):
+    for sign, this, other, near, far in ((-1, row_b, row_a, 1, 0), (1, row_a, row_b, 0, 1)):
         wind = u[pl.ds(0 if sign < 0 else CX - 1, LEV, stride=CX), :]
         add_rows(
-            u_out, v_out, t_out, outside(rows, near), outside(rows, far), sign, coef[...], quarter[...], wind
+            u_out,
+            v_out,
+            t_out,
+            outside(this, other, even_x, near),
+            outside(this, other, even_x, far),
+            sign,
+            coef[...],
+            quarter[...],
+            wind,
         )
     for rl in range(4):
         parts = [t_out[pl.ds(4 * rh + rl, LEV, stride=CX), :] for rh in range(4)]
@@ -334,9 +350,10 @@
     lax.fori_loop(0, owners // 2, pair, 0, unroll=UNROLL)
 
 
-def neighbour(axis, move):
+def swap(axis, first):
     count = lax.axis_size(axis)
-    return [(i, (i + move) % count) for i in range(count)]
+    pairs = [((i + first) % count, (i + first + 1) % count) for i in range(0, count, 2)]
+    return pairs + [(b, a) for a, b in pairs]
 
 
 def on_device(theta, wind_u, wind_v, hyper, damp, cells, levels, bary, vfrac, values, mask):
@@ -363,36 +380,34 @@
     got = lax.all_to_all(sent, BOTH, split_axis=0, concat_axis=0, tiled=True)
     columns = shape((2 * BLOCKS, CY), F32)
     edge = shape((EDGE, CY), F32)
-    first, last, low, high = pl.pallas_call(
+    col_a, col_b, row_a, row_b = pl.pallas_call(
         edges_out,
         out_shape=(columns, columns, edge, edge),
         in_specs=[VMEM] * 3,
         compiler_params=PARAMS,
         cost_estimate=cost(100000, 1000000),
     )(u, v, t)
-    west = lax.ppermute(last, "py", neighbour("py", 1))
-    east = lax.ppermute(first, "py", neighbour("py", -1))
-    above = lax.ppermute(high, "px", neighbour("px", 1))
-    below = lax.ppermute(low, "px", neighbour("px", -1))
+    col_b = lax.ppermute(col_b, "py", swap("py", 1))
+    col_a = lax.ppermute(col_a, "py", swap("py", 0))
+    row_b = lax.ppermute(row_b, "px", swap("px", 1))
+    row_a = lax.ppermute(row_a, "px", swap("px", 0))
+    pick = pl.pallas_call(
+        selector,
+        out_shape=shape((4 * CY, 4 * CY), BF16),
+        compiler_params=PARAMS,
+        cost_estimate=cost(1000000, 500000),
+    )()
     patch = shape((FLAT, CY), F32)
     turn = pltpu.VMEM((CY, CY), F32)
     each = pltpu.VMEM((LEV, CY), F32)
-    u_part, v_part, t_part, pick = pl.pallas_call(
-        inner,
-        out_shape=(patch, patch, patch, shape((4 * CY, 4 * CY), BF16)),
-        in_specs=[VMEM] * 5 + [SMEM] * 2,
-        scratch_shapes=[pltpu.VMEM((FIELDS * FLAT, CY), F32), turn],
+    u_most, v_most, t_most, table = pl.pallas_call(
+        step,
+        out_shape=(patch, patch, patch, shape((24 * LEV, 2 * CY), BF16)),
+        in_specs=[VMEM] * 7 + [SMEM] * 2 + [VMEM],
+        scratch_shapes=[pltpu.VMEM((FIELDS * FLAT, CY), F32), turn, each, each],
         compiler_params=PARAMS,
         cost_estimate=cost(8000000, 3000000),
-    )(u, v, t, east, west, hyper, damp)
-    u_most, v_most, t_most, table = pl.pallas_call(
-        finish,
-        out_shape=(patch, patch, patch, shape((24 * LEV, 2 * CY), BF16)),
-        in_specs=[VMEM] * 6 + [SMEM] * 2 + [VMEM],
-        scratch_shapes=[each, each],
-        compiler_params=PARAMS,
-        cost_estimate=cost(4000000, 3000000),
-    )(u, u_part, v_part, t_part, above, below, hyper, damp, pick)
+    )(u, v, t, col_a, col_b, row_a, row_b, hyper, damp, pick)
     model = pl.pallas_call(
         interpolate,
         out_shape=shape((owners, slots), F32),

time: 59.3 us -> 57.1 us (0.963)
  waiting for transfers between devices: 14.2 us -> 10.4 us
  starting transfers between devices: 24.9 us -> 26.9 us
    ppermute x4, waiting for transfers between devices: 6.19 us -> 1.73 us  [the longest x1 1.72 us: on_device(): col_b = lax.ppermute(col_b, 'py', swap('py', 1))]
    all_to_all x1, starting transfers between devices: 6.35 us -> 7.62 us  [on_device(): back = lax.all_to_all(model, BOTH, split_axis=0, concat_axis=0, tiled=True)]
    all_to_all x1, waiting for transfers between devices: 0.01 us -> 0.88 us  [on_device(): got = lax.all_to_all(sent, BOTH, split_axis=0, concat_axis=0, tiled=True)]
    ppermute x4, starting transfers between devices: 7.03 us -> 7.75 us  [the longest x1 4.7 us: on_device(): col_b = lax.ppermute(col_b, 'py', swap('py', 1))]
where the time goes in v3:
time: 57.1 us; the launch traced here: 56.8 us
  starting transfers between devices  26.9 us (47%)
  Pallas kernels  18.1 us (32%)
  waiting for transfers between devices  10.4 us (18%)
  between operations  0.76 us (1%)
  other arithmetic  0.64 us (1%)
    all_to_all x1, starting transfers between devices, on_device(): got = lax.all_to_all(sent, BOTH, split_axis=0, concat_axis=0, tiled=True)  11.5 us
    pallas_call x1, Pallas kernels, on_device(): pl.pallas_call(interpolate, out_shape=shape((owners, slots), F32), in_spe...  10.2 us
    all_to_all x1, waiting for transfers between devices, on_device(): back = lax.all_to_all(model, BOTH, split_axis=0, concat_axis=0, tiled=True)  7.84 us
    all_to_all x1, starting transfers between devices, on_device(): back = lax.all_to_all(model, BOTH, split_axis=0, concat_axis=0, tiled=True)  7.62 us
    ppermute x1, starting transfers between devices, on_device(): col_b = lax.ppermute(col_b, 'py', swap('py', 1))  4.7 us
    pallas_call x1, Pallas kernels, on_device(): pl.pallas_call(step, out_shape=(patch, patch, patch, shape((24 * LEV, 2 *...  3.4 us
    pallas_call x1, Pallas kernels, on_device(): pl.pallas_call(messages_out, out_shape=shape((owners, SENT, slots), F32),...  2.3 us
    pallas_call x1, Pallas kernels, on_device(): pl.pallas_call(corners, out_shape=(patch, patch, patch), in_specs=[VMEM]...  1.84 us
  transfers between devices with their start and end apart: 6, of which 3 were waited for; matrix products, arithmetic and copies ran while one was open for 0% of the time, Pallas kernels for 10%

profile of v3, /device:TPU:1, one launch (start us, length us, event | category | flops | bytes accessed | tf_op | source)
XLA Modules:
  0.0 56.8 jit_solution(11402067683789665948)
XLA Ops:
  0.6 2.3 %shard_map.138 = f32[128,8,128]{2,1,0:T(8,128)} custom-call(f32[512,128]{1,0:T(8,128)} %bitcast.20, f32[512,128]{1,0:T(8,128)} %bitcast.23, f32[512,128]{1,0:T(8,128)} %bitcast.26, s32[128,128]{1,0:T(8,128)} %bitcast.31, s32[128,128]{1,0:T(8,128)} %bitcast.32, f32[3,128,128]{2,1,0:T(8,128)} %bitcast.30, f32[128,128]{1,0:T(8,128)} %bitcast.33), custom_call_target="tpu_custom_call" | custom-call | flops 100000 | bytes 3000000 | tf_op jit(solution)/shard_map/pallas_call | solution.py:363
  2.9 0.0 copy-start
  3.0 0.0 copy-start.1
  3.0 0.0 copy-start.2
  3.0 11.5 %all-to-all-start = ((f32[128,8,128]{2,1,0:T(8,128)}), f32[128,8,128]{2,1,0:T(8,128)S(1)}, u32[]{:S(2)}, u32[]{:S(2)}) async-start(f32[128,8,128]{2,1,0:T(8,128)} %shard_map.138), calls=%async_computation | async-start | bytes 1048576 | tf_op jit(solution)/shard_map/all_to_all | solution.py:380
  14.5 0.0 copy-done
  14.5 0.0 copy-done.1
  14.5 0.0 copy-done.2
  14.5 0.3 shard_map.139
  14.8 1.1 %collective-permute-start.2 = (f32[192,128]{1,0:T(8,128)S(1)}, f32[192,128]{1,0:T(8,128)S(1)}, u32[]{:S(2)}, u32[]{:S(2)}) collective-permute-start(f32[192,128]{1,0:T(8,128)S(1)} %get-tuple-element.17), channel_id=1, source_target_pairs={{0,16},{32,48},{64,80},{96,112},{16,0},{48,32},{80,64},{112,96},{1... | collective-permute-start | bytes 294920 | tf_op jit(solution)/shard_map/ppermute | solution.py:393
  15.9 0.7 %collective-permute-start.3 = (f32[192,128]{1,0:T(8,128)S(1)}, f32[192,128]{1,0:T(8,128)S(1)}, u32[]{:S(2)}, u32[]{:S(2)}) collective-permute-start(f32[192,128]{1,0:T(8,128)S(1)} %get-tuple-element.18), channel_id=1, source_target_pairs={{16,32},{48,64},{80,96},{112,0},{32,16},{64,48},{96,80},{0,112},{1... | collective-permute-start | bytes 294920 | tf_op jit(solution)/shard_map/ppermute | solution.py:392
  16.7 1.2 %collective-permute-start = (f32[24,128]{1,0:T(8,128)S(1)}, f32[24,128]{1,0:T(8,128)S(1)}, u32[]{:S(2)}, u32[]{:S(2)}) collective-permute-start(f32[24,128]{1,0:T(8,128)S(1)} %get-tuple-element.15), channel_id=1, source_target_pairs={{0,1},{2,3},{4,5},{6,7},{8,9},{10,11},{12,13},{14,15},{1,0},{3,2},... | collective-permute-start | bytes 36872 | tf_op jit(solution)/shard_map/ppermute | solution.py:391
  17.8 0.0 copy-start.3
  17.8 0.0 copy-start.4
  17.8 4.7 %collective-permute-start.1 = (f32[24,128]{1,0:T(8,128)S(1)}, f32[24,128]{1,0:T(8,128)S(1)}, u32[]{:S(2)}, u32[]{:S(2)}) collective-permute-start(f32[24,128]{1,0:T(8,128)S(1)} %get-tuple-element.16), channel_id=1, source_target_pairs={{1,2},{3,4},{5,6},{7,8},{9,10},{11,12},{13,14},{15,0},{2,1},{4,3},... | collective-permute-start | bytes 36872 | tf_op jit(solution)/shard_map/ppermute | solution.py:390
  22.5 0.1 shard_map.140.pick
  22.7 0.0 collective-permute-done.col_a
  22.7 1.7 %collective-permute-done.1.col_b = f32[24,128]{1,0:T(8,128)S(1)} collective-permute-done((f32[24,128]{1,0:T(8,128)S(1)}, f32[24,128]{1,0:T(8,128)S(1)}, u32[]{:S(2)}, u32[]{:S(2)}) %collective-permute-start.1) | collective-permute-done | bytes 12320 | tf_op jit(solution)/shard_map/ppermute | solution.py:390
  24.4 0.0 collective-permute-done.2.row_a
  24.4 0.0 collective-permute-done.3.row_b
  24.4 0.0 copy-done.3
  24.4 0.0 copy-done.4
  24.4 3.4 %shard_map.141 = (f32[512,128]{1,0:T(8,128)S(1)}, f32[512,128]{1,0:T(8,128)S(1)}, f32[512,128]{1,0:T(8,128)S(1)}, bf16[768,256]{1,0:T(8,128)(2,1)S(1)}) custom-call(f32[512,128]{1,0:T(8,128)S(1)} %bitcast.22, f32[512,128]{1,0:T(8,128)S(1)} %bitcast.25, f32[512,128]{1,0:T(8,128)S(1)} %bitcast.28, f32[24,128]{1,0:T(8,128)S(1)} %collective-permute-done.col_a, ...), custom_call_target="tpu_custom_call" | custom-call | flops 8000000 | bytes 3000000 | tf_op jit(solution)/shard_map/pallas_call | solution.py:403
  27.8 0.9 %all-to-all-done.obs = f32[128,8,128]{2,1,0:T(8,128)S(1)} async-done(((f32[128,8,128]{2,1,0:T(8,128)}), f32[128,8,128]{2,1,0:T(8,128)S(1)}, u32[]{:S(2)}, u32[]{:S(2)}) %all-to-all-start) | async-done | bytes 524320 | tf_op jit(solution)/shard_map/all_to_all | solution.py:380
  28.7 10.2 %shard_map.143 = f32[128,128]{1,0:T(8,128)} custom-call(bf16[768,256]{1,0:T(8,128)(2,1)S(1)} %get-tuple-element.25.start, f32[128,8,128]{2,1,0:T(8,128)S(1)} %all-to-all-done.obs, f32[512,128]{1,0:T(8,128)S(1)} %get-tuple-element.21.t_in.t, f32[32]{0:T(128)S(1)} %copy-done.3), custom_call_target="tpu_custom_call" | custom-call | flops 6499999744 | bytes 1000000 | tf_op jit(solution)/shard_map/pallas_call | solution.py:411
  38.9 7.6 %all-to-all-start.1 = ((f32[128,1,128]{2,1,0:T(1,128)}), f32[128,1,128]{2,1,0:T(1,128)S(1)}, u32[]{:S(2)}, u32[]{:S(2)}) async-start(f32[128,1,128]{2,1,0:T(1,128)} %bitcast.12), calls=%async_computation.1 | async-start | bytes 131072 | tf_op jit(solution)/shard_map/all_to_all | solution.py:429
  46.5 0.0 copy-start.5
  46.5 0.0 copy-start.6
  46.5 1.8 %shard_map.142 = (f32[512,128]{1,0:T(8,128)}, f32[512,128]{1,0:T(8,128)}, f32[512,128]{1,0:T(8,128)}) custom-call(f32[128,8,128]{2,1,0:T(8,128)S(1)} %all-to-all-done.obs, f32[512,128]{1,0:T(8,128)S(1)} %get-tuple-element.19.u_in, f32[512,128]{1,0:T(8,128)S(1)} %get-tuple-element.20.v_in, f32[512,128]{1,0:T(8,128)S(1)} %get-tuple-element.21.t_in.t, ...), custom_call_target="tpu_custom_call" | custom-call | flops 4000000 | bytes 3000000 | tf_op jit(solution)/shard_map/pallas_call | solution.py:421
  48.3 7.8 %all-to-all-done.1 = f32[128,1,128]{2,1,0:T(1,128)S(1)} async-done(((f32[128,1,128]{2,1,0:T(1,128)}), f32[128,1,128]{2,1,0:T(1,128)S(1)}, u32[]{:S(2)}, u32[]{:S(2)}) %all-to-all-start.1) | async-done | bytes 65568 | tf_op jit(solution)/shard_map/all_to_all | solution.py:429
  56.2 0.0 copy-done.5
  56.2 0.0 copy-done.6
  56.2 0.6 %fusion = f32[1,128,128]{2,1,0:T(8,128)} fusion(f32[1,128,128]{2,1,0:T(8,128)S(1)} %copy-done.5, s32[1,128,128]{2,1,0:T(8,128)S(1)} %copy-done.6, f32[1,128,128]{2,1,0:T(8,128)S(1)} %bitcast.29), kind=kLoop, calls=%fused_computation.1 | loop fusion | flops 49152 | bytes 262144 | tf_op jit(solution)/shard_map/mul | solution.py:430
Async XLA Ops:
  2.9 11.5 %copy-start = (f32[32,16,128]{2,1,0:T(8,128)S(1)}, f32[32,16,128]{2,1,0:T(8,128)}, u32[]{:S(2)}) copy-start(f32[32,16,128]{2,1,0:T(8,128)} %param.12) | copy-start | bytes 786436
  3.0 11.5 %copy-start.1 = (f32[32,16,128]{2,1,0:T(8,128)S(1)}, f32[32,16,128]{2,1,0:T(8,128)}, u32[]{:S(2)}) copy-start(f32[32,16,128]{2,1,0:T(8,128)} %param.13) | copy-start | bytes 786436
  3.0 11.5 %copy-start.2 = (f32[32,16,128]{2,1,0:T(8,128)S(1)}, f32[32,16,128]{2,1,0:T(8,128)}, u32[]{:S(2)}) copy-start(f32[32,16,128]{2,1,0:T(8,128)} %param.11) | copy-start | bytes 786436
  3.0 25.7 %all-to-all-start = ((f32[128,8,128]{2,1,0:T(8,128)}), f32[128,8,128]{2,1,0:T(8,128)S(1)}, u32[]{:S(2)}, u32[]{:S(2)}) async-start(f32[128,8,128]{2,1,0:T(8,128)} %shard_map.138), calls=%async_computation | async-start | bytes 1048576 | tf_op jit(solution)/shard_map/all_to_all | solution.py:380
  14.8 9.6 %collective-permute-start.2 = (f32[192,128]{1,0:T(8,128)S(1)}, f32[192,128]{1,0:T(8,128)S(1)}, u32[]{:S(2)}, u32[]{:S(2)}) collective-permute-start(f32[192,128]{1,0:T(8,128)S(1)} %get-tuple-element.17), channel_id=1, source_target_pairs={{0,16},{32,48},{64,80},{96,112},{16,0},{48,32},{80,64},{112,96},{1... | collective-permute-start | bytes 294920 | tf_op jit(solution)/shard_map/ppermute | solution.py:393
  15.9 8.5 %collective-permute-start.3 = (f32[192,128]{1,0:T(8,128)S(1)}, f32[192,128]{1,0:T(8,128)S(1)}, u32[]{:S(2)}, u32[]{:S(2)}) collective-permute-start(f32[192,128]{1,0:T(8,128)S(1)} %get-tuple-element.18), channel_id=1, source_target_pairs={{16,32},{48,64},{80,96},{112,0},{32,16},{64,48},{96,80},{0,112},{1... | collective-permute-start | bytes 294920 | tf_op jit(solution)/shard_map/ppermute | solution.py:392
  16.7 6.0 %collective-permute-start = (f32[24,128]{1,0:T(8,128)S(1)}, f32[24,128]{1,0:T(8,128)S(1)}, u32[]{:S(2)}, u32[]{:S(2)}) collective-permute-start(f32[24,128]{1,0:T(8,128)S(1)} %get-tuple-element.15), channel_id=1, source_target_pairs={{0,1},{2,3},{4,5},{6,7},{8,9},{10,11},{12,13},{14,15},{1,0},{3,2},... | collective-permute-start | bytes 36872 | tf_op jit(solution)/shard_map/ppermute | solution.py:391
  17.8 6.6 %copy-start.3 = (f32[32]{0:T(128)S(1)}, f32[32]{0:T(128)}, u32[]{:S(2)}) copy-start(f32[32]{0:T(128)} %hyper.5) | copy-start | bytes 388
  17.8 6.6 %copy-start.4 = (f32[32]{0:T(128)S(1)}, f32[32]{0:T(128)}, u32[]{:S(2)}) copy-start(f32[32]{0:T(128)} %damp.3) | copy-start | bytes 388
  17.8 6.5 %collective-permute-start.1 = (f32[24,128]{1,0:T(8,128)S(1)}, f32[24,128]{1,0:T(8,128)S(1)}, u32[]{:S(2)}, u32[]{:S(2)}) collective-permute-start(f32[24,128]{1,0:T(8,128)S(1)} %get-tuple-element.16), channel_id=1, source_target_pairs={{1,2},{3,4},{5,6},{7,8},{9,10},{11,12},{13,14},{15,0},{2,1},{4,3},... | collective-permute-start | bytes 36872 | tf_op jit(solution)/shard_map/ppermute | solution.py:390
  38.9 17.3 %all-to-all-start.1 = ((f32[128,1,128]{2,1,0:T(1,128)}), f32[128,1,128]{2,1,0:T(1,128)S(1)}, u32[]{:S(2)}, u32[]{:S(2)}) async-start(f32[128,1,128]{2,1,0:T(1,128)} %bitcast.12), calls=%async_computation.1 | async-start | bytes 131072 | tf_op jit(solution)/shard_map/all_to_all | solution.py:429
  46.5 9.7 %copy-start.5 = (f32[1,128,128]{2,1,0:T(8,128)S(1)}, f32[1,128,128]{2,1,0:T(8,128)}, u32[]{:S(2)}) copy-start(f32[1,128,128]{2,1,0:T(8,128)} %param.20) | copy-start | bytes 196612
  46.5 9.7 %copy-start.6 = (s32[1,128,128]{2,1,0:T(8,128)S(1)}, s32[1,128,128]{2,1,0:T(8,128)}, u32[]{:S(2)}) copy-start(s32[1,128,128]{2,1,0:T(8,128)} %param.21) | copy-start | bytes 196612

commit v4 on v3

--- a/solution.py
+++ b/solution.py
@@ -15,7 +15,7 @@
 ROWS = (0, 1, CX - 2, CX - 1)
 BLOCKS = FIELDS * FLAT // 128
 EDGE = 2 * FIELDS * LEV
-UNROLL = 16
+UNROLL = 32
 BOTH = ("px", "py")
 F32 = jnp.float32
 BF16 = jnp.bfloat16
@@ -96,23 +96,10 @@
             col_b[at : at + 2, :] = jnp.where(even_y, first, last)
 
 
-def selector(pick):
-    k = lax.broadcasted_iota(jnp.int32, pick.shape, 0)
-    n = lax.broadcasted_iota(jnp.int32, pick.shape, 1)
-    want = ((n >> 5) & 3) * CY + (n & 31) * 4 + (n >> 7)
-    pick[...] = jnp.where(k == want, 1.0, 0.0).astype(BF16)
-
-
 def shifted(lane, field, border, b):
     if b > 0:
         return pltpu.roll(jnp.where(lane < b, border, field), CY - b, 1)
     return pltpu.roll(jnp.where(lane >= CY + b, border, field), -b, 1)
-
-
-def spread(turn, ahead, behind):
-    turn[0:2, :] = ahead
-    turn[CY - 2 :, :] = behind
-    return turn[...].T
 
 
 def per_level(coef, quarter, hyper, damp):
@@ -149,15 +136,7 @@
     add(t_out, following, -k4 * two(near[2], sign))
 
 
-def step(u, v, t, col_a, col_b, row_a, row_b, hyper, damp, pick, u_out, v_out, t_out, table, side, turn, coef, quarter):
-    even_x, even_y = is_even("px"), is_even("py")
-    turn[...] = jnp.zeros_like(turn)
-    for k in range(BLOCKS):
-        a, b = col_a[2 * k : 2 * k + 2, :], col_b[2 * k : 2 * k + 2, :]
-        side[k * 128 : (k + 1) * 128, :] = spread(
-            turn, jnp.where(even_y, a, b), jnp.where(even_y, b, a)
-        )
-    per_level(coef, quarter, hyper, damp)
+def bulk(u, v, t, hyper, damp, u_out, v_out, t_out, pick):
     lane = lax.broadcasted_iota(jnp.int32, (CX, CY), 1)
     none = jnp.zeros((8, CY), F32)
 
@@ -170,10 +149,9 @@
         at = pl.multiple_of(lev * CX, 8)
         views = []
         fourth = []
-        for f, field in enumerate((u, v, t)):
+        for field in (u, v, t):
             c = field[pl.ds(at, CX), :]
-            h = side[pl.ds(f * FLAT + at, CX), :]
-            e1, e2, w1, w2 = (shifted(lane, c, h, b) for b in (1, 2, -1, -2))
+            e1, e2, w1, w2 = (shifted(lane, c, 0.0, b) for b in (1, 2, -1, -2))
             total = 42.0 * c - 10.0 * (e1 + w1) + (e2 + w2)
             total = total + rows(2.0 * (e1 + w2) - 10.0 * (c + w1), 1)
             total = total + rows(2.0 * (w1 + e2) - 10.0 * (c + e1), -1)
@@ -193,15 +171,87 @@
         return carry
 
     lax.fori_loop(0, LEV, level, 0, unroll=4)
+    k = lax.broadcasted_iota(jnp.int32, pick.shape, 0)
+    n = lax.broadcasted_iota(jnp.int32, pick.shape, 1)
+    want = ((n >> 5) & 3) * CY + (n & 31) * 4 + (n >> 7)
+    pick[...] = jnp.where(k == want, 1.0, 0.0).astype(BF16)
+
+
+def borders(
+    u, u_in, v_in, t_in, own_a, own_b, col_a, col_b, row_a, row_b, hyper, damp, pick,
+    u_out, v_out, t_out, table, coef, quarter, turn, across,
+):
+    even_x, even_y = is_even("px"), is_even("py")
+    per_level(coef, quarter, hyper, damp)
+    parts = FLAT // 128
+    spot = lax.broadcasted_iota(jnp.int32, (1, CY), 1) >> 4
+    for k in range(parts):
+        c, q = jnp.zeros((1, CY), F32), jnp.zeros((1, CY), F32)
+        for i in range(8):
+            c = jnp.where(spot == i, hyper[8 * k + i], c)
+            q = jnp.where(spot == i, damp[8 * k + i] * 0.25, q)
+        across[k : k + 1, :] = c
+        across[parts + k : parts + k + 1, :] = q
+    c4, q4 = across[0:parts, :], across[parts : 2 * parts, :]
+    place = lax.broadcasted_iota(jnp.int32, (parts, CY), 1) & (CX - 1)
+
+    def moved(x, a):
+        inside = place < CX - a if a > 0 else place >= -a
+        return jnp.where(inside, pltpu.roll(x, -a % CY, 1), 0.0)
+
+    def line(yes, no, f, col):
+        at = pl.ds(2 * parts * f + col, parts, stride=2)
+        return jnp.where(even_y, yes[at, :], no[at, :])
+
+    east = [[line(col_a, col_b, f, i) for i in range(2)] for f in range(FIELDS)]
+    west = [[line(col_b, col_a, f, i) for i in (1, 0)] for f in range(FIELDS)]
+    v_first, v_last = line(own_b, own_a, 1, 0), line(own_a, own_b, 1, 1)
+
+    def nearest(x, y, s):
+        total = 2.0 * moved(x, s) - 10.0 * (x + moved(x, -s)) + 2.0 * moved(x, -2 * s)
+        return total + next_one(y, s)
+
+    def next_one(x, s):
+        return x + 2.0 * moved(x, -s) + moved(x, -2 * s)
+
+    def slope(x):
+        return moved(x, 1) - moved(x, -1)
+
+    (ue, ve, te), (uw, vw, tw) = east, west
+    terms = (
+        (
+            -c4 * nearest(*uw, -1) - q4 * slope(vw[0]),
+            -c4 * next_one(uw[0], -1),
+            -c4 * next_one(ue[0], 1),
+            -c4 * nearest(*ue, 1) + q4 * slope(ve[0]),
+        ),
+        (
+            -c4 * nearest(*vw, -1) + q4 * (vw[1] - slope(uw[0])),
+            -c4 * next_one(vw[0], -1) + q4 * vw[0],
+            -c4 * next_one(ve[0], 1) + q4 * ve[0],
+            -c4 * nearest(*ve, 1) + q4 * (ve[1] + slope(ue[0])),
+        ),
+        (
+            -c4 * nearest(*tw, -1) + 0.25 * v_first * tw[0],
+            -c4 * next_one(tw[0], -1),
+            -c4 * next_one(te[0], 1),
+            -c4 * nearest(*te, 1) - 0.25 * v_last * te[0],
+        ),
+    )
+    turn[...] = jnp.zeros_like(turn)
+    for f, (start, out) in enumerate(((u_in, u_out), (v_in, v_out), (t_in, t_out))):
+        for k in range(parts):
+            for col, term in zip((0, 1, CY - 2, CY - 1), terms[f]):
+                turn[col : col + 1, :] = term[k : k + 1, :]
+            out[k * 128 : (k + 1) * 128, :] = start[k * 128 : (k + 1) * 128, :] + turn[...].T
     lane = lax.broadcasted_iota(jnp.int32, (LEV, CY), 1)
-    none = jnp.zeros((LEV, CY), F32)
 
     def outside(this, other, keep, i):
         line = []
         for f in range(FIELDS):
             at = (i * FIELDS + f) * LEV
             c = jnp.where(keep, this[at : at + LEV, :], other[at : at + LEV, :])
-            line.append((c,) + tuple(shifted(lane, c, none, b) for b in (1, 2, -1, -2)))
+            line.append((c,) + tuple(shifted(lane, c, 0.0, b) for b in (1, 2, -1, -2)))
         return line
 
     for sign, this, other, near, far in ((-1, row_b, row_a, 1, 0), (1, row_a, row_b, 0, 1)):
@@ -257,8 +307,7 @@
     return lines
 
 
-def corners(obs, u_in, v_in, t_in, hyper, damp, u_out, v_out, t_out, turn, coef, quarter):
-    per_level(coef, quarter, hyper, damp)
+def corners(obs, u_in, v_in, t_in, coef, quarter, u_out, v_out, t_out, turn):
     u_out[...] = u_in[...]
     v_out[...] = v_in[...]
     t_out[...] = t_in[...]
@@ -278,10 +327,7 @@
         )
 
 
-def interpolate(start, obs, t, hyper, model, table, block, row, col, lev, turn, coef):
-    table[...] = start[...]
-    for k in range(LEV):
-        coef[k : k + 1, :] = jnp.full((1, CY), hyper[k], F32)
+def interpolate(start, obs, t, coef, table, model, block, row, col, lev, turn):
     far_up, near_up, near_down, far_down = corner_lines(obs, turn, 2)
     terms = (
         one(near_up, -1) + two(far_up, -1),
@@ -298,7 +344,7 @@
             high = moved.astype(BF16).astype(F32)
             at = ((r & 3) * 5 + (c & 3)) * LEV
             for k, part in enumerate((high, moved - high)):
-                old = table[at : at + LEV, k * CY : (k + 1) * CY].astype(F32)
+                old = start[at : at + LEV, k * CY : (k + 1) * CY].astype(F32)
                 table[at : at + LEV, k * CY : (k + 1) * CY] = jnp.where(lane == to, part, old).astype(BF16)
     owners = model.shape[0]
     cell = obs[:, 0, :].astype(jnp.int32)
@@ -380,52 +426,53 @@
     got = lax.all_to_all(sent, BOTH, split_axis=0, concat_axis=0, tiled=True)
     columns = shape((2 * BLOCKS, CY), F32)
     edge = shape((EDGE, CY), F32)
-    col_a, col_b, row_a, row_b = pl.pallas_call(
+    own_a, own_b, row_a, row_b = pl.pallas_call(
         edges_out,
         out_shape=(columns, columns, edge, edge),
         in_specs=[VMEM] * 3,
         compiler_params=PARAMS,
         cost_estimate=cost(100000, 1000000),
     )(u, v, t)
-    col_b = lax.ppermute(col_b, "py", swap("py", 1))
-    col_a = lax.ppermute(col_a, "py", swap("py", 0))
+    col_b = lax.ppermute(own_b, "py", swap("py", 1))
+    col_a = lax.ppermute(own_a, "py", swap("py", 0))
     row_b = lax.ppermute(row_b, "px", swap("px", 1))
     row_a = lax.ppermute(row_a, "px", swap("px", 0))
-    pick = pl.pallas_call(
-        selector,
-        out_shape=shape((4 * CY, 4 * CY), BF16),
+    patch = shape((FLAT, CY), F32)
+    plane = shape((LEV, CY), F32)
+    grid = shape((24 * LEV, 2 * CY), BF16)
+    turn = pltpu.VMEM((CY, CY), F32)
+    u_part, v_part, t_part, pick = pl.pallas_call(
+        bulk,
+        out_shape=(patch, patch, patch, shape((4 * CY, 4 * CY), BF16)),
+        in_specs=[VMEM] * 3 + [SMEM] * 2,
         compiler_params=PARAMS,
-        cost_estimate=cost(1000000, 500000),
-    )()
-    patch = shape((FLAT, CY), F32)
-    turn = pltpu.VMEM((CY, CY), F32)
-    each = pltpu.VMEM((LEV, CY), F32)
-    u_most, v_most, t_most, table = pl.pallas_call(
-        step,
-        out_shape=(patch, patch, patch, shape((24 * LEV, 2 * CY), BF16)),
-        in_specs=[VMEM] * 7 + [SMEM] * 2 + [VMEM],
-        scratch_shapes=[pltpu.VMEM((FIELDS * FLAT, CY), F32), turn, each, each],
+        cost_estimate=cost(8000000, 10000000),
+    )(u, v, t, hyper, damp)
+    u_most, v_most, t_most, table, coef, quarter = pl.pallas_call(
+        borders,
+        out_shape=(patch, patch, patch, grid, plane, plane),
+        in_specs=[VMEM] * 10 + [SMEM] * 2 + [VMEM],
+        scratch_shapes=[turn, pltpu.VMEM((8, CY), F32)],
         compiler_params=PARAMS,
-        cost_estimate=cost(8000000, 3000000),
-    )(u, v, t, col_a, col_b, row_a, row_b, hyper, damp, pick)
-    model = pl.pallas_call(
+        cost_estimate=cost(4000000, 3000000),
+    )(u, u_part, v_part, t_part, own_a, own_b, col_a, col_b, row_a, row_b, hyper, damp, pick)
+    _, model = pl.pallas_call(
         interpolate,
-        out_shape=shape((owners, slots), F32),
-        in_specs=[VMEM] * 3 + [SMEM],
-        scratch_shapes=[pltpu.VMEM((24 * LEV, 2 * CY), BF16)]
-        + [pltpu.VMEM((owners, slots), jnp.int32)] * 4
-        + [turn, each],
+        out_shape=(grid, shape((owners, slots), F32)),
+        in_specs=[VMEM] * 4,
+        scratch_shapes=[pltpu.VMEM((owners, slots), jnp.int32)] * 4 + [turn],
+        input_output_aliases={0: 0},
         compiler_params=PARAMS,
         cost_estimate=cost(6500000000, 1000000),
-    )(table, got, t_most, hyper)
+    )(table, got, t_most, coef)
     u_next, v_next, t_next = pl.pallas_call(
         corners,
         out_shape=(patch, patch, patch),
-        in_specs=[VMEM] * 4 + [SMEM] * 2,
-        scratch_shapes=[turn, each, each],
+        in_specs=[VMEM] * 6,
+        scratch_shapes=[turn],
         compiler_params=PARAMS,
         cost_estimate=cost(4000000, 3000000),
-    )(got, u_most, v_most, t_most, hyper, damp)
+    )(got, u_most, v_most, t_most, coef, quarter)
     back = lax.all_to_all(model, BOTH, split_axis=0, concat_axis=0, tiled=True)
     departures = mask.astype(F32) * (values - back[None])
     whole = theta.shape

time: 57.1 us -> 54.1 us (0.947)
  starting transfers between devices: 26.9 us -> 24.9 us
  Pallas kernels: 18.1 us -> 17 us
    all_to_all x1, starting transfers between devices: 7.62 us -> 5.65 us  [on_device(): back = lax.all_to_all(model, BOTH, split_axis=0, concat_axis=0, tiled=True)]
    ppermute x2, waiting for transfers between devices: 1.72 us -> 0.01 us  [the longest x1 0.01 us: on_device(): col_a = lax.ppermute(own_a, 'py', swap('py', 0))]
    all_to_all x1, waiting for transfers between devices: 0.88 us -> 2.15 us  [on_device(): got = lax.all_to_all(sent, BOTH, split_axis=0, concat_axis=0, tiled=True)]
    pallas_call x3, Pallas kernels: 13.7 us -> 13.1 us  [the longest x1 9.15 us: on_device(): pl.pallas_call(interpolate, out_shape=(grid, shape((owners, slots), F32))...]
  transfers between devices with their start and end apart: 6 -> 6, of which waited for: 3 -> 2; matrix products, arithmetic and copies ran while one was open for 0% -> 0% of each run, Pallas kernels for 10% -> 10%
where the time goes in v4:
time: 54.1 us; the launch traced here: 53.9 us
  starting transfers between devices  24.9 us (46%)
  Pallas kernels  17 us (31%)
  waiting for transfers between devices  10.6 us (20%)
  between operations  0.77 us (1%)
  other arithmetic  0.64 us (1%)
    all_to_all x1, starting transfers between devices, on_device(): got = lax.all_to_all(sent, BOTH, split_axis=0, concat_axis=0, tiled=True)  11.5 us
    pallas_call x1, Pallas kernels, on_device(): pl.pallas_call(interpolate, out_shape=(grid, shape((owners, slots), F32))...  9.15 us
    all_to_all x1, waiting for transfers between devices, on_device(): back = lax.all_to_all(model, BOTH, split_axis=0, concat_axis=0, tiled=True)  8.39 us
    all_to_all x1, starting transfers between devices, on_device(): back = lax.all_to_all(model, BOTH, split_axis=0, concat_axis=0, tiled=True)  5.65 us
    ppermute x1, starting transfers between devices, on_device(): col_b = lax.ppermute(own_b, 'py', swap('py', 1))  4.7 us
    pallas_call x1, Pallas kernels, on_device(): pl.pallas_call(bulk, out_shape=(patch, patch, patch, shape((4 * CY, 4 * C...  2.48 us
    pallas_call x1, Pallas kernels, on_device(): pl.pallas_call(messages_out, out_shape=shape((owners, SENT, slots), F32),...  2.31 us
    all_to_all x1, waiting for transfers between devices, on_device(): got = lax.all_to_all(sent, BOTH, split_axis=0, concat_axis=0, tiled=True)  2.15 us
  transfers between devices with their start and end apart: 6, of which 2 were waited for; matrix products, arithmetic and copies ran while one was open for 0% of the time, Pallas kernels for 10%

profile of v4, /device:TPU:1, one launch (start us, length us, event | category | flops | bytes accessed | tf_op | source)
XLA Modules:
  0.0 53.9 jit_solution(14839963351650417745)
XLA Ops:
  0.6 2.3 %shard_map.138 = f32[128,8,128]{2,1,0:T(8,128)} custom-call(f32[512,128]{1,0:T(8,128)} %bitcast.20, f32[512,128]{1,0:T(8,128)} %bitcast.24, f32[512,128]{1,0:T(8,128)} %bitcast.27, s32[128,128]{1,0:T(8,128)} %bitcast.32, s32[128,128]{1,0:T(8,128)} %bitcast.33, f32[3,128,128]{2,1,0:T(8,128)} %bitcast.31, f32[128,128]{1,0:T(8,128)} %bitcast.34), custom_call_target="tpu_custom_call" | custom-call | flops 100000 | bytes 3000000 | tf_op jit(solution)/shard_map/pallas_call | solution.py:409
  3.0 0.0 copy-start
  3.0 0.0 copy-start.1
  3.0 0.0 copy-start.2
  3.0 11.5 %all-to-all-start = ((f32[128,8,128]{2,1,0:T(8,128)}), f32[128,8,128]{2,1,0:T(8,128)S(1)}, u32[]{:S(2)}, u32[]{:S(2)}) async-start(f32[128,8,128]{2,1,0:T(8,128)} %shard_map.138), calls=%async_computation | async-start | bytes 1048576 | tf_op jit(solution)/shard_map/all_to_all | solution.py:426
  14.5 0.0 copy-done
  14.5 0.0 copy-done.1
  14.5 0.0 copy-done.2
  14.5 0.3 shard_map.140
  14.8 1.1 %collective-permute-start.2 = (f32[192,128]{1,0:T(8,128)S(1)}, f32[192,128]{1,0:T(8,128)S(1)}, u32[]{:S(2)}, u32[]{:S(2)}) collective-permute-start(f32[192,128]{1,0:T(8,128)S(1)} %get-tuple-element.27), channel_id=1, source_target_pairs={{0,16},{32,48},{64,80},{96,112},{16,0},{48,32},{80,64},{112,96},{1... | collective-permute-start | bytes 294920 | tf_op jit(solution)/shard_map/ppermute | solution.py:439
  15.9 0.7 %collective-permute-start.3 = (f32[192,128]{1,0:T(8,128)S(1)}, f32[192,128]{1,0:T(8,128)S(1)}, u32[]{:S(2)}, u32[]{:S(2)}) collective-permute-start(f32[192,128]{1,0:T(8,128)S(1)} %get-tuple-element.28), channel_id=1, source_target_pairs={{16,32},{48,64},{80,96},{112,0},{32,16},{64,48},{96,80},{0,112},{1... | collective-permute-start | bytes 294920 | tf_op jit(solution)/shard_map/ppermute | solution.py:438
  16.7 0.0 copy-start.3
  16.7 0.0 copy-start.4
  16.7 1.2 %collective-permute-start = (f32[24,128]{1,0:T(8,128)S(1)}, f32[24,128]{1,0:T(8,128)S(1)}, u32[]{:S(2)}, u32[]{:S(2)}) collective-permute-start(f32[24,128]{1,0:T(8,128)S(1)} %get-tuple-element.25.own_a), channel_id=1, source_target_pairs={{0,1},{2,3},{4,5},{6,7},{8,9},{10,11},{12,13},{14,15},{1,0},{3,2},... | collective-permute-start | bytes 36872 | tf_op jit(solution)/shard_map/ppermute | solution.py:437
  17.9 4.7 %collective-permute-start.1 = (f32[24,128]{1,0:T(8,128)S(1)}, f32[24,128]{1,0:T(8,128)S(1)}, u32[]{:S(2)}, u32[]{:S(2)}) collective-permute-start(f32[24,128]{1,0:T(8,128)S(1)} %get-tuple-element.26.own_b), channel_id=1, source_target_pairs={{1,2},{3,4},{5,6},{7,8},{9,10},{11,12},{13,14},{15,0},{2,1},{4,3},... | collective-permute-start | bytes 36872 | tf_op jit(solution)/shard_map/ppermute | solution.py:436
  22.6 0.0 copy-done.3
  22.6 0.0 copy-done.4
  22.6 2.5 %shard_map.139 = (f32[512,128]{1,0:T(8,128)S(1)}, f32[512,128]{1,0:T(8,128)S(1)}, f32[512,128]{1,0:T(8,128)S(1)}, bf16[512,512]{1,0:T(8,128)(2,1)S(1)}) custom-call(f32[512,128]{1,0:T(8,128)S(1)} %bitcast.22, f32[512,128]{1,0:T(8,128)S(1)} %bitcast.26, f32[512,128]{1,0:T(8,128)S(1)} %bitcast.29, f32[32]{0:T(128)S(1)} %copy-done.3, f32[32]{0:T(128)S(1)} %copy-done.4), custom_call_target="tpu_custom_call" | custom-call | flops 8000000 | bytes 10000000 | tf_op jit(solution)/shard_map/pallas_call | solution.py:444
  25.1 0.0 collective-permute-done.col_a
  25.1 0.0 collective-permute-done.1.col_b
  25.1 0.0 collective-permute-done.2.row_a
  25.1 0.0 collective-permute-done.3.row_b
  25.1 1.5 %shard_map.141 = (f32[512,128]{1,0:T(8,128)S(1)}, f32[512,128]{1,0:T(8,128)S(1)}, f32[512,128]{1,0:T(8,128)S(1)}, bf16[768,256]{1,0:T(8,128)(2,1)S(1)}, f32[32,128]{1,0:T(8,128)S(1)}, /*index=5*/f32[32,128]{1,0:T(8,128)S(1)}) custom-call(f32[512,128]{1,0:T(8,128)S(1)} %bitcast.23, f32[512,128]{1,0:T(8,128)S(1)} %get-tuple-element.22.u_in, ...), custom_call_target="tpu_custom_call" | custom-call | flops 4000000 | bytes 3000000 | tf_op jit(solution)/shard_map/pallas_call | solution.py:451
  26.5 2.2 %all-to-all-done.obs = f32[128,8,128]{2,1,0:T(8,128)S(1)} async-done(((f32[128,8,128]{2,1,0:T(8,128)}), f32[128,8,128]{2,1,0:T(8,128)S(1)}, u32[]{:S(2)}, u32[]{:S(2)}) %all-to-all-start) | async-done | bytes 524320 | tf_op jit(solution)/shard_map/all_to_all | solution.py:426
  28.7 9.2 %shard_map.143 = (bf16[768,256]{1,0:T(8,128)(2,1)S(1)}, f32[128,128]{1,0:T(8,128)}) custom-call(bf16[768,256]{1,0:T(8,128)(2,1)S(1)} %get-tuple-element.38.start, f32[128,8,128]{2,1,0:T(8,128)S(1)} %all-to-all-done.obs, f32[512,128]{1,0:T(8,128)S(1)} %get-tuple-element.32.t_in.t, f32[32,128]{1,0:T(8,128)S(1)} %get-tuple-element.33.coef), custom_call_target="tpu_custom_call", output_to_operand_aliasing={{0}: (0, {})} | custom-call | flops 6499999744 | bytes 1000000 | tf_op jit(solution)/shard_map/pallas_call | solution.py:459
  37.9 5.7 %all-to-all-start.1 = ((f32[128,1,128]{2,1,0:T(1,128)}), f32[128,1,128]{2,1,0:T(1,128)S(1)}, u32[]{:S(2)}, u32[]{:S(2)}) async-start(f32[128,1,128]{2,1,0:T(1,128)} %bitcast.12), calls=%async_computation.1 | async-start | bytes 131072 | tf_op jit(solution)/shard_map/all_to_all | solution.py:476
  43.5 0.0 copy-start.5
  43.5 0.0 copy-start.6
  43.5 1.3 %shard_map.142 = (f32[512,128]{1,0:T(8,128)}, f32[512,128]{1,0:T(8,128)}, f32[512,128]{1,0:T(8,128)}) custom-call(f32[128,8,128]{2,1,0:T(8,128)S(1)} %all-to-all-done.obs, f32[512,128]{1,0:T(8,128)S(1)} %get-tuple-element.30.u_in, f32[512,128]{1,0:T(8,128)S(1)} %get-tuple-element.31.v_in, f32[512,128]{1,0:T(8,128)S(1)} %get-tuple-element.32.t_in.t, ...), custom_call_target="tpu_custom_call" | custom-call | flops 4000000 | bytes 3000000 | tf_op jit(solution)/shard_map/pallas_call | solution.py:468
  44.8 8.4 %all-to-all-done.1 = f32[128,1,128]{2,1,0:T(1,128)S(1)} async-done(((f32[128,1,128]{2,1,0:T(1,128)}), f32[128,1,128]{2,1,0:T(1,128)S(1)}, u32[]{:S(2)}, u32[]{:S(2)}) %all-to-all-start.1) | async-done | bytes 65568 | tf_op jit(solution)/shard_map/all_to_all | solution.py:476
  53.2 0.0 copy-done.5
  53.2 0.0 copy-done.6
  53.2 0.6 %fusion = f32[1,128,128]{2,1,0:T(8,128)} fusion(f32[1,128,128]{2,1,0:T(8,128)S(1)} %copy-done.5, s32[1,128,128]{2,1,0:T(8,128)S(1)} %copy-done.6, f32[1,128,128]{2,1,0:T(8,128)S(1)} %bitcast.30), kind=kLoop, calls=%fused_computation.1 | loop fusion | flops 49152 | bytes 262144 | tf_op jit(solution)/shard_map/mul | solution.py:477
Async XLA Ops:
  3.0 11.5 %copy-start = (f32[32,16,128]{2,1,0:T(8,128)S(1)}, f32[32,16,128]{2,1,0:T(8,128)}, u32[]{:S(2)}) copy-start(f32[32,16,128]{2,1,0:T(8,128)} %param.12) | copy-start | bytes 786436
  3.0 11.5 %copy-start.1 = (f32[32,16,128]{2,1,0:T(8,128)S(1)}, f32[32,16,128]{2,1,0:T(8,128)}, u32[]{:S(2)}) copy-start(f32[32,16,128]{2,1,0:T(8,128)} %param.13) | copy-start | bytes 786436
  3.0 11.5 %copy-start.2 = (f32[32,16,128]{2,1,0:T(8,128)S(1)}, f32[32,16,128]{2,1,0:T(8,128)}, u32[]{:S(2)}) copy-start(f32[32,16,128]{2,1,0:T(8,128)} %param.11) | copy-start | bytes 786436
  3.0 25.7 %all-to-all-start = ((f32[128,8,128]{2,1,0:T(8,128)}), f32[128,8,128]{2,1,0:T(8,128)S(1)}, u32[]{:S(2)}, u32[]{:S(2)}) async-start(f32[128,8,128]{2,1,0:T(8,128)} %shard_map.138), calls=%async_computation | async-start | bytes 1048576 | tf_op jit(solution)/shard_map/all_to_all | solution.py:426
  14.8 10.3 %collective-permute-start.2 = (f32[192,128]{1,0:T(8,128)S(1)}, f32[192,128]{1,0:T(8,128)S(1)}, u32[]{:S(2)}, u32[]{:S(2)}) collective-permute-start(f32[192,128]{1,0:T(8,128)S(1)} %get-tuple-element.27), channel_id=1, source_target_pairs={{0,16},{32,48},{64,80},{96,112},{16,0},{48,32},{80,64},{112,96},{1... | collective-permute-start | bytes 294920 | tf_op jit(solution)/shard_map/ppermute | solution.py:439
  15.9 9.1 %collective-permute-start.3 = (f32[192,128]{1,0:T(8,128)S(1)}, f32[192,128]{1,0:T(8,128)S(1)}, u32[]{:S(2)}, u32[]{:S(2)}) collective-permute-start(f32[192,128]{1,0:T(8,128)S(1)} %get-tuple-element.28), channel_id=1, source_target_pairs={{16,32},{48,64},{80,96},{112,0},{32,16},{64,48},{96,80},{0,112},{1... | collective-permute-start | bytes 294920 | tf_op jit(solution)/shard_map/ppermute | solution.py:438
  16.7 5.9 %copy-start.3 = (f32[32]{0:T(128)S(1)}, f32[32]{0:T(128)}, u32[]{:S(2)}) copy-start(f32[32]{0:T(128)} %hyper.3) | copy-start | bytes 388
  16.7 5.9 %copy-start.4 = (f32[32]{0:T(128)S(1)}, f32[32]{0:T(128)}, u32[]{:S(2)}) copy-start(f32[32]{0:T(128)} %damp.3) | copy-start | bytes 388
  16.7 8.4 %collective-permute-start = (f32[24,128]{1,0:T(8,128)S(1)}, f32[24,128]{1,0:T(8,128)S(1)}, u32[]{:S(2)}, u32[]{:S(2)}) collective-permute-start(f32[24,128]{1,0:T(8,128)S(1)} %get-tuple-element.25.own_a), channel_id=1, source_target_pairs={{0,1},{2,3},{4,5},{6,7},{8,9},{10,11},{12,13},{14,15},{1,0},{3,2},... | collective-permute-start | bytes 36872 | tf_op jit(solution)/shard_map/ppermute | solution.py:437
  17.9 7.2 %collective-permute-start.1 = (f32[24,128]{1,0:T(8,128)S(1)}, f32[24,128]{1,0:T(8,128)S(1)}, u32[]{:S(2)}, u32[]{:S(2)}) collective-permute-start(f32[24,128]{1,0:T(8,128)S(1)} %get-tuple-element.26.own_b), channel_id=1, source_target_pairs={{1,2},{3,4},{5,6},{7,8},{9,10},{11,12},{13,14},{15,0},{2,1},{4,3},... | collective-permute-start | bytes 36872 | tf_op jit(solution)/shard_map/ppermute | solution.py:436
  37.9 15.4 %all-to-all-start.1 = ((f32[128,1,128]{2,1,0:T(1,128)}), f32[128,1,128]{2,1,0:T(1,128)S(1)}, u32[]{:S(2)}, u32[]{:S(2)}) async-start(f32[128,1,128]{2,1,0:T(1,128)} %bitcast.12), calls=%async_computation.1 | async-start | bytes 131072 | tf_op jit(solution)/shard_map/all_to_all | solution.py:476
  43.5 9.7 %copy-start.5 = (f32[1,128,128]{2,1,0:T(8,128)S(1)}, f32[1,128,128]{2,1,0:T(8,128)}, u32[]{:S(2)}) copy-start(f32[1,128,128]{2,1,0:T(8,128)} %param.20) | copy-start | bytes 196612
  43.5 9.7 %copy-start.6 = (s32[1,128,128]{2,1,0:T(8,128)S(1)}, s32[1,128,128]{2,1,0:T(8,128)}, u32[]{:S(2)}) copy-start(s32[1,128,128]{2,1,0:T(8,128)} %param.21) | copy-start | bytes 196612

commit v5 on v4

--- a/solution.py
+++ b/solution.py
@@ -124,16 +124,23 @@
     out[pl.ds(r, LEV, stride=CX), :] += value
 
 
-def add_rows(u_out, v_out, t_out, near, far, sign, k4, k2, wind):
-    edge, following = (CX - 1, CX - 2) if sign > 0 else (0, 1)
-    cross = [line[1] - line[3] for line in near]
-    fourth = [one(near[f], sign) + two(far[f], sign) for f in range(FIELDS)]
-    add(u_out, edge, k2 * (far[0][0] + sign * cross[1]) - k4 * fourth[0])
-    add(u_out, following, k2 * near[0][0] - k4 * two(near[0], sign))
-    add(v_out, edge, k2 * (sign * cross[0]) - k4 * fourth[1])
-    add(v_out, following, -k4 * two(near[1], sign))
-    add(t_out, edge, -k4 * fourth[2] - (0.25 * sign) * wind * near[2][0])
-    add(t_out, following, -k4 * two(near[2], sign))
+def border_rows(sign):
+    return (CX - 1, CX - 2) if sign > 0 else (0, 1)
+
+
+def add_theta_rows(t_out, near, far, sign, k4, wind):
+    edge, following = border_rows(sign)
+    add(t_out, edge, -k4 * (one(near, sign) + two(far, sign)) - (0.25 * sign) * wind * near[0])
+    add(t_out, following, -k4 * two(near, sign))
+
+
+def add_wind_rows(u_out, v_out, near, far, sign, k4, k2):
+    edge, following = border_rows(sign)
+    (u1, v1), (u2, v2) = near, far
+    add(u_out, edge, k2 * (u2[0] + sign * (v1[1] - v1[3])) - k4 * (one(u1, sign) + two(u2, sign)))
+    add(u_out, following, k2 * u1[0] - k4 * two(u1, sign))
+    add(v_out, edge, k2 * (sign * (u1[1] - u1[3])) - k4 * (one(v1, sign) + two(v2, sign)))
+    add(v_out, following, -k4 * two(v1, sign))
 
 
 def bulk(u, v, t, hyper, damp, u_out, v_out, t_out, pick):
@@ -177,12 +184,7 @@
     pick[...] = jnp.where(k == want, 1.0, 0.0).astype(BF16)
 
 
-def borders(
-    u, u_in, v_in, t_in, own_a, own_b, col_a, col_b, row_a, row_b, hyper, damp, pick,
-    u_out, v_out, t_out, table, coef, quarter, turn, across,
-):
-    even_x, even_y = is_even("px"), is_even("py")
-    per_level(coef, quarter, hyper, damp)
+def level_rows(across, hyper, damp):
     parts = FLAT // 128
     spot = lax.broadcasted_iota(jnp.int32, (1, CY), 1) >> 4
     for k in range(parts):
@@ -192,93 +194,87 @@
             q = jnp.where(spot == i, damp[8 * k + i] * 0.25, q)
         across[k : k + 1, :] = c
         across[parts + k : parts + k + 1, :] = q
-    c4, q4 = across[0:parts, :], across[parts : 2 * parts, :]
-    place = lax.broadcasted_iota(jnp.int32, (parts, CY), 1) & (CX - 1)
-
-    def moved(x, a):
-        inside = place < CX - a if a > 0 else place >= -a
-        return jnp.where(inside, pltpu.roll(x, -a % CY, 1), 0.0)
-
-    def line(yes, no, f, col):
-        at = pl.ds(2 * parts * f + col, parts, stride=2)
-        return jnp.where(even_y, yes[at, :], no[at, :])
-
-    east = [[line(col_a, col_b, f, i) for i in range(2)] for f in range(FIELDS)]
-    west = [[line(col_b, col_a, f, i) for i in (1, 0)] for f in range(FIELDS)]
-    v_first, v_last = line(own_b, own_a, 1, 0), line(own_a, own_b, 1, 1)
-
-    def nearest(x, y, s):
-        total = 2.0 * moved(x, s) - 10.0 * (x + moved(x, -s)) + 2.0 * moved(x, -2 * s)
-        return total + next_one(y, s)
-
-    def next_one(x, s):
-        return x + 2.0 * moved(x, -s) + moved(x, -2 * s)
-
-    def slope(x):
-        return moved(x, 1) - moved(x, -1)
-
-    (ue, ve, te), (uw, vw, tw) = east, west
+    return across[0:parts, :], across[parts : 2 * parts, :]
+
+
+def line(yes, no, keep, f, col):
+    parts = FLAT // 128
+    at = pl.ds(2 * parts * f + col, parts, stride=2)
+    return jnp.where(keep, yes[at, :], no[at, :])
+
+
+def beside(col_a, col_b, keep, f):
+    east = [line(col_a, col_b, keep, f, i) for i in range(2)]
+    west = [line(col_b, col_a, keep, f, i) for i in (1, 0)]
+    return east, west
+
+
+def moved(x, a):
+    place = lax.broadcasted_iota(jnp.int32, x.shape, 1) & (CX - 1)
+    inside = place < CX - a if a > 0 else place >= -a
+    return jnp.where(inside, pltpu.roll(x, -a % CY, 1), 0.0)
+
+
+def next_one(x, s):
+    return x + 2.0 * moved(x, -s) + moved(x, -2 * s)
+
+
+def nearest(x, y, s):
+    total = 2.0 * moved(x, s) - 10.0 * (x + moved(x, -s)) + 2.0 * moved(x, -2 * s)
+    return total + next_one(y, s)
+
+
+def slope(x):
+    return moved(x, 1) - moved(x, -1)
+
+
+def add_columns(start, out, terms, turn):
+    for k in range(FLAT // 128):
+        for col, term in zip((0, 1, CY - 2, CY - 1), terms):
+            turn[col : col + 1, :] = term[k : k + 1, :]
+        out[k * 128 : (k + 1) * 128, :] = start[k * 128 : (k + 1) * 128, :] + turn[...].T
+
+
+def outside(this, other, keep, f, i):
+    lane = lax.broadcasted_iota(jnp.int32, (LEV, CY), 1)
+    at = (i * FIELDS + f) * LEV
+    c = jnp.where(keep, this[at : at + LEV, :], other[at : at + LEV, :])
+    return (c,) + tuple(shifted(lane, c, 0.0, b) for b in (1, 2, -1, -2))
+
+
+def theta_borders(
+    u, t_in, own_a, own_b, col_b, col_a, row_a, row_b, hyper, damp, pick, t_out, table, coef, quarter, turn, across
+):
+    even_x, even_y = is_even("px"), is_even("py")
+    per_level(coef, quarter, hyper, damp)
+    c4, _ = level_rows(across, hyper, damp)
+    east, west = beside(col_a, col_b, even_y, 2)
+    v_first, v_last = line(own_b, own_a, even_y, 1, 0), line(own_a, own_b, even_y, 1, 1)
+    turn[...] = jnp.zeros_like(turn)
     terms = (
-        (
-            -c4 * nearest(*uw, -1) - q4 * slope(vw[0]),
-            -c4 * next_one(uw[0], -1),
-            -c4 * next_one(ue[0], 1),
-            -c4 * nearest(*ue, 1) + q4 * slope(ve[0]),
-        ),
-        (
-            -c4 * nearest(*vw, -1) + q4 * (vw[1] - slope(uw[0])),
-            -c4 * next_one(vw[0], -1) + q4 * vw[0],
-            -c4 * next_one(ve[0], 1) + q4 * ve[0],
-            -c4 * nearest(*ve, 1) + q4 * (ve[1] + slope(ue[0])),
-        ),
-        (
-            -c4 * nearest(*tw, -1) + 0.25 * v_first * tw[0],
-            -c4 * next_one(tw[0], -1),
-            -c4 * next_one(te[0], 1),
-            -c4 * nearest(*te, 1) - 0.25 * v_last * te[0],
-        ),
+        -c4 * nearest(*west, -1) + 0.25 * v_first * west[0],
+        -c4 * next_one(west[0], -1),
+        -c4 * next_one(east[0], 1),
+        -c4 * nearest(*east, 1) - 0.25 * v_last * east[0],
     )
-    turn[...] = jnp.zeros_like(turn)
-    for f, (start, out) in enumerate(((u_in, u_out), (v_in, v_out), (t_in, t_out))):
-        for k in range(parts):
-            for col, term in zip((0, 1, CY - 2, CY - 1), terms[f]):
-                turn[col : col + 1, :] = term[k : k + 1, :]
-            out[k * 128 : (k + 1) * 128, :] = start[k * 128 : (k + 1) * 128, :] + turn[...].T
-    lane = lax.broadcasted_iota(jnp.int32, (LEV, CY), 1)
-
-    def outside(this, other, keep, i):
-        line = []
-        for f in range(FIELDS):
-            at = (i * FIELDS + f) * LEV
-            c = jnp.where(keep, this[at : at + LEV, :], other[at : at + LEV, :])
-            line.append((c,) + tuple(shifted(lane, c, 0.0, b) for b in (1, 2, -1, -2)))
-        return line
-
+    add_columns(t_in, t_out, terms, turn)
     for sign, this, other, near, far in ((-1, row_b, row_a, 1, 0), (1, row_a, row_b, 0, 1)):
-        wind = u[pl.ds(0 if sign < 0 else CX - 1, LEV, stride=CX), :]
-        add_rows(
-            u_out,
-            v_out,
-            t_out,
-            outside(this, other, even_x, near),
-            outside(this, other, even_x, far),
-            sign,
-            coef[...],
-            quarter[...],
-            wind,
-        )
+        wind = u[pl.ds(border_rows(sign)[0], LEV, stride=CX), :]
+        near, far = (outside(this, other, even_x, 2, i) for i in (near, far))
+        add_theta_rows(t_out, near, far, sign, coef[...], wind)
+    both = []
     for rl in range(4):
         parts = [t_out[pl.ds(4 * rh + rl, LEV, stride=CX), :] for rh in range(4)]
         tops = [part.astype(BF16) for part in parts]
         rests = [(part - top.astype(F32)).astype(BF16) for part, top in zip(parts, tops)]
-        both = jnp.concatenate(
-            [jnp.concatenate(tops, axis=1), jnp.concatenate(rests, axis=1)], axis=0
-        )
-        put = jnp.dot(both, pick[...], preferred_element_type=F32)
+        both += [jnp.concatenate(tops, axis=1), jnp.concatenate(rests, axis=1)]
+    put = jnp.dot(jnp.concatenate(both, axis=0), pick[...], preferred_element_type=F32)
+    for rl in range(4):
         for half in range(2):
             lanes = slice(half * 128, half * 128 + 128)
             for cl in range(4):
-                x = put[half * LEV : (half + 1) * LEV, cl * 128 : (cl + 1) * 128]
+                at = (2 * rl + half) * LEV
+                x = put[at : at + LEV, cl * 128 : (cl + 1) * 128]
                 table[(rl * 5 + cl) * LEV : (rl * 5 + cl + 1) * LEV, lanes] = x.astype(BF16)
                 if cl == 0:
                     table[(rl * 5 + 4) * LEV : (rl * 5 + 5) * LEV, lanes] = pltpu.roll(
@@ -307,24 +303,48 @@
     return lines
 
 
-def corners(obs, u_in, v_in, t_in, coef, quarter, u_out, v_out, t_out, turn):
-    u_out[...] = u_in[...]
-    v_out[...] = v_in[...]
+def rest(
+    u_in, v_in, t_in, col_b, col_a, row_a, row_b, obs, coef, quarter, hyper, damp, u_out, v_out, t_out, turn, across
+):
+    even_x, even_y = is_even("px"), is_even("py")
+    c4, q4 = level_rows(across, hyper, damp)
+    ue, uw = beside(col_a, col_b, even_y, 0)
+    ve, vw = beside(col_a, col_b, even_y, 1)
+    turn[...] = jnp.zeros_like(turn)
+    add_columns(
+        u_in,
+        u_out,
+        (
+            -c4 * nearest(*uw, -1) - q4 * slope(vw[0]),
+            -c4 * next_one(uw[0], -1),
+            -c4 * next_one(ue[0], 1),
+            -c4 * nearest(*ue, 1) + q4 * slope(ve[0]),
+        ),
+        turn,
+    )
+    add_columns(
+        v_in,
+        v_out,
+        (
+            -c4 * nearest(*vw, -1) + q4 * (vw[1] - slope(uw[0])),
+            -c4 * next_one(vw[0], -1) + q4 * vw[0],
+            -c4 * next_one(ve[0], 1) + q4 * ve[0],
+            -c4 * nearest(*ve, 1) + q4 * (ve[1] + slope(ue[0])),
+        ),
+        turn,
+    )
     t_out[...] = t_in[...]
     lines = [corner_lines(obs, turn, f) for f in range(FIELDS)]
     none = jnp.zeros((LEV, CY), F32)
-    for sign, near, far in ((-1, 1, 0), (1, 2, 3)):
-        add_rows(
-            u_out,
-            v_out,
-            t_out,
-            [line[near] for line in lines],
-            [line[far] for line in lines],
-            sign,
-            coef[...],
-            quarter[...],
-            none,
-        )
+    for sign, this, other, near, far in ((-1, row_b, row_a, 1, 0), (1, row_a, row_b, 0, 1)):
+        spot = 0 if sign < 0 else 2
+        straight = [[outside(this, other, even_x, f, i) for f in range(2)] for i in (near, far)]
+        corner = [[lines[f][spot + i] for f in range(FIELDS)] for i in (near, far)]
+        both = [
+            [tuple(p + q for p, q in zip(straight[i][f], corner[i][f])) for f in range(2)] for i in range(2)
+        ]
+        add_wind_rows(u_out, v_out, both[0], both[1], sign, coef[...], quarter[...])
+        add_theta_rows(t_out, corner[0][2], corner[1][2], sign, coef[...], none)
 
 
 def interpolate(start, obs, t, coef, table, model, block, row, col, lev, turn):
@@ -448,14 +468,15 @@
         compiler_params=PARAMS,
         cost_estimate=cost(8000000, 10000000),
     )(u, v, t, hyper, damp)
-    u_most, v_most, t_most, table, coef, quarter = pl.pallas_call(
-        borders,
-        out_shape=(patch, patch, patch, grid, plane, plane),
-        in_specs=[VMEM] * 10 + [SMEM] * 2 + [VMEM],
-        scratch_shapes=[turn, pltpu.VMEM((8, CY), F32)],
+    across = pltpu.VMEM((8, CY), F32)
+    t_most, table, coef, quarter = pl.pallas_call(
+        theta_borders,
+        out_shape=(patch, grid, plane, plane),
+        in_specs=[VMEM] * 8 + [SMEM] * 2 + [VMEM],
+        scratch_shapes=[turn, across],
         compiler_params=PARAMS,
         cost_estimate=cost(4000000, 3000000),
-    )(u, u_part, v_part, t_part, own_a, own_b, col_a, col_b, row_a, row_b, hyper, damp, pick)
+    )(u, t_part, own_a, own_b, col_b, col_a, row_a, row_b, hyper, damp, pick)
     _, model = pl.pallas_call(
         interpolate,
         out_shape=(grid, shape((owners, slots), F32)),
@@ -466,13 +487,13 @@
         cost_estimate=cost(6500000000, 1000000),
     )(table, got, t_most, coef)
     u_next, v_next, t_next = pl.pallas_call(
-        corners,
+        rest,
         out_shape=(patch, patch, patch),
-        in_specs=[VMEM] * 6,
-        scratch_shapes=[turn],
+        in_specs=[VMEM] * 10 + [SMEM] * 2,
+        scratch_shapes=[turn, across],
         compiler_params=PARAMS,
         cost_estimate=cost(4000000, 3000000),
-    )(got, u_most, v_most, t_most, coef, quarter)
+    )(u_part, v_part, t_most, col_b, col_a, row_a, row_b, got, coef, quarter, hyper, damp)
     back = lax.all_to_all(model, BOTH, split_axis=0, concat_axis=0, tiled=True)
     departures = mask.astype(F32) * (values - back[None])
     whole = theta.shape

time: 54.1 us -> 53.1 us (0.982)
  starting transfers between devices: 24.9 us -> 23.4 us
  Pallas kernels: 17 us -> 17.9 us
    all_to_all x1, waiting for transfers between devices: 8.39 us -> 7.16 us  [on_device(): back = lax.all_to_all(model, BOTH, split_axis=0, concat_axis=0, tiled=True)]
    ppermute x1, starting transfers between devices: 1.19 us -> 0.01 us  [on_device(): col_a = lax.ppermute(own_a, 'py', swap('py', 0))]
    all_to_all x1, starting transfers between devices: 5.65 us -> 4.67 us  [on_device(): back = lax.all_to_all(model, BOTH, split_axis=0, concat_axis=0, tiled=True)]
    pallas_call x2, Pallas kernels: 2.74 us -> 3.69 us  [the longest x1 2.52 us: on_device(): pl.pallas_call(rest, out_shape=(patch, patch, patch), in_specs=[VMEM] * 1...]
    ppermute x1, starting transfers between devices: 4.7 us -> 5.38 us  [on_device(): col_b = lax.ppermute(own_b, 'py', swap('py', 1))]
  transfers between devices with their start and end apart: 6 -> 6, of which waited for: 2 -> 3; matrix products, arithmetic and copies ran while one was open for 0% -> 0% of each run, Pallas kernels for 10% -> 12%
where the time goes in v5:
time: 53.1 us; the launch traced here: 52.9 us
  starting transfers between devices  23.4 us (44%)
  Pallas kernels  17.9 us (34%)
  waiting for transfers between devices  10.1 us (19%)
  between operations  0.75 us (1%)
  other arithmetic  0.64 us (1%)
    all_to_all x1, starting transfers between devices, on_device(): got = lax.all_to_all(sent, BOTH, split_axis=0, concat_axis=0, tiled=True)  11.5 us
    pallas_call x1, Pallas kernels, on_device(): pl.pallas_call(interpolate, out_shape=(grid, shape((owners, slots), F32))...  9.15 us
    all_to_all x1, waiting for transfers between devices, on_device(): back = lax.all_to_all(model, BOTH, split_axis=0, concat_axis=0, tiled=True)  7.16 us
    ppermute x1, starting transfers between devices, on_device(): col_b = lax.ppermute(own_b, 'py', swap('py', 1))  5.38 us
    all_to_all x1, starting transfers between devices, on_device(): back = lax.all_to_all(model, BOTH, split_axis=0, concat_axis=0, tiled=True)  4.67 us
    all_to_all x1, waiting for transfers between devices, on_device(): got = lax.all_to_all(sent, BOTH, split_axis=0, concat_axis=0, tiled=True)  2.61 us
    pallas_call x1, Pallas kernels, on_device(): pl.pallas_call(rest, out_shape=(patch, patch, patch), in_specs=[VMEM] * 1...  2.52 us
    pallas_call x1, Pallas kernels, on_device(): pl.pallas_call(bulk, out_shape=(patch, patch, patch, shape((4 * CY, 4 * C...  2.48 us
  transfers between devices with their start and end apart: 6, of which 3 were waited for; matrix products, arithmetic and copies ran while one was open for 0% of the time, Pallas kernels for 12%

profile of v5, /device:TPU:1, one launch (start us, length us, event | category | flops | bytes accessed | tf_op | source)
XLA Modules:
  0.0 52.9 jit_solution(16236176851578798727)
XLA Ops:
  0.6 2.3 %shard_map.141 = f32[128,8,128]{2,1,0:T(8,128)} custom-call(f32[512,128]{1,0:T(8,128)} %bitcast.20, f32[512,128]{1,0:T(8,128)} %bitcast.24, f32[512,128]{1,0:T(8,128)} %bitcast.27, s32[128,128]{1,0:T(8,128)} %bitcast.32, s32[128,128]{1,0:T(8,128)} %bitcast.33, f32[3,128,128]{2,1,0:T(8,128)} %bitcast.31, f32[128,128]{1,0:T(8,128)} %bitcast.34), custom_call_target="tpu_custom_call" | custom-call | flops 100000 | bytes 3000000 | tf_op jit(solution)/shard_map/pallas_call | solution.py:429
  3.0 0.0 copy-start
  3.0 0.0 copy-start.1
  3.0 0.0 copy-start.2
  3.0 11.5 %all-to-all-start = ((f32[128,8,128]{2,1,0:T(8,128)}), f32[128,8,128]{2,1,0:T(8,128)S(1)}, u32[]{:S(2)}, u32[]{:S(2)}) async-start(f32[128,8,128]{2,1,0:T(8,128)} %shard_map.141), calls=%async_computation | async-start | bytes 1048576 | tf_op jit(solution)/shard_map/all_to_all | solution.py:446
  14.5 0.0 copy-done
  14.5 0.0 copy-done.1
  14.5 0.0 copy-done.2
  14.5 0.3 shard_map.139
  14.8 1.1 %collective-permute-start.2 = (f32[192,128]{1,0:T(8,128)S(1)}, f32[192,128]{1,0:T(8,128)S(1)}, u32[]{:S(2)}, u32[]{:S(2)}) collective-permute-start(f32[192,128]{1,0:T(8,128)S(1)} %get-tuple-element.25), channel_id=1, source_target_pairs={{0,16},{32,48},{64,80},{96,112},{16,0},{48,32},{80,64},{112,96},{1... | collective-permute-start | bytes 294920 | tf_op jit(solution)/shard_map/ppermute | solution.py:459
  15.9 0.7 %collective-permute-start.3 = (f32[192,128]{1,0:T(8,128)S(1)}, f32[192,128]{1,0:T(8,128)S(1)}, u32[]{:S(2)}, u32[]{:S(2)}) collective-permute-start(f32[192,128]{1,0:T(8,128)S(1)} %get-tuple-element.26), channel_id=1, source_target_pairs={{16,32},{48,64},{80,96},{112,0},{32,16},{64,48},{96,80},{0,112},{1... | collective-permute-start | bytes 294920 | tf_op jit(solution)/shard_map/ppermute | solution.py:458
  16.7 0.0 copy-start.3
  16.7 0.0 copy-start.4
  16.7 5.4 %collective-permute-start = (f32[24,128]{1,0:T(8,128)S(1)}, f32[24,128]{1,0:T(8,128)S(1)}, u32[]{:S(2)}, u32[]{:S(2)}) collective-permute-start(f32[24,128]{1,0:T(8,128)S(1)} %get-tuple-element.24.own_b), channel_id=1, source_target_pairs={{1,2},{3,4},{5,6},{7,8},{9,10},{11,12},{13,14},{15,0},{2,1},{4,3},... | collective-permute-start | bytes 36872 | tf_op jit(solution)/shard_map/ppermute | solution.py:456
  22.0 0.0 collective-permute-start.1
  22.1 0.0 copy-done.3
  22.1 0.0 copy-done.4
  22.1 2.5 %shard_map.138 = (f32[512,128]{1,0:T(8,128)S(1)}, f32[512,128]{1,0:T(8,128)S(1)}, f32[512,128]{1,0:T(8,128)S(1)}, bf16[512,512]{1,0:T(8,128)(2,1)S(1)}) custom-call(f32[512,128]{1,0:T(8,128)S(1)} %bitcast.22, f32[512,128]{1,0:T(8,128)S(1)} %bitcast.26, f32[512,128]{1,0:T(8,128)S(1)} %bitcast.29, f32[32]{0:T(128)S(1)} %copy-done.3, f32[32]{0:T(128)S(1)} %copy-done.4), custom_call_target="tpu_custom_call" | custom-call | flops 8000000 | bytes 10000000 | tf_op jit(solution)/shard_map/pallas_call | solution.py:464
  24.5 0.0 collective-permute-done.col_b
  24.6 0.3 collective-permute-done.1.col_a
  24.9 0.0 collective-permute-done.2.row_a
  24.9 0.0 collective-permute-done.3.row_b
  24.9 1.2 %shard_map.140 = (f32[512,128]{1,0:T(8,128)S(1)}, bf16[768,256]{1,0:T(8,128)(2,1)S(1)}, f32[32,128]{1,0:T(8,128)S(1)}, f32[32,128]{1,0:T(8,128)S(1)}) custom-call(f32[512,128]{1,0:T(8,128)S(1)} %bitcast.23, f32[512,128]{1,0:T(8,128)S(1)} %get-tuple-element.22.t_in, f32[24,128]{1,0:T(8,128)S(1)} %get-tuple-element.23.own_a, ...), custom_call_target="tpu_custom_call" | custom-call | flops 4000000 | bytes 3000000 | tf_op jit(solution)/shard_map/pallas_call | solution.py:472
  26.1 2.6 %all-to-all-done.obs = f32[128,8,128]{2,1,0:T(8,128)S(1)} async-done(((f32[128,8,128]{2,1,0:T(8,128)}), f32[128,8,128]{2,1,0:T(8,128)S(1)}, u32[]{:S(2)}, u32[]{:S(2)}) %all-to-all-start) | async-done | bytes 524320 | tf_op jit(solution)/shard_map/all_to_all | solution.py:446
  28.7 9.2 %shard_map.143 = (bf16[768,256]{1,0:T(8,128)(2,1)S(1)}, f32[128,128]{1,0:T(8,128)}) custom-call(bf16[768,256]{1,0:T(8,128)(2,1)S(1)} %get-tuple-element.34.start, f32[128,8,128]{2,1,0:T(8,128)S(1)} %all-to-all-done.obs, f32[512,128]{1,0:T(8,128)S(1)} %get-tuple-element.28.t_in.t, f32[32,128]{1,0:T(8,128)S(1)} %get-tuple-element.29.coef), custom_call_target="tpu_custom_call", output_to_operand_aliasing={{0}: (0, {})} | custom-call | flops 6499999744 | bytes 1000000 | tf_op jit(solution)/shard_map/pallas_call | solution.py:480
  37.9 4.7 %all-to-all-start.1 = ((f32[128,1,128]{2,1,0:T(1,128)}), f32[128,1,128]{2,1,0:T(1,128)S(1)}, u32[]{:S(2)}, u32[]{:S(2)}) async-start(f32[128,1,128]{2,1,0:T(1,128)} %bitcast.12), calls=%async_computation.1 | async-start | bytes 131072 | tf_op jit(solution)/shard_map/all_to_all | solution.py:497
  42.5 0.0 copy-start.5
  42.5 0.0 copy-start.6
  42.6 2.5 %shard_map.142 = (f32[512,128]{1,0:T(8,128)}, f32[512,128]{1,0:T(8,128)}, f32[512,128]{1,0:T(8,128)}) custom-call(f32[512,128]{1,0:T(8,128)S(1)} %get-tuple-element.20.u_in, f32[512,128]{1,0:T(8,128)S(1)} %get-tuple-element.21.v_in, f32[512,128]{1,0:T(8,128)S(1)} %get-tuple-element.28.t_in.t, f32[24,128]{1,0:T(8,128)S(1)} %collective-permute-done.col_b, ...), custom_call_target="tpu_custom_call" | custom-call | flops 4000000 | bytes 3000000 | tf_op jit(solution)/shard_map/pallas_call | solution.py:489
  45.1 7.2 %all-to-all-done.1 = f32[128,1,128]{2,1,0:T(1,128)S(1)} async-done(((f32[128,1,128]{2,1,0:T(1,128)}), f32[128,1,128]{2,1,0:T(1,128)S(1)}, u32[]{:S(2)}, u32[]{:S(2)}) %all-to-all-start.1) | async-done | bytes 65568 | tf_op jit(solution)/shard_map/all_to_all | solution.py:497
  52.2 0.0 copy-done.5
  52.2 0.0 copy-done.6
  52.2 0.6 %fusion = f32[1,128,128]{2,1,0:T(8,128)} fusion(f32[1,128,128]{2,1,0:T(8,128)S(1)} %copy-done.5, s32[1,128,128]{2,1,0:T(8,128)S(1)} %copy-done.6, f32[1,128,128]{2,1,0:T(8,128)S(1)} %bitcast.30), kind=kLoop, calls=%fused_computation.1 | loop fusion | flops 49152 | bytes 262144 | tf_op jit(solution)/shard_map/mul | solution.py:498
Async XLA Ops:
  3.0 11.5 %copy-start = (f32[32,16,128]{2,1,0:T(8,128)S(1)}, f32[32,16,128]{2,1,0:T(8,128)}, u32[]{:S(2)}) copy-start(f32[32,16,128]{2,1,0:T(8,128)} %param.12) | copy-start | bytes 786436
  3.0 11.5 %copy-start.1 = (f32[32,16,128]{2,1,0:T(8,128)S(1)}, f32[32,16,128]{2,1,0:T(8,128)}, u32[]{:S(2)}) copy-start(f32[32,16,128]{2,1,0:T(8,128)} %param.13) | copy-start | bytes 786436
  3.0 11.5 %copy-start.2 = (f32[32,16,128]{2,1,0:T(8,128)S(1)}, f32[32,16,128]{2,1,0:T(8,128)}, u32[]{:S(2)}) copy-start(f32[32,16,128]{2,1,0:T(8,128)} %param.11) | copy-start | bytes 786436
  3.0 25.7 %all-to-all-start = ((f32[128,8,128]{2,1,0:T(8,128)}), f32[128,8,128]{2,1,0:T(8,128)S(1)}, u32[]{:S(2)}, u32[]{:S(2)}) async-start(f32[128,8,128]{2,1,0:T(8,128)} %shard_map.141), calls=%async_computation | async-start | bytes 1048576 | tf_op jit(solution)/shard_map/all_to_all | solution.py:446
  14.8 10.1 %collective-permute-start.2 = (f32[192,128]{1,0:T(8,128)S(1)}, f32[192,128]{1,0:T(8,128)S(1)}, u32[]{:S(2)}, u32[]{:S(2)}) collective-permute-start(f32[192,128]{1,0:T(8,128)S(1)} %get-tuple-element.25), channel_id=1, source_target_pairs={{0,16},{32,48},{64,80},{96,112},{16,0},{48,32},{80,64},{112,96},{1... | collective-permute-start | bytes 294920 | tf_op jit(solution)/shard_map/ppermute | solution.py:459
  15.9 9.0 %collective-permute-start.3 = (f32[192,128]{1,0:T(8,128)S(1)}, f32[192,128]{1,0:T(8,128)S(1)}, u32[]{:S(2)}, u32[]{:S(2)}) collective-permute-start(f32[192,128]{1,0:T(8,128)S(1)} %get-tuple-element.26), channel_id=1, source_target_pairs={{16,32},{48,64},{80,96},{112,0},{32,16},{64,48},{96,80},{0,112},{1... | collective-permute-start | bytes 294920 | tf_op jit(solution)/shard_map/ppermute | solution.py:458
  16.7 5.4 %copy-start.3 = (f32[32]{0:T(128)S(1)}, f32[32]{0:T(128)}, u32[]{:S(2)}) copy-start(f32[32]{0:T(128)} %hyper.5) | copy-start | bytes 388
  16.7 5.4 %copy-start.4 = (f32[32]{0:T(128)S(1)}, f32[32]{0:T(128)}, u32[]{:S(2)}) copy-start(f32[32]{0:T(128)} %damp.5) | copy-start | bytes 388
  16.7 7.9 %collective-permute-start = (f32[24,128]{1,0:T(8,128)S(1)}, f32[24,128]{1,0:T(8,128)S(1)}, u32[]{:S(2)}, u32[]{:S(2)}) collective-permute-start(f32[24,128]{1,0:T(8,128)S(1)} %get-tuple-element.24.own_b), channel_id=1, source_target_pairs={{1,2},{3,4},{5,6},{7,8},{9,10},{11,12},{13,14},{15,0},{2,1},{4,3},... | collective-permute-start | bytes 36872 | tf_op jit(solution)/shard_map/ppermute | solution.py:456
  22.0 2.9 %collective-permute-start.1 = (f32[24,128]{1,0:T(8,128)S(1)}, f32[24,128]{1,0:T(8,128)S(1)}, u32[]{:S(2)}, u32[]{:S(2)}) collective-permute-start(f32[24,128]{1,0:T(8,128)S(1)} %get-tuple-element.23.own_a), channel_id=1, source_target_pairs={{0,1},{2,3},{4,5},{6,7},{8,9},{10,11},{12,13},{14,15},{1,0},{3,2},... | collective-permute-start | bytes 36872 | tf_op jit(solution)/shard_map/ppermute | solution.py:457
  37.9 14.4 %all-to-all-start.1 = ((f32[128,1,128]{2,1,0:T(1,128)}), f32[128,1,128]{2,1,0:T(1,128)S(1)}, u32[]{:S(2)}, u32[]{:S(2)}) async-start(f32[128,1,128]{2,1,0:T(1,128)} %bitcast.12), calls=%async_computation.1 | async-start | bytes 131072 | tf_op jit(solution)/shard_map/all_to_all | solution.py:497
  42.5 9.7 %copy-start.5 = (f32[1,128,128]{2,1,0:T(8,128)S(1)}, f32[1,128,128]{2,1,0:T(8,128)}, u32[]{:S(2)}) copy-start(f32[1,128,128]{2,1,0:T(8,128)} %param.20) | copy-start | bytes 196612
  42.5 9.7 %copy-start.6 = (s32[1,128,128]{2,1,0:T(8,128)S(1)}, s32[1,128,128]{2,1,0:T(8,128)}, u32[]{:S(2)}) copy-start(s32[1,128,128]{2,1,0:T(8,128)} %param.21) | copy-start | bytes 196612

commit v6 on v5

--- a/solution.py
+++ b/solution.py
@@ -38,15 +38,16 @@
     return x * count_y + lax.rem(lax.axis_index("py") + count_y + move_y, count_y)
 
 
-def messages_out(u, v, t, cells, levels, bary, vfrac, sent, fields, ints, floats, weights, packed, turn, sems):
+def messages_out(u, v, t, cells, levels, bary, vfrac, sent, fields, ints, packed, turn, sems):
     copies = [
         pltpu.make_async_copy(u, fields.at[0], sems.at[0]),
         pltpu.make_async_copy(v, fields.at[1], sems.at[1]),
         pltpu.make_async_copy(t, fields.at[2], sems.at[2]),
         pltpu.make_async_copy(cells, ints.at[0], sems.at[3]),
         pltpu.make_async_copy(levels, ints.at[1], sems.at[4]),
-        pltpu.make_async_copy(vfrac, floats, sems.at[5]),
-        pltpu.make_async_copy(bary.at[pl.ds(0, 2)], weights, sems.at[6]),
+        pltpu.make_async_copy(vfrac, packed.at[:, 2, :], sems.at[5]),
+        pltpu.make_async_copy(bary.at[0], packed.at[:, 3, :], sems.at[6]),
+        pltpu.make_async_copy(bary.at[1], packed.at[:, 4, :], sems.at[7]),
     ]
     for copy in copies:
         copy.start()
@@ -55,9 +56,6 @@
         copy.wait()
     packed[:, 0, :] = ints[0].astype(F32)
     packed[:, 1, :] = ints[1].astype(F32)
-    packed[:, 2, :] = floats[...]
-    packed[:, 3, :] = weights[0]
-    packed[:, 4, :] = weights[1]
     half = lax.broadcasted_iota(jnp.int32, (1, CY), 1) < CY // 2
     for f in range(FIELDS):
         for i, r in enumerate(ROWS):
@@ -434,11 +432,9 @@
         scratch_shapes=[
             pltpu.VMEM((FIELDS, FLAT, CY), F32),
             pltpu.VMEM((2, owners, slots), jnp.int32),
-            pltpu.VMEM((owners, slots), F32),
-            pltpu.VMEM((2, owners, slots), F32),
             pltpu.VMEM((owners, SENT, slots), F32),
             pltpu.VMEM((CY, CY), F32),
-            pltpu.SemaphoreType.DMA((7,)),
+            pltpu.SemaphoreType.DMA((8,)),
         ],
         compiler_params=WHOLE,
         cost_estimate=cost(100000, 3000000),

time: 53.1 us -> 53 us (level)
  no operation moved by 1% of the time
where the time goes in v6:
time: 53 us; the launch traced here: 52.8 us
  starting transfers between devices  23.4 us (44%)
  Pallas kernels  17.8 us (34%)
  waiting for transfers between devices  10.1 us (19%)
  between operations  0.75 us (1%)
  other arithmetic  0.64 us (1%)
    all_to_all x1, starting transfers between devices, on_device(): got = lax.all_to_all(sent, BOTH, split_axis=0, concat_axis=0, tiled=True)  11.5 us
    pallas_call x1, Pallas kernels, on_device(): pl.pallas_call(interpolate, out_shape=(grid, shape((owners, slots), F32))...  9.16 us
    all_to_all x1, waiting for transfers between devices, on_device(): back = lax.all_to_all(model, BOTH, split_axis=0, concat_axis=0, tiled=True)  7.16 us
    ppermute x1, starting transfers between devices, on_device(): col_b = lax.ppermute(own_b, 'py', swap('py', 1))  5.38 us
    all_to_all x1, starting transfers between devices, on_device(): back = lax.all_to_all(model, BOTH, split_axis=0, concat_axis=0, tiled=True)  4.66 us
    all_to_all x1, waiting for transfers between devices, on_device(): got = lax.all_to_all(sent, BOTH, split_axis=0, concat_axis=0, tiled=True)  2.6 us
    pallas_call x1, Pallas kernels, on_device(): pl.pallas_call(rest, out_shape=(patch, patch, patch), in_specs=[VMEM] * 1...  2.52 us
    pallas_call x1, Pallas kernels, on_device(): pl.pallas_call(bulk, out_shape=(patch, patch, patch, shape((4 * CY, 4 * C...  2.48 us
  transfers between devices with their start and end apart: 6, of which 3 were waited for; matrix products, arithmetic and copies ran while one was open for 0% of the time, Pallas kernels for 12%

profile of v6, /device:TPU:1, one launch (start us, length us, event | category | flops | bytes accessed | tf_op | source)
XLA Modules:
  0.0 52.8 jit_solution(2193396027976212519)
XLA Ops:
  0.6 2.2 %shard_map.141 = f32[128,8,128]{2,1,0:T(8,128)} custom-call(f32[512,128]{1,0:T(8,128)} %bitcast.20, f32[512,128]{1,0:T(8,128)} %bitcast.24, f32[512,128]{1,0:T(8,128)} %bitcast.27, s32[128,128]{1,0:T(8,128)} %bitcast.32, s32[128,128]{1,0:T(8,128)} %bitcast.33, f32[3,128,128]{2,1,0:T(8,128)} %bitcast.31, f32[128,128]{1,0:T(8,128)} %bitcast.34), custom_call_target="tpu_custom_call" | custom-call | flops 100000 | bytes 3000000 | tf_op jit(solution)/shard_map/pallas_call | solution.py:427
  2.9 0.0 copy-start
  2.9 0.0 copy-start.1
  2.9 0.0 copy-start.2
  2.9 11.5 %all-to-all-start = ((f32[128,8,128]{2,1,0:T(8,128)}), f32[128,8,128]{2,1,0:T(8,128)S(1)}, u32[]{:S(2)}, u32[]{:S(2)}) async-start(f32[128,8,128]{2,1,0:T(8,128)} %shard_map.141), calls=%async_computation | async-start | bytes 1048576 | tf_op jit(solution)/shard_map/all_to_all | solution.py:442
  14.4 0.0 copy-done
  14.4 0.0 copy-done.1
  14.4 0.0 copy-done.2
  14.5 0.3 shard_map.139
  14.7 1.1 %collective-permute-start.2 = (f32[192,128]{1,0:T(8,128)S(1)}, f32[192,128]{1,0:T(8,128)S(1)}, u32[]{:S(2)}, u32[]{:S(2)}) collective-permute-start(f32[192,128]{1,0:T(8,128)S(1)} %get-tuple-element.25), channel_id=1, source_target_pairs={{0,16},{32,48},{64,80},{96,112},{16,0},{48,32},{80,64},{112,96},{1... | collective-permute-start | bytes 294920 | tf_op jit(solution)/shard_map/ppermute | solution.py:455
  15.9 0.7 %collective-permute-start.3 = (f32[192,128]{1,0:T(8,128)S(1)}, f32[192,128]{1,0:T(8,128)S(1)}, u32[]{:S(2)}, u32[]{:S(2)}) collective-permute-start(f32[192,128]{1,0:T(8,128)S(1)} %get-tuple-element.26), channel_id=1, source_target_pairs={{16,32},{48,64},{80,96},{112,0},{32,16},{64,48},{96,80},{0,112},{1... | collective-permute-start | bytes 294920 | tf_op jit(solution)/shard_map/ppermute | solution.py:454
  16.6 0.0 copy-start.3
  16.6 0.0 copy-start.4
  16.6 5.4 %collective-permute-start = (f32[24,128]{1,0:T(8,128)S(1)}, f32[24,128]{1,0:T(8,128)S(1)}, u32[]{:S(2)}, u32[]{:S(2)}) collective-permute-start(f32[24,128]{1,0:T(8,128)S(1)} %get-tuple-element.24.own_b), channel_id=1, source_target_pairs={{1,2},{3,4},{5,6},{7,8},{9,10},{11,12},{13,14},{15,0},{2,1},{4,3},... | collective-permute-start | bytes 36872 | tf_op jit(solution)/shard_map/ppermute | solution.py:452
  22.0 0.0 collective-permute-start.1
  22.0 0.0 copy-done.3
  22.0 0.0 copy-done.4
  22.0 2.5 %shard_map.138 = (f32[512,128]{1,0:T(8,128)S(1)}, f32[512,128]{1,0:T(8,128)S(1)}, f32[512,128]{1,0:T(8,128)S(1)}, bf16[512,512]{1,0:T(8,128)(2,1)S(1)}) custom-call(f32[512,128]{1,0:T(8,128)S(1)} %bitcast.22, f32[512,128]{1,0:T(8,128)S(1)} %bitcast.26, f32[512,128]{1,0:T(8,128)S(1)} %bitcast.29, f32[32]{0:T(128)S(1)} %copy-done.3, f32[32]{0:T(128)S(1)} %copy-done.4), custom_call_target="tpu_custom_call" | custom-call | flops 8000000 | bytes 10000000 | tf_op jit(solution)/shard_map/pallas_call | solution.py:460
  24.5 0.0 collective-permute-done.col_b
  24.5 0.3 collective-permute-done.1.col_a
  24.8 0.0 collective-permute-done.2.row_a
  24.8 0.0 collective-permute-done.3.row_b
  24.8 1.2 %shard_map.140 = (f32[512,128]{1,0:T(8,128)S(1)}, bf16[768,256]{1,0:T(8,128)(2,1)S(1)}, f32[32,128]{1,0:T(8,128)S(1)}, f32[32,128]{1,0:T(8,128)S(1)}) custom-call(f32[512,128]{1,0:T(8,128)S(1)} %bitcast.23, f32[512,128]{1,0:T(8,128)S(1)} %get-tuple-element.22.t_in, f32[24,128]{1,0:T(8,128)S(1)} %get-tuple-element.23.own_a, ...), custom_call_target="tpu_custom_call" | custom-call | flops 4000000 | bytes 3000000 | tf_op jit(solution)/shard_map/pallas_call | solution.py:468
  26.0 2.6 %all-to-all-done.obs = f32[128,8,128]{2,1,0:T(8,128)S(1)} async-done(((f32[128,8,128]{2,1,0:T(8,128)}), f32[128,8,128]{2,1,0:T(8,128)S(1)}, u32[]{:S(2)}, u32[]{:S(2)}) %all-to-all-start) | async-done | bytes 524320 | tf_op jit(solution)/shard_map/all_to_all | solution.py:442
  28.6 9.2 %shard_map.143 = (bf16[768,256]{1,0:T(8,128)(2,1)S(1)}, f32[128,128]{1,0:T(8,128)}) custom-call(bf16[768,256]{1,0:T(8,128)(2,1)S(1)} %get-tuple-element.34.start, f32[128,8,128]{2,1,0:T(8,128)S(1)} %all-to-all-done.obs, f32[512,128]{1,0:T(8,128)S(1)} %get-tuple-element.28.t_in.t, f32[32,128]{1,0:T(8,128)S(1)} %get-tuple-element.29.coef), custom_call_target="tpu_custom_call", output_to_operand_aliasing={{0}: (0, {})} | custom-call | flops 6499999744 | bytes 1000000 | tf_op jit(solution)/shard_map/pallas_call | solution.py:476
  37.8 4.7 %all-to-all-start.1 = ((f32[128,1,128]{2,1,0:T(1,128)}), f32[128,1,128]{2,1,0:T(1,128)S(1)}, u32[]{:S(2)}, u32[]{:S(2)}) async-start(f32[128,1,128]{2,1,0:T(1,128)} %bitcast.12), calls=%async_computation.1 | async-start | bytes 131072 | tf_op jit(solution)/shard_map/all_to_all | solution.py:493
  42.5 0.0 copy-start.5
  42.5 0.0 copy-start.6
  42.5 2.5 %shard_map.142 = (f32[512,128]{1,0:T(8,128)}, f32[512,128]{1,0:T(8,128)}, f32[512,128]{1,0:T(8,128)}) custom-call(f32[512,128]{1,0:T(8,128)S(1)} %get-tuple-element.20.u_in, f32[512,128]{1,0:T(8,128)S(1)} %get-tuple-element.21.v_in, f32[512,128]{1,0:T(8,128)S(1)} %get-tuple-element.28.t_in.t, f32[24,128]{1,0:T(8,128)S(1)} %collective-permute-done.col_b, ...), custom_call_target="tpu_custom_call" | custom-call | flops 4000000 | bytes 3000000 | tf_op jit(solution)/shard_map/pallas_call | solution.py:485
  45.0 7.2 %all-to-all-done.1 = f32[128,1,128]{2,1,0:T(1,128)S(1)} async-done(((f32[128,1,128]{2,1,0:T(1,128)}), f32[128,1,128]{2,1,0:T(1,128)S(1)}, u32[]{:S(2)}, u32[]{:S(2)}) %all-to-all-start.1) | async-done | bytes 65568 | tf_op jit(solution)/shard_map/all_to_all | solution.py:493
  52.2 0.0 copy-done.5
  52.2 0.0 copy-done.6
  52.2 0.6 %fusion = f32[1,128,128]{2,1,0:T(8,128)} fusion(f32[1,128,128]{2,1,0:T(8,128)S(1)} %copy-done.5, s32[1,128,128]{2,1,0:T(8,128)S(1)} %copy-done.6, f32[1,128,128]{2,1,0:T(8,128)S(1)} %bitcast.30), kind=kLoop, calls=%fused_computation.1 | loop fusion | flops 49152 | bytes 262144 | tf_op jit(solution)/shard_map/mul | solution.py:494
Async XLA Ops:
  2.9 11.5 %copy-start = (f32[32,16,128]{2,1,0:T(8,128)S(1)}, f32[32,16,128]{2,1,0:T(8,128)}, u32[]{:S(2)}) copy-start(f32[32,16,128]{2,1,0:T(8,128)} %param.12) | copy-start | bytes 786436
  2.9 11.5 %copy-start.1 = (f32[32,16,128]{2,1,0:T(8,128)S(1)}, f32[32,16,128]{2,1,0:T(8,128)}, u32[]{:S(2)}) copy-start(f32[32,16,128]{2,1,0:T(8,128)} %param.13) | copy-start | bytes 786436
  2.9 11.5 %copy-start.2 = (f32[32,16,128]{2,1,0:T(8,128)S(1)}, f32[32,16,128]{2,1,0:T(8,128)}, u32[]{:S(2)}) copy-start(f32[32,16,128]{2,1,0:T(8,128)} %param.11) | copy-start | bytes 786436
  2.9 25.7 %all-to-all-start = ((f32[128,8,128]{2,1,0:T(8,128)}), f32[128,8,128]{2,1,0:T(8,128)S(1)}, u32[]{:S(2)}, u32[]{:S(2)}) async-start(f32[128,8,128]{2,1,0:T(8,128)} %shard_map.141), calls=%async_computation | async-start | bytes 1048576 | tf_op jit(solution)/shard_map/all_to_all | solution.py:442
  14.7 10.1 %collective-permute-start.2 = (f32[192,128]{1,0:T(8,128)S(1)}, f32[192,128]{1,0:T(8,128)S(1)}, u32[]{:S(2)}, u32[]{:S(2)}) collective-permute-start(f32[192,128]{1,0:T(8,128)S(1)} %get-tuple-element.25), channel_id=1, source_target_pairs={{0,16},{32,48},{64,80},{96,112},{16,0},{48,32},{80,64},{112,96},{1... | collective-permute-start | bytes 294920 | tf_op jit(solution)/shard_map/ppermute | solution.py:455
  15.9 9.0 %collective-permute-start.3 = (f32[192,128]{1,0:T(8,128)S(1)}, f32[192,128]{1,0:T(8,128)S(1)}, u32[]{:S(2)}, u32[]{:S(2)}) collective-permute-start(f32[192,128]{1,0:T(8,128)S(1)} %get-tuple-element.26), channel_id=1, source_target_pairs={{16,32},{48,64},{80,96},{112,0},{32,16},{64,48},{96,80},{0,112},{1... | collective-permute-start | bytes 294920 | tf_op jit(solution)/shard_map/ppermute | solution.py:454
  16.6 5.4 %copy-start.3 = (f32[32]{0:T(128)S(1)}, f32[32]{0:T(128)}, u32[]{:S(2)}) copy-start(f32[32]{0:T(128)} %hyper.5) | copy-start | bytes 388
  16.6 5.4 %copy-start.4 = (f32[32]{0:T(128)S(1)}, f32[32]{0:T(128)}, u32[]{:S(2)}) copy-start(f32[32]{0:T(128)} %damp.5) | copy-start | bytes 388
  16.6 7.9 %collective-permute-start = (f32[24,128]{1,0:T(8,128)S(1)}, f32[24,128]{1,0:T(8,128)S(1)}, u32[]{:S(2)}, u32[]{:S(2)}) collective-permute-start(f32[24,128]{1,0:T(8,128)S(1)} %get-tuple-element.24.own_b), channel_id=1, source_target_pairs={{1,2},{3,4},{5,6},{7,8},{9,10},{11,12},{13,14},{15,0},{2,1},{4,3},... | collective-permute-start | bytes 36872 | tf_op jit(solution)/shard_map/ppermute | solution.py:452
  22.0 2.9 %collective-permute-start.1 = (f32[24,128]{1,0:T(8,128)S(1)}, f32[24,128]{1,0:T(8,128)S(1)}, u32[]{:S(2)}, u32[]{:S(2)}) collective-permute-start(f32[24,128]{1,0:T(8,128)S(1)} %get-tuple-element.23.own_a), channel_id=1, source_target_pairs={{0,1},{2,3},{4,5},{6,7},{8,9},{10,11},{12,13},{14,15},{1,0},{3,2},... | collective-permute-start | bytes 36872 | tf_op jit(solution)/shard_map/ppermute | solution.py:453
  37.8 14.4 %all-to-all-start.1 = ((f32[128,1,128]{2,1,0:T(1,128)}), f32[128,1,128]{2,1,0:T(1,128)S(1)}, u32[]{:S(2)}, u32[]{:S(2)}) async-start(f32[128,1,128]{2,1,0:T(1,128)} %bitcast.12), calls=%async_computation.1 | async-start | bytes 131072 | tf_op jit(solution)/shard_map/all_to_all | solution.py:493
  42.5 9.7 %copy-start.5 = (f32[1,128,128]{2,1,0:T(8,128)S(1)}, f32[1,128,128]{2,1,0:T(8,128)}, u32[]{:S(2)}) copy-start(f32[1,128,128]{2,1,0:T(8,128)} %param.20) | copy-start | bytes 196612
  42.5 9.7 %copy-start.6 = (s32[1,128,128]{2,1,0:T(8,128)S(1)}, s32[1,128,128]{2,1,0:T(8,128)}, u32[]{:S(2)}) copy-start(s32[1,128,128]{2,1,0:T(8,128)} %param.21) | copy-start | bytes 196612

commit v7 on v6

--- a/solution.py
+++ b/solution.py
@@ -141,7 +141,9 @@
     add(v_out, following, -k4 * two(v1, sign))
 
 
-def bulk(u, v, t, hyper, damp, u_out, v_out, t_out, pick):
+def bulk(u, v, t, hyper, damp, u_out, v_out, t_out, pick, coef_out, quarter_out, across):
+    per_level(coef_out, quarter_out, hyper, damp)
+    level_rows(across, hyper, damp)
     lane = lax.broadcasted_iota(jnp.int32, (CX, CY), 1)
     none = jnp.zeros((8, CY), F32)
 
@@ -192,7 +194,6 @@
             q = jnp.where(spot == i, damp[8 * k + i] * 0.25, q)
         across[k : k + 1, :] = c
         across[parts + k : parts + k + 1, :] = q
-    return across[0:parts, :], across[parts : 2 * parts, :]
 
 
 def line(yes, no, keep, f, col):
@@ -241,11 +242,10 @@
 
 
 def theta_borders(
-    u, t_in, own_a, own_b, col_b, col_a, row_a, row_b, hyper, damp, pick, t_out, table, coef, quarter, turn, across
+    u, t_in, own_a, own_b, col_b, col_a, row_a, row_b, pick, coef, across, t_out, table, turn
 ):
     even_x, even_y = is_even("px"), is_even("py")
-    per_level(coef, quarter, hyper, damp)
-    c4, _ = level_rows(across, hyper, damp)
+    c4 = across[0 : FLAT // 128, :]
     east, west = beside(col_a, col_b, even_y, 2)
     v_first, v_last = line(own_b, own_a, even_y, 1, 0), line(own_a, own_b, even_y, 1, 1)
     turn[...] = jnp.zeros_like(turn)
@@ -302,10 +302,10 @@
 
 
 def rest(
-    u_in, v_in, t_in, col_b, col_a, row_a, row_b, obs, coef, quarter, hyper, damp, u_out, v_out, t_out, turn, across
+    u_in, v_in, t_in, col_b, col_a, row_a, row_b, obs, coef, quarter, across, u_out, v_out, t_out, turn
 ):
     even_x, even_y = is_even("px"), is_even("py")
-    c4, q4 = level_rows(across, hyper, damp)
+    c4, q4 = across[0 : FLAT // 128, :], across[FLAT // 128 :, :]
     ue, uw = beside(col_a, col_b, even_y, 0)
     ve, vw = beside(col_a, col_b, even_y, 1)
     turn[...] = jnp.zeros_like(turn)
@@ -457,22 +457,21 @@
     plane = shape((LEV, CY), F32)
     grid = shape((24 * LEV, 2 * CY), BF16)
     turn = pltpu.VMEM((CY, CY), F32)
-    u_part, v_part, t_part, pick = pl.pallas_call(
+    u_part, v_part, t_part, pick, coef, quarter, across = pl.pallas_call(
         bulk,
-        out_shape=(patch, patch, patch, shape((4 * CY, 4 * CY), BF16)),
+        out_shape=(patch, patch, patch, shape((4 * CY, 4 * CY), BF16), plane, plane, shape((8, CY), F32)),
         in_specs=[VMEM] * 3 + [SMEM] * 2,
         compiler_params=PARAMS,
         cost_estimate=cost(8000000, 10000000),
     )(u, v, t, hyper, damp)
-    across = pltpu.VMEM((8, CY), F32)
-    t_most, table, coef, quarter = pl.pallas_call(
+    t_most, table = pl.pallas_call(
         theta_borders,
-        out_shape=(patch, grid, plane, plane),
-        in_specs=[VMEM] * 8 + [SMEM] * 2 + [VMEM],
-        scratch_shapes=[turn, across],
+        out_shape=(patch, grid),
+        in_specs=[VMEM] * 11,
+        scratch_shapes=[turn],
         compiler_params=PARAMS,
         cost_estimate=cost(4000000, 3000000),
-    )(u, t_part, own_a, own_b, col_b, col_a, row_a, row_b, hyper, damp, pick)
+    )(u, t_part, own_a, own_b, col_b, col_a, row_a, row_b, pick, coef, across)
     _, model = pl.pallas_call(
         interpolate,
         out_shape=(grid, shape((owners, slots), F32)),
@@ -485,11 +484,11 @@
     u_next, v_next, t_next = pl.pallas_call(
         rest,
         out_shape=(patch, patch, patch),
-        in_specs=[VMEM] * 10 + [SMEM] * 2,
-        scratch_shapes=[turn, across],
+        in_specs=[VMEM] * 11,
+        scratch_shapes=[turn],
         compiler_params=PARAMS,
         cost_estimate=cost(4000000, 3000000),
-    )(u_part, v_part, t_most, col_b, col_a, row_a, row_b, got, coef, quarter, hyper, damp)
+    )(u_part, v_part, t_most, col_b, col_a, row_a, row_b, got, coef, quarter, across)
     back = lax.all_to_all(model, BOTH, split_axis=0, concat_axis=0, tiled=True)
     departures = mask.astype(F32) * (values - back[None])
     whole = theta.shape

time: 53 us -> 53.1 us (level)
  waiting for transfers between devices: 10.1 us -> 11.3 us
  Pallas kernels: 17.8 us -> 17.2 us
    all_to_all x1, waiting for transfers between devices: 7.16 us -> 7.85 us  [on_device(): back = lax.all_to_all(model, BOTH, split_axis=0, concat_axis=0, tiled=True)]
    pallas_call x1, Pallas kernels: 1.18 us -> 0.63 us  [on_device(): pl.pallas_call(theta_borders, out_shape=(patch, grid), in_specs=[VMEM] *...]
    all_to_all x1, waiting for transfers between devices: 2.6 us -> 3.15 us  [on_device(): got = lax.all_to_all(sent, BOTH, split_axis=0, concat_axis=0, tiled=True)]
    pallas_call x1, Pallas kernels: 2.52 us -> 1.97 us  [on_device(): pl.pallas_call(rest, out_shape=(patch, patch, patch), in_specs=[VMEM] * 1...]
  transfers between devices with their start and end apart: 6 -> 6, of which waited for: 3 -> 3; matrix products, arithmetic and copies ran while one was open for 0% -> 0% of each run, Pallas kernels for 12% -> 10%
where the time goes in v7:
time: 53.1 us; the launch traced here: 52.8 us
  starting transfers between devices  22.9 us (43%)
  Pallas kernels  17.2 us (32%)
  waiting for transfers between devices  11.3 us (21%)
  between operations  0.75 us (1%)
  other arithmetic  0.64 us (1%)
    all_to_all x1, starting transfers between devices, on_device(): got = lax.all_to_all(sent, BOTH, split_axis=0, concat_axis=0, tiled=True)  11.5 us
    pallas_call x1, Pallas kernels, on_device(): pl.pallas_call(interpolate, out_shape=(grid, shape((owners, slots), F32))...  9.56 us
    all_to_all x1, waiting for transfers between devices, on_device(): back = lax.all_to_all(model, BOTH, split_axis=0, concat_axis=0, tiled=True)  7.85 us
    ppermute x1, starting transfers between devices, on_device(): col_b = lax.ppermute(own_b, 'py', swap('py', 1))  5.38 us
    all_to_all x1, starting transfers between devices, on_device(): back = lax.all_to_all(model, BOTH, split_axis=0, concat_axis=0, tiled=True)  4.16 us
    all_to_all x1, waiting for transfers between devices, on_device(): got = lax.all_to_all(sent, BOTH, split_axis=0, concat_axis=0, tiled=True)  3.15 us
    pallas_call x1, Pallas kernels, on_device(): pl.pallas_call(bulk, out_shape=(patch, patch, patch, shape((4 * CY, 4 * C...  2.5 us
    pallas_call x1, Pallas kernels, on_device(): pl.pallas_call(messages_out, out_shape=shape((owners, SENT, slots), F32),...  2.24 us
  transfers between devices with their start and end apart: 6, of which 3 were waited for; matrix products, arithmetic and copies ran while one was open for 0% of the time, Pallas kernels for 10%

profile of v7, /device:TPU:1, one launch (start us, length us, event | category | flops | bytes accessed | tf_op | source)
XLA Modules:
  0.0 52.8 jit_solution(11895518751688238149)
XLA Ops:
  0.6 2.2 %shard_map.141 = f32[128,8,128]{2,1,0:T(8,128)} custom-call(f32[512,128]{1,0:T(8,128)} %bitcast.20, f32[512,128]{1,0:T(8,128)} %bitcast.24, f32[512,128]{1,0:T(8,128)} %bitcast.27, s32[128,128]{1,0:T(8,128)} %bitcast.32, s32[128,128]{1,0:T(8,128)} %bitcast.33, f32[3,128,128]{2,1,0:T(8,128)} %bitcast.31, f32[128,128]{1,0:T(8,128)} %bitcast.34), custom_call_target="tpu_custom_call" | custom-call | flops 100000 | bytes 3000000 | tf_op jit(solution)/shard_map/pallas_call | solution.py:427
  2.9 0.0 copy-start
  2.9 0.0 copy-start.1
  2.9 0.0 copy-start.2
  2.9 11.5 %all-to-all-start = ((f32[128,8,128]{2,1,0:T(8,128)}), f32[128,8,128]{2,1,0:T(8,128)S(1)}, u32[]{:S(2)}, u32[]{:S(2)}) async-start(f32[128,8,128]{2,1,0:T(8,128)} %shard_map.141), calls=%async_computation | async-start | bytes 1048576 | tf_op jit(solution)/shard_map/all_to_all | solution.py:442
  14.4 0.0 copy-done
  14.4 0.0 copy-done.1
  14.4 0.0 copy-done.2
  14.5 0.3 shard_map.139
  14.7 1.1 %collective-permute-start.2 = (f32[192,128]{1,0:T(8,128)S(1)}, f32[192,128]{1,0:T(8,128)S(1)}, u32[]{:S(2)}, u32[]{:S(2)}) collective-permute-start(f32[192,128]{1,0:T(8,128)S(1)} %get-tuple-element.26), channel_id=1, source_target_pairs={{0,16},{32,48},{64,80},{96,112},{16,0},{48,32},{80,64},{112,96},{1... | collective-permute-start | bytes 294920 | tf_op jit(solution)/shard_map/ppermute | solution.py:455
  15.9 0.7 %collective-permute-start.3 = (f32[192,128]{1,0:T(8,128)S(1)}, f32[192,128]{1,0:T(8,128)S(1)}, u32[]{:S(2)}, u32[]{:S(2)}) collective-permute-start(f32[192,128]{1,0:T(8,128)S(1)} %get-tuple-element.27), channel_id=1, source_target_pairs={{16,32},{48,64},{80,96},{112,0},{32,16},{64,48},{96,80},{0,112},{1... | collective-permute-start | bytes 294920 | tf_op jit(solution)/shard_map/ppermute | solution.py:454
  16.6 0.0 copy-start.3
  16.6 0.0 copy-start.4
  16.6 5.4 %collective-permute-start = (f32[24,128]{1,0:T(8,128)S(1)}, f32[24,128]{1,0:T(8,128)S(1)}, u32[]{:S(2)}, u32[]{:S(2)}) collective-permute-start(f32[24,128]{1,0:T(8,128)S(1)} %get-tuple-element.25.own_b), channel_id=1, source_target_pairs={{1,2},{3,4},{5,6},{7,8},{9,10},{11,12},{13,14},{15,0},{2,1},{4,3},... | collective-permute-start | bytes 36872 | tf_op jit(solution)/shard_map/ppermute | solution.py:452
  22.0 0.0 collective-permute-start.1
  22.0 0.0 copy-done.3
  22.0 0.0 copy-done.4
  22.0 2.5 %shard_map.138 = (f32[512,128]{1,0:T(8,128)S(1)}, f32[512,128]{1,0:T(8,128)S(1)}, f32[512,128]{1,0:T(8,128)S(1)}, bf16[512,512]{1,0:T(8,128)(2,1)S(1)}, f32[32,1...) custom-call(f32[512,128]{1,0:T(8,128)S(1)} %bitcast.22, f32[512,128]{1,0:T(8,128)S(1)} %bitcast.26, ...), custom_call_target="tpu_custom_call" | custom-call | flops 8000000 | bytes 10000000 | tf_op jit(solution)/shard_map/pallas_call | solution.py:460
  24.5 0.0 collective-permute-done.col_b
  24.5 0.3 collective-permute-done.1.col_a
  24.8 0.0 collective-permute-done.2.row_a
  24.8 0.0 collective-permute-done.3.row_b
  24.8 0.6 %shard_map.140 = (f32[512,128]{1,0:T(8,128)S(1)}, bf16[768,256]{1,0:T(8,128)(2,1)S(1)}) custom-call(f32[512,128]{1,0:T(8,128)S(1)} %bitcast.23, f32[512,128]{1,0:T(8,128)S(1)} %get-tuple-element.23.t_in, f32[24,128]{1,0:T(8,128)S(1)} %get-tuple-element.24.own_a, f32[24,128]{1,0:T(8,128)S(1)} %get-tuple-element.25.own_b, ...), custom_call_target="tpu_custom_call" | custom-call | flops 4000000 | bytes 3000000 | tf_op jit(solution)/shard_map/pallas_call | solution.py:467
  25.5 3.2 %all-to-all-done.obs = f32[128,8,128]{2,1,0:T(8,128)S(1)} async-done(((f32[128,8,128]{2,1,0:T(8,128)}), f32[128,8,128]{2,1,0:T(8,128)S(1)}, u32[]{:S(2)}, u32[]{:S(2)}) %all-to-all-start) | async-done | bytes 524320 | tf_op jit(solution)/shard_map/all_to_all | solution.py:442
  28.6 9.6 %shard_map.143 = (bf16[768,256]{1,0:T(8,128)(2,1)S(1)}, f32[128,128]{1,0:T(8,128)}) custom-call(bf16[768,256]{1,0:T(8,128)(2,1)S(1)} %get-tuple-element.36.start, f32[128,8,128]{2,1,0:T(8,128)S(1)} %all-to-all-done.obs, f32[512,128]{1,0:T(8,128)S(1)} %get-tuple-element.31.t_in.t, f32[32,128]{1,0:T(8,128)S(1)} %get-tuple-element.29.coef), custom_call_target="tpu_custom_call", output_to_operand_aliasing={{0}: (0, {})} | custom-call | flops 6499999744 | bytes 1000000 | tf_op jit(solution)/shard_map/pallas_call | solution.py:475
  38.2 4.2 %all-to-all-start.1 = ((f32[128,1,128]{2,1,0:T(1,128)}), f32[128,1,128]{2,1,0:T(1,128)S(1)}, u32[]{:S(2)}, u32[]{:S(2)}) async-start(f32[128,1,128]{2,1,0:T(1,128)} %bitcast.12), calls=%async_computation.1 | async-start | bytes 131072 | tf_op jit(solution)/shard_map/all_to_all | solution.py:492
  42.4 0.0 copy-start.5
  42.4 0.0 copy-start.6
  42.4 2.0 %shard_map.142 = (f32[512,128]{1,0:T(8,128)}, f32[512,128]{1,0:T(8,128)}, f32[512,128]{1,0:T(8,128)}) custom-call(f32[512,128]{1,0:T(8,128)S(1)} %get-tuple-element.21.u_in, f32[512,128]{1,0:T(8,128)S(1)} %get-tuple-element.22.v_in, f32[512,128]{1,0:T(8,128)S(1)} %get-tuple-element.31.t_in.t, f32[24,128]{1,0:T(8,128)S(1)} %collective-permute-done.col_b, ...), custom_call_target="tpu_custom_call" | custom-call | flops 4000000 | bytes 3000000 | tf_op jit(solution)/shard_map/pallas_call | solution.py:484
  44.4 7.8 %all-to-all-done.1 = f32[128,1,128]{2,1,0:T(1,128)S(1)} async-done(((f32[128,1,128]{2,1,0:T(1,128)}), f32[128,1,128]{2,1,0:T(1,128)S(1)}, u32[]{:S(2)}, u32[]{:S(2)}) %all-to-all-start.1) | async-done | bytes 65568 | tf_op jit(solution)/shard_map/all_to_all | solution.py:492
  52.2 0.0 copy-done.5
  52.2 0.0 copy-done.6
  52.2 0.6 %fusion = f32[1,128,128]{2,1,0:T(8,128)} fusion(f32[1,128,128]{2,1,0:T(8,128)S(1)} %copy-done.5, s32[1,128,128]{2,1,0:T(8,128)S(1)} %copy-done.6, f32[1,128,128]{2,1,0:T(8,128)S(1)} %bitcast.30), kind=kLoop, calls=%fused_computation.1 | loop fusion | flops 49152 | bytes 262144 | tf_op jit(solution)/shard_map/mul | solution.py:493
Async XLA Ops:
  2.9 11.5 %copy-start = (f32[32,16,128]{2,1,0:T(8,128)S(1)}, f32[32,16,128]{2,1,0:T(8,128)}, u32[]{:S(2)}) copy-start(f32[32,16,128]{2,1,0:T(8,128)} %param.12) | copy-start | bytes 786436
  2.9 11.5 %copy-start.1 = (f32[32,16,128]{2,1,0:T(8,128)S(1)}, f32[32,16,128]{2,1,0:T(8,128)}, u32[]{:S(2)}) copy-start(f32[32,16,128]{2,1,0:T(8,128)} %param.13) | copy-start | bytes 786436
  2.9 11.5 %copy-start.2 = (f32[32,16,128]{2,1,0:T(8,128)S(1)}, f32[32,16,128]{2,1,0:T(8,128)}, u32[]{:S(2)}) copy-start(f32[32,16,128]{2,1,0:T(8,128)} %param.11) | copy-start | bytes 786436
  2.9 25.7 %all-to-all-start = ((f32[128,8,128]{2,1,0:T(8,128)}), f32[128,8,128]{2,1,0:T(8,128)S(1)}, u32[]{:S(2)}, u32[]{:S(2)}) async-start(f32[128,8,128]{2,1,0:T(8,128)} %shard_map.141), calls=%async_computation | async-start | bytes 1048576 | tf_op jit(solution)/shard_map/all_to_all | solution.py:442
  14.7 10.1 %collective-permute-start.2 = (f32[192,128]{1,0:T(8,128)S(1)}, f32[192,128]{1,0:T(8,128)S(1)}, u32[]{:S(2)}, u32[]{:S(2)}) collective-permute-start(f32[192,128]{1,0:T(8,128)S(1)} %get-tuple-element.26), channel_id=1, source_target_pairs={{0,16},{32,48},{64,80},{96,112},{16,0},{48,32},{80,64},{112,96},{1... | collective-permute-start | bytes 294920 | tf_op jit(solution)/shard_map/ppermute | solution.py:455
  15.9 9.0 %collective-permute-start.3 = (f32[192,128]{1,0:T(8,128)S(1)}, f32[192,128]{1,0:T(8,128)S(1)}, u32[]{:S(2)}, u32[]{:S(2)}) collective-permute-start(f32[192,128]{1,0:T(8,128)S(1)} %get-tuple-element.27), channel_id=1, source_target_pairs={{16,32},{48,64},{80,96},{112,0},{32,16},{64,48},{96,80},{0,112},{1... | collective-permute-start | bytes 294920 | tf_op jit(solution)/shard_map/ppermute | solution.py:454
  16.6 5.4 %copy-start.3 = (f32[32]{0:T(128)S(1)}, f32[32]{0:T(128)}, u32[]{:S(2)}) copy-start(f32[32]{0:T(128)} %hyper.1) | copy-start | bytes 388
  16.6 5.4 %copy-start.4 = (f32[32]{0:T(128)S(1)}, f32[32]{0:T(128)}, u32[]{:S(2)}) copy-start(f32[32]{0:T(128)} %damp.1) | copy-start | bytes 388
  16.6 7.9 %collective-permute-start = (f32[24,128]{1,0:T(8,128)S(1)}, f32[24,128]{1,0:T(8,128)S(1)}, u32[]{:S(2)}, u32[]{:S(2)}) collective-permute-start(f32[24,128]{1,0:T(8,128)S(1)} %get-tuple-element.25.own_b), channel_id=1, source_target_pairs={{1,2},{3,4},{5,6},{7,8},{9,10},{11,12},{13,14},{15,0},{2,1},{4,3},... | collective-permute-start | bytes 36872 | tf_op jit(solution)/shard_map/ppermute | solution.py:452
  22.0 2.9 %collective-permute-start.1 = (f32[24,128]{1,0:T(8,128)S(1)}, f32[24,128]{1,0:T(8,128)S(1)}, u32[]{:S(2)}, u32[]{:S(2)}) collective-permute-start(f32[24,128]{1,0:T(8,128)S(1)} %get-tuple-element.24.own_a), channel_id=1, source_target_pairs={{0,1},{2,3},{4,5},{6,7},{8,9},{10,11},{12,13},{14,15},{1,0},{3,2},... | collective-permute-start | bytes 36872 | tf_op jit(solution)/shard_map/ppermute | solution.py:453
  38.2 14.0 %all-to-all-start.1 = ((f32[128,1,128]{2,1,0:T(1,128)}), f32[128,1,128]{2,1,0:T(1,128)S(1)}, u32[]{:S(2)}, u32[]{:S(2)}) async-start(f32[128,1,128]{2,1,0:T(1,128)} %bitcast.12), calls=%async_computation.1 | async-start | bytes 131072 | tf_op jit(solution)/shard_map/all_to_all | solution.py:492
  42.4 9.8 %copy-start.5 = (f32[1,128,128]{2,1,0:T(8,128)S(1)}, f32[1,128,128]{2,1,0:T(8,128)}, u32[]{:S(2)}) copy-start(f32[1,128,128]{2,1,0:T(8,128)} %param.20) | copy-start | bytes 196612
  42.4 9.8 %copy-start.6 = (s32[1,128,128]{2,1,0:T(8,128)S(1)}, s32[1,128,128]{2,1,0:T(8,128)}, u32[]{:S(2)}) copy-start(s32[1,128,128]{2,1,0:T(8,128)} %param.21) | copy-start | bytes 196612
